TPU v7x, 32 devices: a whole 2x2x4 slice. The times are simulated.
32 devices in a mesh: rep: 4 (over z), ex: 8 (over y, x, core).
Axes of the slice: x: 2, y: 2, z: 4, core: 2. Of those that a mesh axis runs over, the one named last changes fastest.
Arguments:
- tokens: bfloat16 [25088, 768], P(('rep', 'ex')), may hold values from -6 to 6
- gain_one: float32 [768], replicated, may hold values from 0.5 to 1.5
- shift_one: float32 [768], replicated, may hold values from -0.625 to 0.625
- w_qkv: bfloat16 [768, 2304], replicated, may hold values from -0.21875 to 0.21875
- w_out: bfloat16 [768, 768], replicated, may hold values from -1.75 to 1.75
- gain_two: float32 [768], replicated, may hold values from 0.5 to 1.5
- shift_two: float32 [768], replicated, may hold values from -0.625 to 0.625
- w_router: bfloat16 [768, 8], replicated, may hold values from -0.15625 to 0.15625
- w_in: bfloat16 [8, 768, 3072], P('ex'), may hold values from -0.21875 to 0.21875
- bias_in: float32 [8, 3072], P('ex'), may hold values from -0.625 to 0.625
- w_back: bfloat16 [8, 3072, 768], P('ex'), may hold values from -0.5 to 0.5
- bias_back: float32 [8, 768], P('ex'), may hold values from -2 to 2
- cotangent: bfloat16 [25088, 768], P(('rep', 'ex')), may hold values from -6 to 6
- routes: int32 [25088, 2], P(('rep', 'ex')), may hold values from 0 to 7, all different within a row
- priority: int32 [32, 784], P(('rep', 'ex')), may hold values from 0 to 783, each once within a row
- image_kind: int32 [32], P(('rep', 'ex')), may hold values from 0 to 1
Outputs:
- result: bfloat16 [25088, 768], P(('rep', 'ex'))
- grad_tokens: bfloat16 [25088, 768], P(('rep', 'ex'))
- grad_gain_one: float32 [768], replicated
- grad_shift_one: float32 [768], replicated
- grad_w_qkv: float32 [768, 2304], replicated
- grad_w_out: float32 [768, 768], replicated
- grad_gain_two: float32 [768], replicated
- grad_shift_two: float32 [768], replicated
- grad_w_router: float32 [768, 8], replicated
- grad_w_in: float32 [8, 768, 3072], P('ex', 'rep')
- grad_bias_in: float32 [8, 3072], P('ex', 'rep')
- grad_w_back: float32 [8, 3072, 768], P('ex', 'rep')
- grad_bias_back: float32 [8, 768], P('ex', 'rep')
Inputs may be any that keep to these rules, and one draw needn't show every extreme that they name: `routes`: each row names two different experts. `priority`: each device's row holds every rank once. `image_kind`: 0: a set holds four images of 196 patches; 1: one image of 576 patches, one of 196, then 3 * 196 - 576 padding rows that attend only to one another.
All inputs are finite; a program needn't handle non-finite values.
Results may differ from a plain program's by a relative error of at most 0.015.
Values may be sent and summed in bfloat16 or wider, within the bound.
No kernel may reach another device: no remote copies, remote signals or barrier semaphores. Data moves between devices by JAX's collectives and lax.ppermute only.
A program may use at most 256 MiB of HBM per device.

v0:
```python
import jax
import jax.numpy as jnp
from jax import lax
from jax.sharding import PartitionSpec as P

HEADS = 12
HEAD_DIM = 64
PATCH_S = 196
PATCH_L = 576


EPS = 1e-06
NEG = -1e30
INV_ROOT_TWO = 0.7071067811865476
INV_ROOT_TAU = 0.3989422804014327


def norm_forward(values, gain, shift):
    average = jnp.mean(values, axis=-1, keepdims=True)
    centered = values - average
    variance = jnp.mean(centered * centered, axis=-1, keepdims=True)
    inverse = lax.rsqrt(variance + EPS)
    scaled = centered * inverse
    return (scaled * gain + shift, scaled, inverse)


def norm_backward(upstream, scaled, inverse, gain):
    through = upstream * gain
    first_mean = jnp.mean(through, axis=-1, keepdims=True)
    second = jnp.mean(through * scaled, axis=-1, keepdims=True)
    grad_values = inverse * (through - first_mean - scaled * second)
    return (grad_values, jnp.sum(upstream * scaled, axis=0), jnp.sum(upstream, axis=0))


def set_segments(set_kind):
    positions = jnp.arange(4 * PATCH_S, dtype=jnp.int32)
    small_ids = positions // PATCH_S
    large_ids = jnp.where(
        positions < PATCH_L, 0, jnp.where(positions < PATCH_L + PATCH_S, 1, 2)
    ).astype(jnp.int32)
    return jnp.where(set_kind == 1, large_ids, small_ids)


def device_slots(chosen, ranking, experts, slot_cap):
    tok_count = chosen.shape[0]
    pair_order = jnp.concatenate([ranking, ranking + tok_count])
    target = jnp.concatenate([chosen[:, 0], chosen[:, 1]])
    by_rank = jnp.zeros((2 * tok_count,), jnp.int32).at[pair_order].set(target)
    labels = jnp.arange(experts, dtype=jnp.int32)
    one_hot = (by_rank[:, None] == labels[None, :]).astype(jnp.int32)
    before = jnp.cumsum(one_hot, axis=0) - one_hot
    placed = jnp.sum(before * one_hot, axis=1)
    position = placed[pair_order]
    kept_mask = position < slot_cap
    slot_ids = jnp.where(kept_mask, target * slot_cap + position, -1)
    pair_ids = jnp.arange(2 * tok_count, dtype=jnp.int32)
    landing = jnp.where(kept_mask, slot_ids, experts * slot_cap)
    source = jnp.full((experts * slot_cap,), -1, jnp.int32).at[landing].set(pair_ids, mode="drop")
    return (source, slot_ids.reshape(2, tok_count).T)


def masked_scores(queries, keys_part, segment):
    scores = jnp.einsum(
        "qhd,khd->hqk", queries, keys_part, preferred_element_type=jnp.float32
    ) * HEAD_DIM ** (-0.5)
    linked = segment[:, None] == segment[None, :]
    return jnp.where(linked[None], scores, NEG)


def attention_forward(set_rows, segment, w_qkv, w_out):
    row_total = set_rows.shape[0]
    packed = jnp.dot(set_rows, w_qkv, preferred_element_type=jnp.float32).astype(jnp.bfloat16)
    by_heads = packed.reshape(row_total, 3, HEADS, HEAD_DIM)
    scores = masked_scores(by_heads[:, 0], by_heads[:, 1], segment)
    row_max = jnp.max(scores, axis=-1, keepdims=True)
    exp_scores = jnp.exp(scores - row_max)
    exp_total = jnp.sum(exp_scores, axis=-1, keepdims=True)
    weights = exp_scores / exp_total
    logsum = (row_max + jnp.log(exp_total))[:, :, 0]
    head_mix = jnp.einsum(
        "hqk,khd->qhd",
        weights.astype(jnp.bfloat16),
        by_heads[:, 2],
        preferred_element_type=jnp.float32,
    )
    head_mix = head_mix.reshape(row_total, -1).astype(jnp.bfloat16)
    branch = jnp.dot(head_mix, w_out, preferred_element_type=jnp.float32)
    return (branch, packed, head_mix, logsum)


def attention_backward(upstream, set_rows, segment, packed, head_mix, logsum, w_qkv, w_out):
    row_total = packed.shape[0]
    grad_out_part = jnp.einsum("rd,re->de", head_mix, upstream, preferred_element_type=jnp.float32)
    grad_mix = jnp.dot(upstream, w_out.T, preferred_element_type=jnp.float32).astype(jnp.bfloat16)
    grad_mix = grad_mix.reshape(row_total, HEADS, HEAD_DIM)
    by_heads = packed.reshape(row_total, 3, HEADS, HEAD_DIM)
    queries = by_heads[:, 0]
    keys_part = by_heads[:, 1]
    values = by_heads[:, 2]
    scores = masked_scores(queries, keys_part, segment)
    weights = jnp.exp(scores - logsum[:, :, None])
    grad_weights = jnp.einsum("qhd,khd->hqk", grad_mix, values, preferred_element_type=jnp.float32)
    grad_values = jnp.einsum(
        "hqk,qhd->khd", weights.astype(jnp.bfloat16), grad_mix, preferred_element_type=jnp.float32
    )
    inner_sum = jnp.sum(grad_weights * weights, axis=-1, keepdims=True)
    grad_scores = (weights * (grad_weights - inner_sum)).astype(jnp.bfloat16)
    grad_queries = jnp.einsum(
        "hqk,khd->qhd", grad_scores, keys_part, preferred_element_type=jnp.float32
    ) * HEAD_DIM ** (-0.5)
    grad_keys = jnp.einsum(
        "hqk,qhd->khd", grad_scores, queries, preferred_element_type=jnp.float32
    ) * HEAD_DIM ** (-0.5)
    grad_packed = (
        jnp.stack([grad_queries, grad_keys, grad_values], axis=1)
        .reshape(row_total, -1)
        .astype(jnp.bfloat16)
    )
    grad_qkv_part = jnp.einsum(
        "rd,re->de", set_rows, grad_packed, preferred_element_type=jnp.float32
    )
    grad_rows = jnp.dot(grad_packed, w_qkv.T, preferred_element_type=jnp.float32)
    return (grad_rows, grad_qkv_part, grad_out_part)


def local(
    tokens,
    gain_one,
    shift_one,
    w_qkv,
    w_out,
    gain_two,
    shift_two,
    w_router,
    w_in,
    bias_in,
    w_back,
    bias_back,
    cotangent,
    routes,
    priority,
    image_kind,
):
    tok_count = tokens.shape[0]
    model_width = tokens.shape[1]
    experts = w_router.shape[1]
    slot_cap = (42 * tok_count + 20 * experts - 1) // (20 * experts)
    first_w = w_in[0]
    first_bias = bias_in[0]
    second_w = w_back[0]
    second_bias = bias_back[0]
    inputs = tokens.astype(jnp.float32)
    normed_one, scaled_one, inverse_one = norm_forward(inputs, gain_one, shift_one)
    sets_low = normed_one.astype(jnp.bfloat16).reshape(-1, 4 * PATCH_S, model_width)

    def set_forward(packed_in):
        set_rows, set_kind = packed_in
        return attention_forward(set_rows, set_segments(set_kind), w_qkv, w_out)

    branch, packed, head_mix, logsum = lax.map(set_forward, (sets_low, image_kind))
    residual = inputs + branch.reshape(tok_count, model_width)
    normed_two, scaled_two, inverse_two = norm_forward(residual, gain_two, shift_two)
    lowered = normed_two.astype(jnp.bfloat16)
    logits = jnp.dot(lowered, w_router, preferred_element_type=jnp.float32)
    router_probs = jax.nn.softmax(logits, axis=-1)
    source, slot_index = device_slots(routes, priority[0], experts, slot_cap)
    slot_used = source >= 0
    pair_token = jnp.maximum(source, 0) % tok_count
    dispatch = jnp.where(slot_used[:, None], lowered[pair_token], jnp.zeros((), jnp.bfloat16))
    dispatch = dispatch.reshape(experts, slot_cap, model_width)
    received = lax.all_to_all(dispatch, "ex", split_axis=0, concat_axis=0, tiled=True)
    flat_rows = received.reshape(-1, model_width)
    pre_act = jnp.dot(flat_rows, first_w, preferred_element_type=jnp.float32) + first_bias
    hidden = jax.nn.gelu(pre_act, approximate=False).astype(jnp.bfloat16)
    produced = (jnp.dot(hidden, second_w, preferred_element_type=jnp.float32) + second_bias).astype(
        jnp.bfloat16
    )
    produced = produced.reshape(received.shape[0], received.shape[1], model_width)
    returned = lax.all_to_all(produced, "ex", split_axis=0, concat_axis=0, tiled=True)
    item_shape = (received.shape[0], received.shape[1], -1)
    returned, kept_rows, kept_pre, kept_hidden = (
        returned,
        received,
        pre_act.reshape(item_shape),
        hidden.reshape(item_shape),
    )
    upstream = cotangent.astype(jnp.float32)
    slot_flat = slot_index.reshape(-1)
    kept_mask = slot_index >= 0
    pair_out = returned.reshape(-1, model_width)[jnp.maximum(slot_flat, 0)].reshape(
        tok_count, 2, model_width
    )
    chosen_probs = jnp.take_along_axis(router_probs, routes, axis=1)
    gate_values = jnp.where(kept_mask, chosen_probs, 0.0)
    pair_float = pair_out.astype(jnp.float32)
    combined = jnp.sum(gate_values[:, :, None] * pair_float, axis=1)
    result = (residual + combined).astype(jnp.bfloat16)
    grad_gate = jnp.where(kept_mask, jnp.sum(upstream[:, None, :] * pair_float, axis=-1), 0.0)
    labels = jnp.arange(experts, dtype=jnp.int32)
    one_hot = (routes[:, :, None] == labels[None, None, :]).astype(jnp.float32)
    grad_probs = jnp.sum(one_hot * grad_gate[:, :, None], axis=1)
    grad_logits = router_probs * (
        grad_probs - jnp.sum(router_probs * grad_probs, axis=-1, keepdims=True)
    )
    grad_logits = grad_logits.astype(jnp.bfloat16)
    grad_router = jnp.einsum("td,te->de", lowered, grad_logits, preferred_element_type=jnp.float32)
    grad_from_router = jnp.dot(grad_logits, w_router.T, preferred_element_type=jnp.float32)
    gate_pairs = jnp.concatenate([gate_values[:, 0], gate_values[:, 1]])
    slot_gate = jnp.where(slot_used, gate_pairs[jnp.maximum(source, 0)], 0.0)
    grad_slots = (slot_gate[:, None] * upstream[pair_token]).astype(jnp.bfloat16)
    grad_slots = grad_slots.reshape(experts, slot_cap, model_width)
    incoming, resent = (
        lax.all_to_all(grad_slots, "ex", split_axis=0, concat_axis=0, tiled=True),
        lax.all_to_all(dispatch, "ex", split_axis=0, concat_axis=0, tiled=True),
    )
    rows_in = resent.reshape(-1, model_width)
    pre_act = jnp.dot(rows_in, first_w, preferred_element_type=jnp.float32) + first_bias
    hidden = jax.nn.gelu(pre_act, approximate=False).astype(jnp.bfloat16)
    flat_grad = incoming.reshape(-1, model_width)
    grad_second = jnp.einsum("rf,rd->fd", hidden, flat_grad, preferred_element_type=jnp.float32)
    grad_second_bias = jnp.sum(flat_grad.astype(jnp.float32), axis=0)
    grad_hidden = jnp.dot(flat_grad, second_w.T, preferred_element_type=jnp.float32)
    gelu_slope = (
        0.5 * (1.0 + lax.erf(pre_act * INV_ROOT_TWO))
        + pre_act * jnp.exp(-0.5 * pre_act * pre_act) * INV_ROOT_TAU
    )
    grad_pre = (grad_hidden * gelu_slope).astype(jnp.bfloat16)
    grad_first = jnp.einsum("rd,rf->df", rows_in, grad_pre, preferred_element_type=jnp.float32)
    grad_first_bias = jnp.sum(grad_pre.astype(jnp.float32), axis=0)
    grad_rows = jnp.dot(grad_pre, first_w.T, preferred_element_type=jnp.float32).astype(
        jnp.bfloat16
    )
    grad_rows = grad_rows.reshape(incoming.shape)
    grad_back = lax.all_to_all(grad_rows, "ex", split_axis=0, concat_axis=0, tiled=True).reshape(
        -1, model_width
    )
    grad_pairs = (
        grad_back[jnp.maximum(slot_flat, 0)].astype(jnp.float32).reshape(tok_count, 2, model_width)
    )
    grad_dispatch = jnp.sum(jnp.where(kept_mask[:, :, None], grad_pairs, 0.0), axis=1)
    grad_lowered = grad_from_router + grad_dispatch
    grad_res_norm, grad_gain_two, grad_shift_two = norm_backward(
        grad_lowered, scaled_two, inverse_two, gain_two
    )
    grad_residual = upstream + grad_res_norm
    grad_branch = grad_residual.astype(jnp.bfloat16).reshape(-1, 4 * PATCH_S, model_width)

    def set_backward(packed_in):
        set_upstream, set_rows, set_kind, set_packed, set_mix, set_logsum = packed_in
        return attention_backward(
            set_upstream,
            set_rows,
            set_segments(set_kind),
            set_packed,
            set_mix,
            set_logsum,
            w_qkv,
            w_out,
        )

    grad_normed_one, grad_qkv_sets, grad_out_sets = lax.map(
        set_backward, (grad_branch, sets_low, image_kind, packed, head_mix, logsum)
    )
    grad_norm_one, grad_gain_one, grad_shift_one = norm_backward(
        grad_normed_one.reshape(tok_count, model_width), scaled_one, inverse_one, gain_one
    )
    grad_tokens = (grad_residual + grad_norm_one).astype(jnp.bfloat16)
    dense_grads = lax.psum(
        (
            grad_gain_one,
            grad_shift_one,
            jnp.sum(grad_qkv_sets, axis=0),
            jnp.sum(grad_out_sets, axis=0),
            grad_gain_two,
            grad_shift_two,
            grad_router,
        ),
        ("rep", "ex"),
    )
    expert_grads = (
        lax.psum_scatter(
            grad_first[None].astype(jnp.bfloat16), "rep", scatter_dimension=1, tiled=True
        ).astype(jnp.float32),
        lax.psum_scatter(
            grad_first_bias[None].astype(jnp.bfloat16), "rep", scatter_dimension=1, tiled=True
        ).astype(jnp.float32),
        lax.psum_scatter(
            grad_second[None].astype(jnp.bfloat16), "rep", scatter_dimension=1, tiled=True
        ).astype(jnp.float32),
        lax.psum_scatter(
            grad_second_bias[None].astype(jnp.bfloat16), "rep", scatter_dimension=1, tiled=True
        ).astype(jnp.float32),
    )
    return (
        result,
        grad_tokens,
        dense_grads[0],
        dense_grads[1],
        dense_grads[2],
        dense_grads[3],
        dense_grads[4],
        dense_grads[5],
        dense_grads[6],
        expert_grads[0],
        expert_grads[1],
        expert_grads[2],
        expert_grads[3],
    )


def solution(mesh):
    in_specs = (
        P(("rep", "ex"), None),
        P(),
        P(),
        P(),
        P(),
        P(),
        P(),
        P(),
        P("ex", None, None),
        P("ex", None),
        P("ex", None, None),
        P("ex", None),
        P(("rep", "ex"), None),
        P(("rep", "ex"), None),
        P(("rep", "ex"), None),
        P(("rep", "ex")),
    )
    out_specs = (
        P(("rep", "ex"), None),
        P(("rep", "ex"), None),
        P(),
        P(),
        P(),
        P(),
        P(),
        P(),
        P(),
        P("ex", "rep", None),
        P("ex", "rep"),
        P("ex", "rep", None),
        P("ex", "rep"),
    )
    return jax.shard_map(local, mesh=mesh, in_specs=in_specs, out_specs=out_specs, check_vma=False)
```

profile of v0, /device:TPU:0, one launch (start us, length us, event | category | flops | bytes accessed | tf_op | source)
XLA Modules:
  0.0 851.0 jit_solution(15414379771671306783)
XLA Ops:
  18.8 9.0 %scatter_custom_fusion = s32[1568]{0:T(1024)S(1)} fusion(s32[1568]{0:T(1024)S(1)} %fusion.71, s32[1568]{0:T(1024)} %pad_add_fusion, s32[]{:T(128)} %constant.78.clone.1), kind=kCustom, calls=%fused_computation.169 | custom fusion | bytes 6784 | tf_op jit(solution)/shard_map/scatter | solution.py:48
  28.4 5.1 reduce-window.6
  35.8 8.9 %gather_fusion = s32[1568]{0:T(1024)S(1)} fusion(s32[1568]{0:T(1024)S(1)} %fusion.67, s32[2048]{0:T(1024)} %pad_clamp_fusion.3), kind=kCustom, calls=%fused_computation | custom fusion | bytes 18816 | tf_op jit(solution)/shard_map/gather | solution.py:53
  48.2 9.1 %scatter_custom_fusion.1 = s32[1648]{0:T(1024)S(1)} fusion(s32[1568]{0:T(1024)} %fusion.72, s32[1568]{0:T(1024)} %iota.26, s32[]{:T(128)} %constant.97.clone.1), kind=kCustom, calls=%fused_computation.164 | custom fusion | bytes 7104 | tf_op jit(solution)/shard_map/scatter | solution.py:58
  66.0 4.8 convolution_convert_fusion
  70.8 6.3 copy.99
  78.4 9.2 %gather_fusion.4 = f32[1648,768]{1,0:T(8,128)} fusion(f32[784,768]{1,0:T(8,128)} %convert_element_type.163, s32[2048]{0:T(1024)S(1)} %get-tuple-element.120), kind=kCustom, calls=%fused_computation.4 | custom fusion | bytes 10131904 | tf_op jit(solution)/shard_map/gather | solution.py:210
  87.7 4.3 gather.36
  92.0 18.4 %fusion.22 = (f32[12,784]{1,0:T(8,128)S(1)}, f32[12,784,784]{1,2,0:T(8,128)}) fusion(pred[784,784]{0,1:T(8,128)(4,1)} %broadcast_compare_fusion, bf16[784,3,12,64]{0,3,2,1:T(8,128)(2,1)} %bitcast.116), kind=kOutput, calls=%fused_computation.46 | convolution fusion | flops 966229824 | bytes 32996096 | tf_op jit(solution)/shard_map/while/body/eval_jaxpr/qhd,khd->hqk/dot_general | solution.py:63
  110.4 14.6 %fusion = f32[12,784]{1,0:T(8,128)S(1)} fusion(f32[12,784]{1,0:T(8,128)S(1)} %get-tuple-element.105, f32[12,784,784]{1,2,0:T(8,128)} %get-tuple-element.106, pred[784,784]{0,1:T(8,128)(4,1)S(1)} %copy-done.4), kind=kLoop, calls=%fused_computation.17 | loop fusion | flops 29494080 | bytes 30193408 | tf_op jit(solution)/shard_map/while/body/eval_jaxpr/reduce_sum | solution.py:77
  125.0 17.0 %fusion.55 = bf16[12,64,784]{2,1,0:T(8,128)(2,1)} fusion(f32[12,784]{1,0:T(8,128)S(1)} %fusion, f32[12,784]{1,0:T(8,128)S(1)} %get-tuple-element.105, f32[12,784,784]{1,2,0:T(8,128)} %get-tuple-element.106, pred[784,784]{0,1:T(8,128)(4,1)S(1)} %copy-done.4, bf16[784,3,12,64]{0,3,2,1:T(8,128)(2,1)} %bitcast.117), kind=kOutput, calls=%fused_computation.98 | convolution fusion | flops 981593088 | bytes 36988672 | tf_op jit(solution)/shard_map/while/body/eval_jaxpr/hqk,khd->qhd/dot_general | solution.py:80
  142.0 3.3 fusion.89
  149.6 19.7 %gather_fusion.6 = f32[1568]{0:T(1024)S(1)} fusion(f32[784,8]{0,1:T(8,128)} %fusion.68, s32[1568]{0:T(1024)S(1)} %reshape.511), kind=kCustom, calls=%fused_computation.6 | custom fusion | bytes 25088 | tf_op jit(solution)/shard_map/jit(take_along_axis)/gather | solution.py:193
  173.0 13.3 %gather_fusion.3 = f32[1648]{0:T(1024)} fusion(f32[1568]{0:T(1024)S(1)} %pad_maximum_fusion.1, s32[2048]{0:T(1024)} %get-tuple-element.119), kind=kCustom, calls=%fused_computation.3 | custom fusion | bytes 19776 | tf_op jit(solution)/shard_map/gather | solution.py:209
  188.3 4.3 multiply_convert_fusion.1
  192.6 5.8 all-to-all-start.2
  198.4 9.0 %gather_fusion.1 = bf16[1648,768]{1,0:T(8,128)(2,1)} fusion(bf16[784,768]{1,0:T(8,128)(2,1)} %copy-done.1, s32[2048]{0:T(1024)S(1)} %copy-done.24), kind=kCustom, calls=%fused_computation.1 | custom fusion | bytes 5069248 | tf_op jit(solution)/shard_map/gather | solution.py:169
  210.6 3.5 broadcast_select_fusion
  214.1 15.9 %all-to-all-done.2 = bf16[8,206,768]{2,1,0:T(8,128)(2,1)} async-done(((bf16[8,206,768]{2,1,0:T(8,128)(2,1)}), bf16[8,206,768]{2,1,0:T(8,128)(2,1)}, u32[]{:S(2)}, u32[]{:S(2)}) %all-to-all-start.2) | async-done | bytes 2531360 | tf_op jit(solution)/shard_map/all_to_all | solution.py:213
  230.0 4.4 all-to-all-start
  237.6 28.4 %all-to-all-done = bf16[8,206,768]{2,1,0:T(8,128)(2,1)} async-done(((bf16[8,206,768]{2,1,0:T(8,128)(2,1)}), bf16[8,206,768]{2,1,0:T(8,128)(2,1)}, u32[]{:S(2)}, u32[]{:S(2)}) %all-to-all-start) | async-done | bytes 2531360 | tf_op jit(solution)/shard_map/all_to_all | solution.py:171
  269.1 52.4 %fusion.4 = (bf16[1648,3072]{1,0:T(8,128)(2,1)}, f32[1648,3072]{1,0:T(8,128)}) fusion(f32[3072]{0:T(1024)S(1)} %bitcast.132, bf16[1648,768]{1,0:T(8,128)(2,1)} %reshape.453, bf16[1,768,3072]{2,1,0:T(8,128)(2,1)} %param.24), kind=kOutput, calls=%fused_computation.21 | convolution fusion | flops 8110374912 | bytes 37638144 | tf_op jit(solution)/shard_map/dot_general | solution.py:173
  324.6 19.6 %fusion.91 = (bf16[3072]{0:T(1024)(128)(2,1)S(1)}, bf16[1648,3072]{1,0:T(8,128)(2,1)}) fusion(f32[1648,3072]{1,0:T(8,128)} %get-tuple-element.112, f32[3072]{0:T(1024)S(1)} %bitcast.133, bf16[1648,768]{1,0:T(8,128)(2,1)} %reshape.456, bf16[1,3072,768]{2,1,0:T(8,128)(2,1)} %param.26), kind=kOutput, calls=%fused_computation.192 | convolution fusion | flops 7836988416 | bytes 37644288 | tf_op jit(solution)/shard_map/dot_general | solution.py:222
  345.6 13.9 %fusion.30 = bf16[1,768,3072]{2,1,0:T(8,128)(2,1)} fusion(bf16[1648,768]{1,0:T(8,128)(2,1)} %reshape.453, bf16[1648,3072]{1,0:T(8,128)(2,1)} %get-tuple-element.118), kind=kOutput, calls=%fused_computation.62 | convolution fusion | flops 7778598912 | bytes 17375232 | tf_op jit(solution)/shard_map/rd,rf->df/dot_general | solution.py:228
  364.4 13.2 %fusion.34 = bf16[1648,768]{1,0:T(8,128)(2,1)} fusion(bf16[1648,3072]{1,0:T(8,128)(2,1)} %get-tuple-element.118, bf16[1,768,3072]{2,1,0:T(8,128)(2,1)} %param.24), kind=kOutput, calls=%fused_computation.68 | convolution fusion | flops 7777505280 | bytes 17375232 | tf_op jit(solution)/shard_map/dot_general | solution.py:230
  380.8 4.4 all-to-all-start.3
  389.0 13.1 %add_convert_fusion = bf16[1648,768]{1,0:T(8,128)(2,1)} fusion(bf16[1648,3072]{1,0:T(8,128)(2,1)} %get-tuple-element.111, bf16[1,3072,768]{2,1,0:T(8,128)(2,1)} %param.26, f32[768]{0:T(1024)S(1)} %reduce.12), kind=kOutput, calls=%fused_computation.51 | convolution fusion | flops 7778770944 | bytes 17378304 | tf_op jit(solution)/shard_map/dot_general | solution.py:175
  405.3 11.4 %all-to-all-done.3 = bf16[8,206,768]{2,1,0:T(8,128)(2,1)} async-done(((bf16[8,206,768]{2,1,0:T(8,128)(2,1)}), bf16[8,206,768]{2,1,0:T(8,128)(2,1)}, u32[]{:S(2)}, u32[]{:S(2)}) %all-to-all-start.3) | async-done | bytes 2531360 | tf_op jit(solution)/shard_map/all_to_all | solution.py:234
  416.7 4.4 all-to-all-start.1
  422.7 14.0 %fusion.31 = bf16[1,3072,768]{2,1,0:T(8,128)(2,1)} fusion(bf16[1648,3072]{1,0:T(8,128)(2,1)} %get-tuple-element.111, bf16[1648,768]{1,0:T(8,128)(2,1)} %reshape.456), kind=kOutput, calls=%fused_computation.63 | convolution fusion | flops 7778598912 | bytes 17375232 | tf_op jit(solution)/shard_map/rf,rd->fd/dot_general | solution.py:220
  439.9 9.5 %gather_fusion.5 = bf16[1568,768]{1,0:T(8,128)(2,1)} fusion(bf16[1648,768]{1,0:T(8,128)(2,1)} %reshape.458, s32[2048]{0:T(1024)S(1)} %pad_clamp_fusion.1), kind=kCustom, calls=%fused_computation.5 | custom fusion | bytes 4823168 | tf_op jit(solution)/shard_map/gather | solution.py:238
  449.4 3.3 all-to-all-done.1
  455.8 9.5 %gather_fusion.2 = bf16[1568,768]{1,0:T(8,128)(2,1)} fusion(bf16[1648,768]{1,0:T(8,128)(2,1)} %reshape.455, s32[2048]{0:T(1024)S(1)} %pad_clamp_fusion.1), kind=kCustom, calls=%fused_computation.2 | custom fusion | bytes 4823168 | tf_op jit(solution)/shard_map/gather | solution.py:190
  465.3 6.4 reshape.461
  471.7 13.8 %multiply_reduce_fusion.1 = (f32[784,2]{1,0:T(8,128)}, f32[784,768]{1,0:T(8,128)}) fusion(f32[784,2,768]{2,1,0:T(2,128)} %reshape.461, f32[784,768]{1,0:T(8,128)} %convert_element_type.163, f32[784,2]{1,0:T(8,128)} %copy.104), kind=kLoop, calls=%fused_computation.53 | loop fusion | flops 4213216 | bytes 9646336 | tf_op jit(solution)/shard_map/reduce_sum | solution.py:198
  489.6 6.3 reshape.462
  496.0 26.2 %select_reduce_fusion = f32[784,768]{1,0:T(8,128)S(1)} fusion(f32[784,2,768]{2,1,0:T(2,128)} %reshape.462, pred[784,2]{1,0:T(8,128)(4,1)} %copy.107), kind=kLoop, calls=%fused_computation.52 | loop fusion | flops 1806336 | bytes 7226912 | tf_op jit(solution)/shard_map/reduce_sum | solution.py:240
  532.2 28.6 %multiply_reduce_fusion = (f32[12,784]{1,0:T(8,128)}, f32[12,784,784]{1,2,0:T(8,128)}) fusion(f32[12,784]{1,0:T(8,128)} %log_add_fusion, f32[12,784,784]{1,2,0:T(8,128)} %get-tuple-element.106, pred[784,784]{0,1:T(8,128)(4,1)} %broadcast_compare_fusion, bf16[784,12,64]{0,2,1:T(8,128)(2,1)} %bitcast.121, bf16[784,3,12,64]{0,3,2,1:T(8,128)(2,1)} %bitcast.118), kind=kOutput, calls=%fused_computation.10 | convolution fusion | flops 980981568 | bytes 66771712 | tf_op jit(solution)/shard_map/while/body/eval_jaxpr/qhd,khd->hqk/dot_general | solution.py:102
  560.8 30.8 %multiply_convert_fusion = bf16[12,784,784]{1,2,0:T(8,128)(2,1)} fusion(f32[12,784,784]{1,2,0:T(8,128)} %get-tuple-element.115, f32[12,784]{1,0:T(8,128)} %get-tuple-element.114, f32[12,784]{1,0:T(8,128)} %log_add_fusion, f32[12,784,784]{1,2,0:T(8,128)} %get-tuple-element.106, pred[784,784]{0,1:T(8,128)(4,1)} %broadcast_compare_fusion), kind=kLoop, calls=%fused_computation.9 | loop fusion | flops 44255232 | bytes 74448640 | tf_op jit(solution)/shard_map/while/body/eval_jaxpr/convert_element_type | solution.py:107
  591.6 12.6 %fusion.60 = bf16[784,1,12,64]{0,3,2,1:T(8,128)(2,1)} fusion(bf16[12,784,784]{1,2,0:T(8,128)(2,1)} %multiply_convert_fusion, bf16[784,3,12,64]{0,3,2,1:T(8,128)(2,1)} %bitcast.119), kind=kOutput, calls=%fused_computation.102 | convolution fusion | flops 945315840 | bytes 19439616 | tf_op jit(solution)/shard_map/while/body/eval_jaxpr/hqk,qhd->khd/dot_general | solution.py:111
  604.2 10.5 %fusion.59 = bf16[784,1,12,64]{0,3,2,1:T(8,128)(2,1)} fusion(bf16[12,784,784]{1,2,0:T(8,128)(2,1)} %multiply_convert_fusion, bf16[784,3,12,64]{0,3,2,1:T(8,128)(2,1)} %bitcast.120), kind=kOutput, calls=%fused_computation.101 | convolution fusion | flops 945315840 | bytes 19439616 | tf_op jit(solution)/shard_map/while/body/eval_jaxpr/hqk,khd->qhd/dot_general | solution.py:108
  614.8 16.3 %fusion.56 = bf16[784,1,12,64]{0,3,2,1:T(8,128)(2,1)} fusion(bf16[784,12,64]{0,2,1:T(8,128)(2,1)} %bitcast.122, f32[12,784]{1,0:T(8,128)} %log_add_fusion, f32[12,784,784]{1,2,0:T(8,128)} %get-tuple-element.106, pred[784,784]{0,1:T(8,128)(4,1)} %broadcast_compare_fusion), kind=kOutput, calls=%fused_computation.100 | convolution fusion | flops 974217216 | bytes 32564224 | tf_op jit(solution)/shard_map/while/body/eval_jaxpr/hqk,qhd->khd/dot_general | solution.py:103
  637.3 6.5 fusion.86
  651.9 8.5 %fusion.50 = (f32[768]{0:T(1024)}, f32[784]{0:T(1024)}, f32[784]{0:T(1024)}, f32[768]{0:T(1024)}, f32[784,768]{1,0:T(8,128)}) fusion(bf16[784,768]{1,0:T(8,128)(2,1)} %param.16, f32[784]{0:T(1024)} %add_rsqrt_fusion.1, f32[784]{0:T(1024)} %copy-done.41, f32[768]{0:T(1024)} %param.17, bf16[784,2304]{0,1:T(8,128)(2,1)} %bitcast.124, ...), kind=kOutput, calls=%fused_computation.85 | convolution fusion | flops 2780550144 | bytes 10786048 | tf_op jit(solution)/shard_map/while/body/eval_jaxpr/dot_general | solution.py:122
  660.4 42.6 %all-reduce.1 = (f32[768]{0:T(1024)}, f32[768]{0:T(1024)}, f32[768]{0:T(1024)}, f32[768]{0:T(1024)}, f32[768,8]{0,1:T(8,128)}) all-reduce(f32[768]{0:T(1024)} %get-tuple-element.68, f32[768]{0:T(1024)} %get-tuple-element.85, f32[768]{0:T(1024)S(1)} %copy-done.45, ...), channel_id=1, replica_groups=mesh['rep'=4,'ex'=8] {'rep','ex'}, use_global_device_ids=true, to_apply=%region_24.25 | all-reduce | flops 9216 | bytes 73728 | tf_op jit(solution)/shard_map/psum | solution.py:268
  704.5 4.0 fusion.49
  714.3 121.3 %all-reduce.5.cloned.1.call-done = (f32[768,2304]{1,0:T(8,128)}, f32[768,768]{1,0:T(8,128)}) async-done(((f32[768,2304]{1,0:T(8,128)}, f32[768,768]{1,0:T(8,128)}), (f32[768,2304]{1,0:T(8,128)}, f32[768,768]{1,0:T(8,128)})) %all-reduce.5.cloned.1.call-update) | async-done | bytes 9437200 | tf_op jit(solution)/shard_map/psum | solution.py:268
  835.6 6.6 copy.126
  (218 shorter events, 110.0 us)
Async XLA Ops:
  8.0 58.0 %copy-start = (bf16[768,2304]{1,0:T(8,128)(2,1)S(1)}, bf16[768,2304]{1,0:T(8,128)(2,1)}, u32[]{:S(2)}) copy-start(bf16[768,2304]{1,0:T(8,128)(2,1)} %param.19) | copy-start | bytes 10616836
  10.8 7.3 copy-start.29
  10.8 7.3 copy-start.31
  14.3 3.8 copy-start.41
  44.8 26.1 %copy-start.16 = (s32[1568]{0:T(1024)}, s32[1568]{0:T(1024)S(1)}, u32[]{:S(2)}) copy-start(s32[1568]{0:T(1024)S(1)} %gather_fusion) | copy-start | bytes 18820
  60.8 5.2 copy-start.5
  60.8 5.2 copy-start.42
  60.9 5.1 copy-start.47
  60.9 5.1 copy-start.52
  60.9 5.1 copy-start.56
  78.4 9.2 %copy-start.23 = (s32[2048]{0:T(1024)}, s32[2048]{0:T(1024)S(1)}, u32[]{:S(2)}) copy-start(s32[2048]{0:T(1024)S(1)} %get-tuple-element.120) | copy-start | bytes 24580
  92.0 18.4 %copy-start.4 = (pred[784,784]{0,1:T(8,128)(4,1)S(1)}, pred[784,784]{0,1:T(8,128)(4,1)}, u32[]{:S(2)}) copy-start(pred[784,784]{0,1:T(8,128)(4,1)} %broadcast_compare_fusion) | copy-start | bytes 1843972
  110.4 14.6 %copy-start.14 = (f32[12,784]{1,0:T(8,128)}, f32[12,784]{1,0:T(8,128)S(1)}, u32[]{:S(2)}) copy-start(f32[12,784]{1,0:T(8,128)S(1)} %get-tuple-element.105) | copy-start | bytes 112900
  125.0 17.0 %copy-start.15 = (f32[12,784]{1,0:T(8,128)}, f32[12,784]{1,0:T(8,128)S(1)}, u32[]{:S(2)}) copy-start(f32[12,784]{1,0:T(8,128)S(1)} %fusion) | copy-start | bytes 112900
  142.0 3.8 copy-start.39
  142.0 3.8 copy-start.51
  173.0 13.3 %copy-start.26 = (s32[1648]{0:T(1024)S(1)}, s32[1648]{0:T(1024)}, u32[]{:S(2)}) copy-start(s32[1648]{0:T(1024)} %copy-done.25) | copy-start | bytes 19780
  192.6 5.9 copy-start.24
  192.6 37.4 %all-to-all-start.2 = ((bf16[8,206,768]{2,1,0:T(8,128)(2,1)}), bf16[8,206,768]{2,1,0:T(8,128)(2,1)}, u32[]{:S(2)}, u32[]{:S(2)}) async-start(bf16[8,206,768]{2,1,0:T(8,128)(2,1)} %multiply_convert_fusion.1), calls=%async_computation.2 | async-start | bytes 5111808 | tf_op jit(solution)/shard_map/all_to_all | solution.py:213
  198.4 9.0 %copy-start.50 = (pred[1648]{0:T(1024)(128)(4,1)S(1)}, pred[1648]{0:T(1024)(128)(4,1)}, u32[]{:S(2)}) copy-start(pred[1648]{0:T(1024)(128)(4,1)} %get-tuple-element.98) | copy-start | bytes 4948
  230.0 35.9 %all-to-all-start = ((bf16[8,206,768]{2,1,0:T(8,128)(2,1)}), bf16[8,206,768]{2,1,0:T(8,128)(2,1)}, u32[]{:S(2)}, u32[]{:S(2)}) async-start(bf16[8,206,768]{2,1,0:T(8,128)(2,1)} %broadcast_select_fusion), calls=%async_computation | async-start | bytes 5111808 | tf_op jit(solution)/shard_map/all_to_all | solution.py:171
  234.4 34.6 %copy-start.55 = (f32[1,3072]{1,0:T(1,128)S(1)}, f32[1,3072]{1,0:T(1,128)}, u32[]{:S(2)}) copy-start(f32[1,3072]{1,0:T(1,128)} %param.25) | copy-start | bytes 36868
  234.4 409.4 %reduce-scatter.15.cloned.1.call-start = ((), (), s32[]{:S(2)}) async-start(), calls=%async_computation.11 | async-start | bytes 245760
  237.5 409.0 %reduce-scatter.13.cloned.1.call-start = ((), (), s32[]{:S(2)}) async-start(), calls=%async_computation.10 | async-start | bytes 983040
  345.6 363.0 %reduce-scatter.9.cloned.1.call-start = ((), (), s32[]{:S(2)}) async-start(), calls=%async_computation.8 | async-start | bytes 5898240 | tf_op jit(solution)/shard_map/reduce_scatter | solution.py:281
  377.6 8.2 copy-start.36
  380.8 36.0 %all-to-all-start.3 = ((bf16[8,206,768]{2,1,0:T(8,128)(2,1)}), bf16[8,206,768]{2,1,0:T(8,128)(2,1)}, u32[]{:S(2)}, u32[]{:S(2)}) async-start(bf16[8,206,768]{2,1,0:T(8,128)(2,1)} %reshape.457), calls=%async_computation.3 | async-start | bytes 5111808 | tf_op jit(solution)/shard_map/all_to_all | solution.py:234
  416.7 36.0 %all-to-all-start.1 = ((bf16[8,206,768]{2,1,0:T(8,128)(2,1)}), bf16[8,206,768]{2,1,0:T(8,128)(2,1)}, u32[]{:S(2)}, u32[]{:S(2)}) async-start(bf16[8,206,768]{2,1,0:T(8,128)(2,1)} %reshape.454), calls=%async_computation.1 | async-start | bytes 5111808 | tf_op jit(solution)/shard_map/all_to_all | solution.py:179
  421.1 290.3 %reduce-scatter.11.cloned.1.call-start = ((), (), s32[]{:S(2)}) async-start(), calls=%async_computation.9 | async-start | bytes 5898240 | tf_op jit(solution)/shard_map/reduce_scatter | solution.py:287
  436.7 398.9 %all-reduce.5.cloned.1.call-start = ((), (), s32[]{:S(2)}) async-start(), calls=%async_computation.12 | async-start | bytes 18874368 | tf_op jit(solution)/shard_map/psum | solution.py:268
  471.7 16.3 %copy-start.18 = (s32[784,2]{0,1:T(2,128)S(1)}, s32[784,2]{0,1:T(2,128)}, u32[]{:S(2)}) copy-start(s32[784,2]{0,1:T(2,128)} %param.29) | copy-start | bytes 18820
  471.7 16.4 %copy-start.22 = (f32[784]{0:T(1024)S(1)}, f32[784]{0:T(1024)}, u32[]{:S(2)}) copy-start(f32[784]{0:T(1024)} %copy-done.21) | copy-start | bytes 9412
  471.7 16.4 %copy-start.34 = (f32[784]{0:T(1024)S(1)}, f32[784]{0:T(1024)}, u32[]{:S(2)}) copy-start(f32[784]{0:T(1024)} %copy-done.33) | copy-start | bytes 9412
  496.0 26.2 %copy-start.3 = (f32[784,768]{1,0:T(8,128)S(1)}, f32[784,768]{1,0:T(8,128)}, u32[]{:S(2)}) copy-start(f32[784,768]{1,0:T(8,128)} %copy-done.2) | copy-start | bytes 7225348
  496.0 26.2 %copy-start.20 = (f32[784]{0:T(1024)S(1)}, f32[784]{0:T(1024)}, u32[]{:S(2)}) copy-start(f32[784]{0:T(1024)} %copy-done.19) | copy-start | bytes 9412
  496.0 26.2 %copy-start.28 = (f32[784]{0:T(1024)S(1)}, f32[784]{0:T(1024)}, u32[]{:S(2)}) copy-start(f32[784]{0:T(1024)} %copy-done.27) | copy-start | bytes 9412
  496.0 26.3 %copy-start.38 = (bf16[768,8]{0,1:T(8,128)(2,1)S(1)}, bf16[768,8]{0,1:T(8,128)(2,1)}, u32[]{:S(2)}) copy-start(bf16[768,8]{0,1:T(8,128)(2,1)} %param.23) | copy-start | bytes 36868
  496.0 26.3 %copy-start.40 = (f32[768]{0:T(1024)S(1)}, f32[768]{0:T(1024)}, u32[]{:S(2)}) copy-start(f32[768]{0:T(1024)} %param.21) | copy-start | bytes 9220
  524.3 3.3 copy-start.54
  631.1 2.9 copy-start.9
  631.1 3.3 copy-start.58
  634.4 2.8 copy-start.48
  634.4 2.8 copy-start.53
  651.9 8.5 %copy-start.45 = (f32[768]{0:T(1024)S(1)}, f32[768]{0:T(1024)}, u32[]{:S(2)}) copy-start(f32[768]{0:T(1024)} %get-tuple-element.64) | copy-start | bytes 9220
  651.9 8.5 %copy-start.46 = (f32[768]{0:T(1024)S(1)}, f32[768]{0:T(1024)}, u32[]{:S(2)}) copy-start(f32[768]{0:T(1024)} %get-tuple-element.84) | copy-start | bytes 9220
  651.9 52.6 %copy-start.44 = (f32[784]{0:T(1024)S(1)}, f32[784]{0:T(1024)}, u32[]{:S(2)}) copy-start(f32[784]{0:T(1024)} %copy-done.41) | copy-start | bytes 9412
  651.9 52.6 %copy-start.49 = (f32[784]{0:T(1024)S(1)}, f32[784]{0:T(1024)}, u32[]{:S(2)}) copy-start(f32[784]{0:T(1024)} %add_rsqrt_fusion.1) | copy-start | bytes 9412
  835.6 6.6 copy-start.12
  (20 other events, 31.7 us)
Sparse Core Ops, SparseCore 0:
  237.6 21.7 reduce-scatter.14
  345.7 23.1 reduce-scatter.12
  371.2 84.8 reduce-scatter.8
  458.2 85.7 reduce-scatter.10
Sparse Core Ops, SparseCore 1:
  643.9 191.7 all-reduce.4
where the time goes:
time: 858 us; the launch traced here: 851 us
  matrix products  263 us (31%)
  local copies, waits for them, and re-layouts  182 us (21%)
  waiting for transfers between devices  180 us (21%)
  other arithmetic  147 us (17%)
  blocking collectives  42.6 us (5%)
  starting transfers between devices  19.3 us (2%)
  between operations  16.8 us (2%)
    psum x1, waiting for transfers between devices, local(): lax.psum((grad_gain_one, grad_shift_one, jnp.sum(grad_qkv_sets, axis=0),...  121 us
    dot_general x1, matrix products, local(): jnp.dot(flat_rows, first_w, preferred_element_type=jnp.float32) + first_bias  52.4 us
    psum x1, blocking collectives, local(): lax.psum((grad_gain_one, grad_shift_one, jnp.sum(grad_qkv_sets, axis=0),...  42.6 us
    convert_element_type x1, other arithmetic, attention_backward(): grad_scores = (weights * (grad_weights - inner_sum)).astype(jnp.bfloat16)  30.8 us
    dot_general x1, matrix products, attention_backward(): jnp.einsum('qhd,khd->hqk', grad_mix, values, preferred_element_type=jnp.f...  28.6 us
    all_to_all x1, waiting for transfers between devices, local(): lax.all_to_all(dispatch, 'ex', split_axis=0, concat_axis=0, tiled=True)  28.4 us
    reduce_sum x1, other arithmetic, local(): jnp.sum(jnp.where(kept_mask[:, :, None], grad_pairs, 0.0), axis=1)  26.2 us
    gather x5, local copies, waits for them, and re-layouts, local(): chosen_probs = jnp.take_along_axis(router_probs, routes, axis=1)  24.8 us
  transfers between devices with their start and end apart: 9, of which 5 were waited for; matrix products, arithmetic and copies ran while one was open for 47% of the time, Pallas kernels for 0%

commit v1 on v0

v1 whole, which is shorter than its diff:
```python
import functools

import jax
import jax.numpy as jnp
from jax import lax
from jax.experimental import pallas as pl
from jax.experimental.pallas import tpu as pltpu
from jax.sharding import PartitionSpec as P

HEADS = 12
HEAD_DIM = 64
PATCH_S = 196
PATCH_L = 576
GROUP = 4
LANES = GROUP * HEAD_DIM

EPS = 1e-06
NEG = -1e30
SCALE = HEAD_DIM ** (-0.5)
LOG2E = 1.4426950408889634
INV_ROOT_TAU = 0.3989422804014327
PHI_RATE = 0.3
PHI_FIT = (
    0.11962929778234231,
    0.1207539739440115,
    0.09991336806177473,
    0.1285620774229096,
    -0.05368457415108751,
    0.20635459820469867,
    -0.1572037608415104,
    0.03567494667893269,
)
F32 = jnp.float32
BF16 = jnp.bfloat16


def dot_nn(a, b):
    return lax.dot_general(a, b, (((1,), (0,)), ((), ())), preferred_element_type=F32)


def dot_nt(a, b):
    return lax.dot_general(a, b, (((1,), (1,)), ((), ())), preferred_element_type=F32)


def dot_tn(a, b):
    return lax.dot_general(a, b, (((0,), (0,)), ((), ())), preferred_element_type=F32)


def iota(shape, dim):
    return lax.broadcasted_iota(jnp.int32, shape, dim)


def call(body, out_shape, in_specs=None, out_specs=None, grid=None, scratch=(), cost=None, name=None):
    args = dict(out_shape=out_shape, scratch_shapes=list(scratch), name=name)
    if grid is not None:
        args["grid"] = grid
    if in_specs is not None:
        args["in_specs"] = in_specs
    if out_specs is not None:
        args["out_specs"] = out_specs
    if cost is not None:
        args["cost_estimate"] = pl.CostEstimate(
            flops=int(cost[0]), bytes_accessed=int(cost[1]), transcendentals=int(cost[2])
        )
    return pl.pallas_call(
        body,
        compiler_params=pltpu.CompilerParams(vmem_limit_bytes=60 * 1024 * 1024),
        **args,
    )


def whole(shape, memory_space=None):
    zeros = (0,) * len(shape)
    if memory_space is not None:
        return pl.BlockSpec(shape, lambda *_: zeros, memory_space=memory_space)
    return pl.BlockSpec(shape, lambda *_: zeros)


def norm_stats(values):
    average = jnp.mean(values, axis=-1, keepdims=True)
    centered = values - average
    variance = jnp.mean(centered * centered, axis=-1, keepdims=True)
    inverse = lax.rsqrt(variance + EPS)
    return centered * inverse, inverse


def norm_grad(grad, scaled, inverse, gain):
    through = grad * gain
    first = jnp.mean(through, axis=-1, keepdims=True)
    second = jnp.mean(through * scaled, axis=-1, keepdims=True)
    return inverse * (through - first - scaled * second)


def row_chunk(rows):
    for size in (112, 128, 64, 48, 32, 16):
        if rows % size == 0:
            return size
    return rows


def prep_body(experts, cap, cap_pad, routes_ref, prio_ref, cot_ref, slot_ref, col_ref, out_ref):
    toks = cot_ref.shape[0]
    prio = prio_ref[...].astype(F32)
    prio_col = jnp.sum(
        jnp.where(iota((toks, toks), 0) == iota((toks, toks), 1), prio, 0.0), axis=1, keepdims=True
    )
    below = jnp.where(prio_col < prio, 1.0, 0.0).astype(BF16)
    labels = iota((experts, toks), 0)
    first = routes_ref[0:1, :]
    second = routes_ref[1:2, :]
    hot_one = jnp.where(labels == first, 1.0, 0.0)
    hot_two = jnp.where(labels == second, 1.0, 0.0)
    count_one = dot_nn(hot_one.astype(BF16), below)
    count_two = dot_nn(hot_two.astype(BF16), below)
    total_one = jnp.sum(hot_one, axis=1, keepdims=True)
    place_one = jnp.sum(hot_one * count_one, axis=0, keepdims=True)
    place_two = jnp.sum(hot_two * (count_two + total_one), axis=0, keepdims=True)
    slot_one = jnp.where(
        place_one < cap, first * cap_pad + place_one.astype(jnp.int32), -1
    )
    slot_two = jnp.where(
        place_two < cap, second * cap_pad + place_two.astype(jnp.int32), -1
    )
    slot_ref[0:1, :] = slot_one
    slot_ref[1:2, :] = slot_two
    eye = iota((toks, toks), 0) == iota((toks, toks), 1)
    col_one = jnp.sum(jnp.where(eye, slot_one, 0), axis=1, keepdims=True)
    col_two = jnp.sum(jnp.where(eye, slot_two, 0), axis=1, keepdims=True)
    lane = iota((toks, 128), 1)
    col_ref[...] = jnp.where(lane == 0, col_one, jnp.where(lane == 1, col_two, -1))

    def block(expert, carry):
        spots = iota((cap_pad, toks), 0) + expert * cap_pad
        hot = jnp.where((spots == slot_one) | (spots == slot_two), 1.0, 0.0).astype(BF16)
        out_ref[expert] = dot_nn(hot, cot_ref[...]).astype(BF16)
        return carry

    lax.fori_loop(0, experts, block, 0)


def region_bias(kind, start, size, lower, upper, by_rows=True):
    first = iota((size, size), 0) + start
    second = iota((size, size), 1) + start
    if kind == 1:
        seg = lambda p: jnp.where(p < PATCH_L, 0, jnp.where(p < PATCH_L + PATCH_S, 1, 2))
    else:
        seg = lambda p: (
            jnp.where(p >= PATCH_S, 1, 0)
            + jnp.where(p >= 2 * PATCH_S, 1, 0)
            + jnp.where(p >= 3 * PATCH_S, 1, 0)
        )
    linked = seg(first) == seg(second)
    inside = (first >= lower) & (first < upper)
    return jnp.where(linked & inside, 0.0, NEG)


def kind_regions(kind, toks):
    if kind == 1:
        return ((0, PATCH_L, 0, PATCH_L, False), (PATCH_L, toks - PATCH_L, PATCH_L, toks, True))
    half = 2 * PATCH_S
    size = -(-half // 16) * 16
    begin = toks - size
    return ((0, size, 0, half, True), (begin, size, half, toks, True))


def forward_body(
    experts,
    cap_pad,
    kind_ref,
    x_ref,
    gain_one_ref,
    shift_one_ref,
    wq_ref,
    wk_ref,
    wv_ref,
    wo_ref,
    gain_two_ref,
    shift_two_ref,
    router_ref,
    routes_ref,
    slot_ref,
    qkv_ref,
    mix_ref,
    lse_ref,
    low_ref,
    residual_ref,
    lowered_ref,
    probs_ref,
    send_ref,
    acc_ref,
    out_ref,
    lse_scr,
    kept_ref,
):
    step = pl.program_id(0)
    steps = pl.num_programs(0)
    toks, width = x_ref.shape
    chunk = row_chunk(toks)

    @pl.when(step == 0)
    def _():
        def rows(i, carry):
            spot = pl.ds(pl.multiple_of(i * chunk, 16), chunk)
            scaled, _ = norm_stats(x_ref[spot, :].astype(F32))
            low_ref[spot, :] = (scaled * gain_one_ref[...] + shift_one_ref[...]).astype(BF16)
            return carry

        lax.fori_loop(0, toks // chunk, rows, 0)
        lse_scr[...] = jnp.zeros_like(lse_scr)

    low = low_ref[...]
    qkv_ref[0, :, 0:LANES] = dot_nn(low, wq_ref[...]).astype(BF16)
    qkv_ref[0, :, LANES : 2 * LANES] = dot_nn(low, wk_ref[...]).astype(BF16)
    qkv_ref[0, :, 2 * LANES : 3 * LANES] = dot_nn(low, wv_ref[...]).astype(BF16)

    def attend(kind):
        for start, size, lower, upper, masked in kind_regions(kind, toks):
            bias = region_bias(kind, start, size, lower, upper) if masked else None
            spot = slice(start, start + size)
            out_ref[lower:upper, :] = jnp.zeros((upper - lower, LANES), F32)

            def head(h, carry):
                mine = (iota((1, LANES), 1) // HEAD_DIM) == h
                queries = jnp.where(mine, qkv_ref[0, spot, 0:LANES], 0) * jnp.asarray(SCALE, BF16)
                scores = dot_nt(queries, qkv_ref[0, spot, LANES : 2 * LANES])
                if bias is not None:
                    scores = scores + bias
                top = jnp.max(scores, axis=-1, keepdims=True)
                weights = jnp.exp(scores - top)
                total = jnp.sum(weights, axis=-1, keepdims=True)
                values = jnp.where(mine, qkv_ref[0, spot, 2 * LANES : 3 * LANES], 0)
                mixed = dot_nn(weights.astype(BF16), values) * (1.0 / total)
                logsum = top + jnp.log(total)
                cut = slice(lower - start, upper - start)
                out_ref[lower:upper, :] += mixed[cut]
                lane = iota((upper - lower, 128), 1) == step * GROUP + h
                lse_scr[lower:upper, :] = jnp.where(lane, logsum[cut], lse_scr[lower:upper, :])
                return carry

            lax.fori_loop(0, GROUP, head, 0)

    @pl.when(kind_ref[0] == 1)
    def _():
        attend(1)

    @pl.when(kind_ref[0] != 1)
    def _():
        attend(0)

    mix = out_ref[...].astype(BF16)
    mix_ref[...] = mix
    branch = dot_nn(mix, wo_ref[...])

    @pl.when(step == 0)
    def _():
        acc_ref[...] = x_ref[...].astype(F32) + branch

    @pl.when(step > 0)
    def _():
        acc_ref[...] += branch

    @pl.when(step == steps - 1)
    def _():
        lse_ref[...] = lse_scr[...].T[0 : lse_ref.shape[0], 0:toks]

        def rows(i, carry):
            spot = pl.ds(pl.multiple_of(i * chunk, 16), chunk)
            residual = acc_ref[spot, :]
            residual_ref[spot, :] = residual
            scaled, _ = norm_stats(residual)
            lowered_ref[spot, :] = (scaled * gain_two_ref[...] + shift_two_ref[...]).astype(BF16)
            return carry

        lax.fori_loop(0, toks // chunk, rows, 0)
        lowered = lowered_ref[...]
        logits = dot_nt(router_ref[...], lowered)
        top = jnp.max(logits, axis=0, keepdims=True)
        raised = jnp.exp(logits - top)
        probs = raised / jnp.sum(raised, axis=0, keepdims=True)
        probs_ref[...] = probs
        labels = iota((experts, toks), 0)
        slot_one = slot_ref[0:1, :]
        slot_two = slot_ref[1:2, :]
        gate_one = jnp.sum(jnp.where(labels == routes_ref[0:1, :], probs, 0.0), axis=0, keepdims=True)
        gate_two = jnp.sum(jnp.where(labels == routes_ref[1:2, :], probs, 0.0), axis=0, keepdims=True)
        gate_one = jnp.where(slot_one >= 0, gate_one, 0.0)
        gate_two = jnp.where(slot_two >= 0, gate_two, 0.0)
        which = iota((16, toks), 0)

        def parts(gate):
            high = gate.astype(BF16).astype(F32)
            rest = gate - high
            return jnp.where(which == 0, high, jnp.where(which == 1, rest, 0.0)).astype(BF16)

        kept_ref[0] = parts(gate_one)
        kept_ref[1] = parts(gate_two)
        wide = -(-cap_pad // 128) * 128

        def block(expert, carry):
            spots = iota((wide, toks), 0) + expert * cap_pad
            hot_one = jnp.where(spots == slot_one, 1.0, 0.0)
            hot_two = jnp.where(spots == slot_two, 1.0, 0.0)
            gates = dot_nt(kept_ref[0], hot_one.astype(BF16)) + dot_nt(
                kept_ref[1], hot_two.astype(BF16)
            )
            picked = dot_nn((hot_one + hot_two)[0:cap_pad].astype(BF16), lowered)
            gates = jnp.concatenate([gates, jnp.zeros((16, width - wide), F32)], axis=1)
            row = iota((cap_pad, width), 0)
            picked = jnp.where(
                row == cap_pad - 2, gates[0:1], jnp.where(row == cap_pad - 1, gates[1:2], picked)
            )
            send_ref[expert] = picked.astype(BF16)
            return carry

        lax.fori_loop(0, experts, block, 0)


def phi_parts(v):
    a = jnp.abs(v)
    bell = jnp.exp(-0.5 * (v * v))
    t = 1.0 / (1.0 + PHI_RATE * a)
    poly = PHI_FIT[-1] * t
    for part in PHI_FIT[-2::-1]:
        poly = (poly + part) * t
    tail = poly * bell
    return jnp.where(v > 0, 1.0 - tail, tail), bell


def expert_body(
    x_ref,
    u_ref,
    w_ref,
    bias_ref,
    back_ref,
    z_ref,
    hidden_ref,
    grad_ref,
    g_ref,
    gg_ref,
    bin_ref,
    bback_ref,
    gate_scr,
    acc_scr,
):
    step = pl.program_id(0)
    blocks, cap_pad, width = x_ref.shape
    wide = gg_ref.shape[2]
    tile = w_ref.shape[1]

    @pl.when(step == 0)
    def _():
        bback_ref[...] = jnp.zeros_like(bback_ref)

        def block(b, carry):
            tail = x_ref[b, cap_pad - 16 : cap_pad, 0:wide].astype(F32)
            gate_row = tail[14:15] + tail[15:16]
            same = iota((cap_pad, wide), 0) == iota((cap_pad, wide), 1)
            gate = jnp.sum(jnp.where(same, gate_row, 0.0), axis=1, keepdims=True)
            gate_scr[b] = jnp.broadcast_to(gate, (cap_pad, 128))
            rows = u_ref[b].astype(F32)
            made = (rows * gate).astype(BF16)
            g_ref[b] = made
            bback_ref[0:1, :] += jnp.sum(made.astype(F32), axis=0, keepdims=True)
            part = rows * back_ref[...]
            total = part[:, 0:128]
            for i in range(1, width // 128):
                total = total + part[:, i * 128 : (i + 1) * 128]
            acc_scr[b] = total
            return carry

        lax.fori_loop(0, blocks, block, 0)

    bin_ref[...] = jnp.zeros_like(bin_ref)

    def block(b, carry):
        pre = dot_nn(x_ref[b], w_ref[...]) + bias_ref[...]
        cdf, bell = phi_parts(pre)
        hidden = (pre * cdf).astype(BF16)
        hidden_ref[b] = hidden
        z = z_ref[b].astype(F32)
        part = hidden.astype(F32) * z
        total = acc_scr[b]
        for i in range(tile // 128):
            total = total + part[:, i * 128 : (i + 1) * 128]
        acc_scr[b] = total
        slope = cdf + pre * (bell * INV_ROOT_TAU)
        gate = jnp.concatenate([gate_scr[b]] * (tile // 128), axis=1)
        grad = (gate * z * slope).astype(BF16)
        grad_ref[b] = grad
        bin_ref[0:1, :] += jnp.sum(grad.astype(F32), axis=0, keepdims=True)
        return carry

    lax.fori_loop(0, blocks, block, 0)

    @pl.when(step == pl.num_programs(0) - 1)
    def _():
        def last(b, carry):
            column = jnp.sum(acc_scr[b], axis=1, keepdims=True)
            same = iota((cap_pad, wide), 0) == iota((cap_pad, wide), 1)
            gg_ref[b, 0:1, :] = jnp.sum(jnp.where(same, column, 0.0), axis=0, keepdims=True)
            return carry

        lax.fori_loop(0, blocks, last, 0)


def combine_body(experts, kept_ref, gates_ref, residual_ref, back_ref, result_ref):
    blocks, cap_pad, width = back_ref.shape
    toks = residual_ref.shape[0]
    chunk = row_chunk(toks)
    flat = back_ref[...].reshape(blocks * cap_pad, width)

    def rows(i, carry):
        spot = pl.ds(pl.multiple_of(i * chunk, 16), chunk)
        spots = iota((chunk, blocks * cap_pad), 1)
        hot = jnp.where(spots == kept_ref[spot, 0:1], gates_ref[spot, 0:1], 0.0) + jnp.where(
            spots == kept_ref[spot, 1:2], gates_ref[spot, 1:2], 0.0
        )
        result_ref[spot, :] = (residual_ref[spot, :] + dot_nn(hot.astype(BF16), flat)).astype(BF16)
        return carry

    lax.fori_loop(0, toks // chunk, rows, 0)


def row_grad_body(
    experts,
    col_ref,
    slot_ref,
    routes_ref,
    probs_ref,
    lowered_ref,
    residual_ref,
    cot_ref,
    gain_ref,
    router_ref,
    back_ref,
    grad_ref,
    low_ref,
    small_ref,
    route_grad_ref,
    logit_ref,
):
    blocks, cap_pad, width = back_ref.shape
    toks = lowered_ref.shape[0]
    chunk = row_chunk(toks)
    labels = iota((experts, toks), 0)
    slot_one = slot_ref[0:1, :]
    slot_two = slot_ref[1:2, :]
    wide = -(-cap_pad // 128) * 128
    gate_one = jnp.zeros((16, toks), F32)
    gate_two = jnp.zeros((16, toks), F32)

    def block(expert, carry):
        one, two = carry
        spots = iota((cap_pad, toks), 0) + expert * cap_pad
        tail = back_ref[expert, cap_pad - 16 : cap_pad, 0:cap_pad]
        hot_one = jnp.where(spots == slot_one, 1.0, 0.0).astype(BF16)
        hot_two = jnp.where(spots == slot_two, 1.0, 0.0).astype(BF16)
        return one + dot_nn(tail, hot_one), two + dot_nn(tail, hot_two)

    gate_one, gate_two = lax.fori_loop(0, experts, block, (gate_one, gate_two))
    gate_one = gate_one[14:15] + gate_one[15:16]
    gate_two = gate_two[14:15] + gate_two[15:16]
    probs = probs_ref[...]
    grad_probs = jnp.where(labels == routes_ref[0:1, :], gate_one, 0.0) + jnp.where(
        labels == routes_ref[1:2, :], gate_two, 0.0
    )
    grad_logits = probs * (grad_probs - jnp.sum(probs * grad_probs, axis=0, keepdims=True))
    grad_logits = grad_logits.astype(BF16)
    route_grad_ref[...] = dot_nn(grad_logits, lowered_ref[...])
    logit_ref[...] = dot_tn(grad_logits, router_ref[...])
    small_ref[...] = jnp.zeros_like(small_ref)
    flat = back_ref[...].reshape(blocks * cap_pad, width)

    def rows(i, carry):
        spot = pl.ds(pl.multiple_of(i * chunk, 16), chunk)
        spots = iota((chunk, blocks * cap_pad), 1)
        hot = jnp.where(
            (spots == col_ref[spot, 0:1]) | (spots == col_ref[spot, 1:2]), 1.0, 0.0
        ).astype(BF16)
        grad = logit_ref[spot, :] + dot_nn(hot, flat)
        scaled, inverse = norm_stats(residual_ref[spot, :])
        small_ref[0:1, :] += jnp.sum(grad * scaled, axis=0, keepdims=True)
        small_ref[1:2, :] += jnp.sum(grad, axis=0, keepdims=True)
        total = cot_ref[spot, :].astype(F32) + norm_grad(grad, scaled, inverse, gain_ref[...])
        grad_ref[spot, :] = total
        low_ref[spot, :] = total.astype(BF16)
        return carry

    lax.fori_loop(0, toks // chunk, rows, 0)


def backward_body(
    first_group,
    kind_ref,
    up_ref,
    wo_ref,
    qkv_ref,
    mix_ref,
    lse_ref,
    grad_ref,
    do_ref,
    delta_ref,
    dq_ref,
    dk_ref,
    dv_ref,
):
    toks = up_ref.shape[0]
    group = pl.program_id(0) + first_group
    do = dot_nt(up_ref[...], wo_ref[...]).astype(BF16)
    do_ref[...] = do
    both = do.astype(F32) * mix_ref[...].astype(F32)
    high = both.astype(BF16)
    rest = (both - high.astype(F32)).astype(BF16)
    owner = jnp.where(iota((16, LANES), 1) // HEAD_DIM == iota((16, LANES), 0), 1.0, 0.0).astype(BF16)
    delta_ref[...] = dot_nt(owner, high) + dot_nt(owner, rest)
    dq_ref[...] = jnp.zeros_like(dq_ref)
    dk_ref[...] = jnp.zeros_like(dk_ref)
    dv_ref[...] = jnp.zeros_like(dv_ref)

    def attend(kind):
        for start, size, lower, upper, masked in kind_regions(kind, toks):
            bias = region_bias(kind, start, size, lower, upper) if masked else None
            spot = slice(start, start + size)

            def head(h, carry):
                mine = (iota((1, LANES), 1) // HEAD_DIM) == h
                queries = jnp.where(mine, qkv_ref[0, spot, 0:LANES], 0) * jnp.asarray(SCALE, BF16)
                keys_all = qkv_ref[0, spot, LANES : 2 * LANES]
                own = jnp.where(mine, do_ref[spot, :], 0)
                logsum = lse_ref[pl.ds(group * GROUP + h, 1), :][:, spot]
                delta = delta_ref[pl.ds(h, 1), :][:, spot]
                scores = dot_nt(keys_all, queries)
                if bias is not None:
                    scores = scores + bias
                weights = jnp.exp(scores - logsum)
                grad_weights = dot_nt(qkv_ref[0, spot, 2 * LANES : 3 * LANES], own)
                grad_scores = (weights * (grad_weights - delta)).astype(BF16)
                dv_ref[spot, :] += dot_nn(weights.astype(BF16), own)
                dk_ref[spot, :] += dot_nn(grad_scores, queries)
                dq_ref[spot, :] += dot_tn(grad_scores, jnp.where(mine, keys_all, 0))
                return carry

            lax.fori_loop(0, GROUP, head, 0)

    @pl.when(kind_ref[0] == 1)
    def _():
        attend(1)

    @pl.when(kind_ref[0] != 1)
    def _():
        attend(0)

    grad_ref[:, 0:LANES] = (dq_ref[...] * SCALE).astype(BF16)
    grad_ref[:, LANES : 2 * LANES] = dk_ref[...].astype(BF16)
    grad_ref[:, 2 * LANES : 3 * LANES] = dv_ref[...].astype(BF16)


def final_body(groups, *refs):
    packed = refs[0:groups]
    weights = refs[groups : 2 * groups]
    x_ref, gain_ref, up_ref, out_ref, small_ref, acc_ref = refs[2 * groups :]
    toks = x_ref.shape[0]
    chunk = row_chunk(toks)
    total = dot_nt(packed[0][...], weights[0][...])
    for i in range(1, groups):
        total = total + dot_nt(packed[i][...], weights[i][...])
    acc_ref[...] = total
    small_ref[...] = jnp.zeros_like(small_ref)

    def rows(i, carry):
        spot = pl.ds(pl.multiple_of(i * chunk, 16), chunk)
        grad = acc_ref[spot, :]
        scaled, inverse = norm_stats(x_ref[spot, :].astype(F32))
        small_ref[0:1, :] += jnp.sum(grad * scaled, axis=0, keepdims=True)
        small_ref[1:2, :] += jnp.sum(grad, axis=0, keepdims=True)
        out_ref[spot, :] = (
            up_ref[spot, :] + norm_grad(grad, scaled, inverse, gain_ref[...])
        ).astype(BF16)
        return carry

    lax.fori_loop(0, toks // chunk, rows, 0)


def swap(values, axis, bit, size):
    return lax.ppermute(values, axis, [(j, j ^ bit) for j in range(size)])


def add_pair(a, b):
    return (a.astype(F32) + b.astype(F32)).astype(a.dtype)


def halve(values, axis, bit, size):
    mine = (lax.axis_index(axis) // bit) % 2
    halves = values.reshape((2, values.shape[0] // 2) + values.shape[1:])
    keep = lax.dynamic_index_in_dim(halves, mine, 0, keepdims=False)
    send = lax.dynamic_index_in_dim(halves, 1 - mine, 0, keepdims=False)
    return add_pair(keep, swap(send, axis, bit, size))


def unhalve(values, axis, bit, size):
    mine = (lax.axis_index(axis) // bit) % 2
    other = swap(values, axis, bit, size)
    return jnp.concatenate(
        [jnp.where(mine == 0, values, other), jnp.where(mine == 0, other, values)], axis=0
    )


def axis_bits(axis, size):
    bits = []
    bit = 1
    while bit < size:
        bits.append((axis, bit, size))
        bit *= 2
    return bits


def sum_all(values, sizes):
    inner = axis_bits("ex", sizes["ex"])
    outer = axis_bits("rep", sizes["rep"])
    core, plane = inner[:1], inner[1:]
    shape = values.shape
    if shape[0] % (2 * sizes["ex"] * sizes["rep"]):
        values = values.reshape(-1, 128)
    half = values.shape[0] // 2
    done = []
    for part, order in (
        (values[:half], core + plane + outer),
        (values[half:], core + plane[::-1] + outer),
    ):
        for hop in order:
            part = halve(part, *hop)
        for hop in order[::-1]:
            part = unhalve(part, *hop)
        done.append(part)
    return jnp.concatenate(done, axis=0).reshape(shape)


def sum_small(values, bits):
    for hop in bits:
        values = values + swap(values, *hop)
    return values


def local(
    sizes,
    tokens,
    gain_one,
    shift_one,
    w_qkv,
    w_out,
    gain_two,
    shift_two,
    w_router,
    w_in,
    bias_in,
    w_back,
    bias_back,
    cotangent,
    routes,
    priority,
    image_kind,
):
    toks, width = tokens.shape
    experts = w_router.shape[1]
    hidden_units = w_in.shape[2]
    cap = (42 * toks + 20 * experts - 1) // (20 * experts)
    cap_pad = -(-(cap + 2) // 16) * 16
    wide = -(-cap_pad // 128) * 128
    groups = HEADS // GROUP
    first_w, second_w = w_in[0], w_back[0]
    routes_row = routes.T
    router_row = w_router.T
    sds = jax.ShapeDtypeStruct
    dispatched = (experts, cap_pad, width)

    slots, slot_col, up_rows = call(
        functools.partial(prep_body, experts, cap, cap_pad),
        (sds((8, toks), jnp.int32), sds((toks, 128), jnp.int32), sds(dispatched, BF16)),
        cost=(4e9, 6e6, 0),
        name="prep",
    )(routes_row, priority, cotangent)
    up_in = lax.all_to_all(up_rows, "ex", split_axis=0, concat_axis=0, tiled=True)

    gains = [a.reshape(1, width) for a in (gain_one, shift_one, gain_two, shift_two)]
    col = lambda offset: pl.BlockSpec((width, LANES), lambda g: (0, offset * groups + g))
    smem = pl.BlockSpec(memory_space=pltpu.SMEM)
    per_group = lambda: pl.BlockSpec((1, toks, 3 * LANES), lambda g: (g, 0, 0))
    qkv, mix, logsum, low_one, residual, lowered, probs, sent = call(
        functools.partial(forward_body, experts, cap_pad),
        (
            sds((groups, toks, 3 * LANES), BF16),
            sds((toks, width), BF16),
            sds((16, toks), F32),
            sds((toks, width), BF16),
            sds((toks, width), F32),
            sds((toks, width), BF16),
            sds((experts, toks), F32),
            sds(dispatched, BF16),
        ),
        in_specs=[
            smem,
            whole((toks, width)),
            whole((1, width)),
            whole((1, width)),
            col(0),
            col(1),
            col(2),
            pl.BlockSpec((LANES, width), lambda g: (g, 0)),
            whole((1, width)),
            whole((1, width)),
            whole((experts, width)),
            whole((2, toks)),
            whole((8, toks)),
        ],
        out_specs=[
            per_group(),
            pl.BlockSpec((toks, LANES), lambda g: (0, g)),
            whole((16, toks)),
            whole((toks, width)),
            whole((toks, width)),
            whole((toks, width)),
            whole((experts, toks)),
            whole(dispatched),
        ],
        grid=(groups,),
        scratch=[
            pltpu.VMEM((toks, width), F32),
            pltpu.VMEM((toks, LANES), F32),
            pltpu.VMEM((-(-toks // 128) * 128, 128), F32),
            pltpu.VMEM((2, 16, toks), BF16),
        ],
        cost=(10e9, 20e6, 4e6),
        name="attend",
    )(
        image_kind,
        tokens,
        gains[0],
        gains[1],
        w_qkv,
        w_qkv,
        w_qkv,
        w_out,
        gains[2],
        gains[3],
        router_row,
        routes_row,
        slots,
    )
    rows_in = lax.all_to_all(sent, "ex", split_axis=0, concat_axis=0, tiled=True)

    blocks = rows_in.shape[0]
    flat_up = up_in.reshape(-1, width)
    z = dot_nt(flat_up, second_w).astype(BF16).reshape(blocks, cap_pad, hidden_units)
    tile = 512 if hidden_units % 512 == 0 else 256
    ff = lambda: pl.BlockSpec((blocks, cap_pad, tile), lambda j: (0, 0, j))
    hidden, grad_pre, grad_slots, grad_gate, bin_sum, bback_sum = call(
        expert_body,
        (
            sds((blocks, cap_pad, hidden_units), BF16),
            sds((blocks, cap_pad, hidden_units), BF16),
            sds((blocks, cap_pad, width), BF16),
            sds((blocks, 8, wide), F32),
            sds((8, hidden_units), F32),
            sds((8, width), F32),
        ),
        in_specs=[
            whole((blocks, cap_pad, width)),
            whole((blocks, cap_pad, width)),
            pl.BlockSpec((width, tile), lambda j: (0, j)),
            pl.BlockSpec((1, tile), lambda j: (0, j)),
            whole((1, width)),
            ff(),
        ],
        out_specs=[
            ff(),
            ff(),
            whole((blocks, cap_pad, width)),
            whole((blocks, 8, wide)),
            pl.BlockSpec((8, tile), lambda j: (0, j)),
            whole((8, width)),
        ],
        grid=(hidden_units // tile,),
        scratch=[
            pltpu.VMEM((blocks, cap_pad, 128), F32),
            pltpu.VMEM((blocks, cap_pad, 128), F32),
        ],
        cost=(8e9, 40e6, 10e6),
        name="expert",
    )(rows_in, up_in, first_w, bias_in, bias_back, z)
    flat_rows = rows_in.reshape(-1, width)
    flat_hidden = hidden.reshape(-1, hidden_units)
    flat_pre = grad_pre.reshape(-1, hidden_units)
    flat_slots = grad_slots.reshape(-1, width)

    gate_row = grad_gate[:, 0:1, :]
    gate_high = gate_row.astype(BF16).astype(F32)
    gate_rows = jnp.concatenate([gate_high, gate_row - gate_high], axis=1)
    gate_rows = jnp.pad(gate_rows, ((0, 0), (cap_pad - 2, 0), (0, width - wide)))
    grad_rows = dot_nt(flat_pre, first_w).reshape(blocks, cap_pad, width)
    tail = lax.broadcasted_iota(jnp.int32, (blocks, cap_pad, width), 1) >= cap_pad - 2
    grad_rows = jnp.where(tail, gate_rows, grad_rows).astype(BF16)
    grad_back = lax.all_to_all(grad_rows, "ex", split_axis=0, concat_axis=0, tiled=True)

    second_grad = dot_tn(flat_hidden, flat_slots).astype(BF16)
    second_out = lax.psum_scatter(second_grad, "rep", scatter_dimension=0, tiled=True)
    first_grad = dot_tn(flat_rows, flat_pre).astype(BF16)
    first_out = lax.psum_scatter(first_grad, "rep", scatter_dimension=0, tiled=True)
    produced = (dot_nn(flat_hidden, second_w) + bias_back).astype(BF16)
    returned = lax.all_to_all(
        produced.reshape(blocks, cap_pad, width), "ex", split_axis=0, concat_axis=0, tiled=True
    )

    reps = sizes["rep"]
    bias_sum = sum_small(
        jnp.concatenate([bin_sum[0], bback_sum[0]]).reshape(-1, 128), axis_bits("rep", reps)
    ).reshape(-1)
    rank = lax.axis_index("rep")
    bin_out = lax.dynamic_slice_in_dim(bias_sum, rank * (hidden_units // reps), hidden_units // reps)
    bback_out = lax.dynamic_slice_in_dim(
        bias_sum, hidden_units + rank * (width // reps), width // reps
    )

    grad_residual, grad_branch, small_two, route_grad = call(
        functools.partial(row_grad_body, experts),
        (
            sds((toks, width), F32),
            sds((toks, width), BF16),
            sds((8, width), F32),
            sds((experts, width), F32),
        ),
        scratch=[pltpu.VMEM((toks, width), F32)],
        cost=(5e9, 12e6, 0),
        name="row_grad",
    )(
        slot_col,
        slots,
        routes_row,
        probs,
        lowered,
        residual,
        cotangent,
        gains[2],
        router_row,
        grad_back,
    )
    out_grad = sum_all(dot_tn(mix, grad_branch).astype(BF16), sizes)

    packed_grads = []
    qkv_sums = []
    for g in range(groups):
        packed = call(
            functools.partial(backward_body, g),
            sds((toks, 3 * LANES), BF16),
            in_specs=[
                smem,
                whole((toks, width)),
                pl.BlockSpec((LANES, width), lambda i, g=g: (g, 0)),
                pl.BlockSpec((1, toks, 3 * LANES), lambda i, g=g: (g, 0, 0)),
                pl.BlockSpec((toks, LANES), lambda i, g=g: (0, g)),
                whole((16, toks)),
            ],
            out_specs=whole((toks, 3 * LANES)),
            grid=(1,),
            scratch=[
                pltpu.VMEM((toks, LANES), BF16),
                pltpu.VMEM((16, toks), F32),
                pltpu.VMEM((toks, LANES), F32),
                pltpu.VMEM((toks, LANES), F32),
                pltpu.VMEM((toks, LANES), F32),
            ],
            cost=(8e9, 6e6, 2e6),
            name="attend_back_" + "abcdef"[g],
        )(image_kind, grad_branch, w_out, qkv, mix, logsum)
        packed_grads.append(packed)
        qkv_sums.append(sum_all(dot_tn(low_one, packed).astype(BF16), sizes))

    w_groups = [
        jnp.concatenate(
            [w_qkv[:, (p * groups + g) * LANES : (p * groups + g + 1) * LANES] for p in range(3)],
            axis=1,
        )
        for g in range(groups)
    ]
    grad_tokens, small_one = call(
        functools.partial(final_body, groups),
        (sds((toks, width), BF16), sds((8, width), F32)),
        scratch=[pltpu.VMEM((toks, width), F32)],
        cost=(3e9, 14e6, 0),
        name="final",
    )(*packed_grads, *w_groups, tokens, gains[0], grad_residual)

    gates = jnp.take_along_axis(probs, routes_row, axis=0)
    gates = gates.T
    result = call(
        functools.partial(combine_body, experts),
        sds((toks, width), BF16),
        cost=(2e9, 8e6, 0),
        name="combine",
    )(slot_col, gates, residual, returned)

    everyone = axis_bits("ex", sizes["ex"]) + axis_bits("rep", reps)
    small_two = sum_small(jnp.concatenate([small_two, route_grad], axis=0), everyone)
    small_one = sum_small(small_one, everyone)
    qkv_grad = jnp.concatenate(
        [
            qkv_sums[g][:, p * LANES : (p + 1) * LANES]
            for p in range(3)
            for g in range(groups)
        ],
        axis=1,
    ).astype(F32)
    return (
        result,
        grad_tokens,
        small_one[0],
        small_one[1],
        qkv_grad,
        out_grad.astype(F32),
        small_two[0],
        small_two[1],
        small_two[8:].T,
        first_out.astype(F32)[None],
        bin_out[None],
        second_out.astype(F32)[None],
        bback_out[None],
    )


def solution(mesh):
    both = ("rep", "ex")
    in_specs = (
        P(both, None),
        P(),
        P(),
        P(),
        P(),
        P(),
        P(),
        P(),
        P("ex", None, None),
        P("ex", None),
        P("ex", None, None),
        P("ex", None),
        P(both, None),
        P(both, None),
        P(both, None),
        P(both),
    )
    out_specs = (
        P(both, None),
        P(both, None),
        P(),
        P(),
        P(),
        P(),
        P(),
        P(),
        P(),
        P("ex", "rep", None),
        P("ex", "rep"),
        P("ex", "rep", None),
        P("ex", "rep"),
    )
    return jax.shard_map(
        functools.partial(local, dict(mesh.shape)),
        mesh=mesh,
        in_specs=in_specs,
        out_specs=out_specs,
        check_vma=False,
    )
```

time: 858 us -> 470 us (0.55)
  matrix products: 263 us -> 72.9 us
  Pallas kernels: 0 us -> 158 us
  local copies, waits for them, and re-layouts: 182 us -> 33.1 us
  waiting for transfers between devices: 180 us -> 34.5 us
  other arithmetic: 147 us -> 21.9 us
  starting transfers between devices: 19.3 us -> 125 us
  blocking collectives: 42.6 us -> 0 us
    dot_general x21 -> x9, matrix products: 263 us -> 72.9 us  [the longest x6 35.1 us: dot_tn(): lax.dot_general(a, b, (((0,), (0,)), ((), ())), preferred_element_type=F32)]
    pallas_call x0 -> x9, Pallas kernels: none -> 158 us  [the longest x1 51.7 us: local(): call(expert_body, (sds((blocks, cap_pad, hidden_units), BF16), sds((block...]
    psum x1 -> x0, waiting for transfers between devices: 121 us -> none  [local(): lax.psum((grad_gain_one, grad_shift_one, jnp.sum(grad_qkv_sets, axis=0),...]
    ppermute x0 -> x92, starting transfers between devices: none -> 101 us  [swap(): return lax.ppermute(values, axis, [(j, j ^ bit) for j in range(size)])]
    gather x13 -> x4, local copies, waits for them, and re-layouts: 91.7 us -> 9.54 us  [local(): gates = jnp.take_along_axis(probs, routes_row, axis=0)]
    reduce_sum x11 -> x0, other arithmetic: 61.4 us -> none  [the longest x1 26.2 us: local(): jnp.sum(jnp.where(kept_mask[:, :, None], grad_pairs, 0.0), axis=1)]
    convert_element_type x10 -> x42, other arithmetic: 51.6 us -> 8.35 us  [the longest x1 3.48 us: local(): qkv_grad = jnp.concatenate([qkv_sums[g][:, p * LANES:(p + 1) * LANES] for...]
    psum x1 -> x0, blocking collectives: 42.6 us -> none  [local(): lax.psum((grad_gain_one, grad_shift_one, jnp.sum(grad_qkv_sets, axis=0),...]
  transfers between devices with their start and end apart: 9 -> 98, of which waited for: 5 -> 12; matrix products, arithmetic and copies ran while one was open for 47% -> 23% of each run, Pallas kernels for 0% -> 21%
where the time goes in v1:
time: 470 us; the launch traced here: 463 us
  Pallas kernels  158 us (34%)
  starting transfers between devices  125 us (27%)
  matrix products  72.9 us (16%)
  waiting for transfers between devices  34.5 us (7%)
  local copies, waits for them, and re-layouts  33.1 us (7%)
  other arithmetic  21.9 us (5%)
  between operations  17.4 us (4%)
    ppermute x92, starting transfers between devices, swap(): return lax.ppermute(values, axis, [(j, j ^ bit) for j in range(size)])  101 us
    pallas_call x1, Pallas kernels, local(): call(expert_body, (sds((blocks, cap_pad, hidden_units), BF16), sds((block...  51.7 us
    dot_general x6, matrix products, dot_tn(): lax.dot_general(a, b, (((0,), (0,)), ((), ())), preferred_element_type=F32)  35.1 us
    pallas_call x1, Pallas kernels, local(): call(functools.partial(forward_body, experts, cap_pad), (sds((groups, tok...  34.9 us
    pallas_call x3, Pallas kernels, local(): call(functools.partial(backward_body, g), sds((toks, 3 * LANES), BF16), i...  30.3 us
    dot_general x2, matrix products, dot_nt(): lax.dot_general(a, b, (((1,), (1,)), ((), ())), preferred_element_type=F32)  24.6 us
    all_to_all x1, waiting for transfers between devices, local(): lax.all_to_all(sent, 'ex', split_axis=0, concat_axis=0, tiled=True)  18.7 us
    ppermute x92, waiting for transfers between devices, swap(): return lax.ppermute(values, axis, [(j, j ^ bit) for j in range(size)])  15.7 us
  transfers between devices with their start and end apart: 98, of which 12 were waited for; matrix products, arithmetic and copies ran while one was open for 23% of the time, Pallas kernels for 21%

profile of v1, /device:TPU:0, one launch (start us, length us, event | category | flops | bytes accessed | tf_op | source)
XLA Modules:
  0.0 462.8 jit_solution(14129950366722349751)
XLA Ops:
  7.2 7.9 %prep.1 = (s32[8,784]{1,0:T(8,128)}, s32[784,128]{1,0:T(8,128)}, bf16[8,208,768]{2,1,0:T(8,128)(2,1)}) custom-call(s32[2,784]{1,0:T(2,128)} %bitcast.365, s32[1,784]{1,0:T(1,128)} %prio_ref.1, bf16[784,768]{1,0:T(8,128)(2,1)} %cot_ref.3), custom_call_target="tpu_custom_call" | custom-call | flops 4000000000 | bytes 6000000 | tf_op jit(solution)/shard_map/prep/pallas_call | solution.py:676
  15.1 5.3 %all-to-all-start.1 = ((bf16[8,208,768]{2,1,0:T(8,128)(2,1)}), bf16[8,208,768]{2,1,0:T(8,128)(2,1)S(1)}, u32[]{:S(2)}, u32[]{:S(2)}) async-start(bf16[8,208,768]{2,1,0:T(8,128)(2,1)} %get-tuple-element.41), calls=%async_computation.1 | async-start | bytes 5111808 | tf_op jit(solution)/shard_map/all_to_all | solution.py:682
  23.4 34.9 %attend.1 = (bf16[3,784,768]{2,1,0:T(8,128)(2,1)}, bf16[784,768]{1,0:T(8,128)(2,1)}, f32[16,784]{1,0:T(8,128)}, bf16[784,768]{1,0:T(8,128)(2,1)}, f32[784,768]{1...) custom-call(s32[1]{0:T(128)S(6)} %copy.167.kind_ref, ...), custom_call_target="tpu_custom_call" | custom-call | flops 10000000000 | bytes 20000000 | tf_op jit(solution)/shard_map/attend/pallas_call | solution.py:688
  58.4 10.6 %all-to-all-start = ((bf16[8,208,768]{2,1,0:T(8,128)(2,1)}), bf16[8,208,768]{2,1,0:T(8,128)(2,1)}, u32[]{:S(2)}, u32[]{:S(2)}) async-start(bf16[8,208,768]{2,1,0:T(8,128)(2,1)} %get-tuple-element.40), calls=%async_computation | async-start | bytes 5111808 | tf_op jit(solution)/shard_map/all_to_all | solution.py:749
  69.3 12.7 %convolution_convert_fusion = bf16[1664,3072]{1,0:T(8,128)(2,1)} fusion(bf16[1664,768]{1,0:T(8,128)(2,1)S(1)} %bitcast.297, bf16[1,3072,768]{2,1,0:T(8,128)(2,1)} %param.26), kind=kOutput, calls=%fused_computation.1 | convolution fusion | flops 7856848896 | bytes 17498112 | tf_op jit(solution)/shard_map/dot_general | solution.py:42
  82.0 18.7 %all-to-all-done.x_ref = bf16[8,208,768]{2,1,0:T(8,128)(2,1)} async-done(((bf16[8,208,768]{2,1,0:T(8,128)(2,1)}), bf16[8,208,768]{2,1,0:T(8,128)(2,1)}, u32[]{:S(2)}, u32[]{:S(2)}) %all-to-all-start) | async-done | bytes 2555936 | tf_op jit(solution)/shard_map/all_to_all | solution.py:749
  100.7 51.7 %expert.1 = (bf16[8,208,3072]{2,1,0:T(8,128)(2,1)}, bf16[8,208,3072]{2,1,0:T(8,128)(2,1)}, bf16[8,208,768]{2,1,0:T(8,128)(2,1)}, f32[8,8,256]{2,1,0:T(8,128)}, f32[8,3072]{1,0:T(8,128)}, /*index=5*/f32[8,768]{1,0:T(8,128)}) custom-call(bf16[8,208,768]{2,1,0:T(8,128)(2,1)} %all-to-all-done.x_ref, bf16[8,208,768]{2,1,0:T(8,128)(2,1)} %copy-done.3, ...), custom_call_target="tpu_custom_call" | custom-call | flops 8000000000 | bytes 40000000 | tf_op jit(solution)/shard_map/expert/pallas_call | solution.py:756
  152.4 13.9 %bitcast_convert_fusion.1 = bf16[768,3072]{1,0:T(8,128)(2,1)} fusion(bf16[8,208,768]{2,1,0:T(8,128)(2,1)} %all-to-all-done.x_ref, bf16[8,208,3072]{2,1,0:T(8,128)(2,1)} %get-tuple-element.45), kind=kOutput, calls=%fused_computation.3 | convolution fusion | flops 7854096384 | bytes 17498112 | tf_op jit(solution)/shard_map/dot_general | solution.py:46
  167.0 9.2 %gather_fusion = f32[1568]{0:T(1024)S(1)} fusion(f32[8,784]{1,0:T(8,128)S(1)} %copy-done, s32[1568]{0:T(1024)S(1)} %reshape.364), kind=kCustom, calls=%fused_computation | custom fusion | bytes 25088 | tf_op jit(solution)/shard_map/jit(take_along_axis)/gather | solution.py:892
  177.1 2.4 fusion.56
  184.0 11.9 %fusion.1 = bf16[8,208,768]{2,1,0:T(8,128)(2,1)} fusion(bf16[8,1,256]{2,1,0:T(2,128)(2,1)S(1)} %get-tuple-element.145, bf16[8,1,256]{2,1,0:T(2,128)(2,1)S(1)} %get-tuple-element.144, bf16[8,208,3072]{2,1,0:T(8,128)(2,1)} %get-tuple-element.45, bf16[1,768,3072]{2,1,0:T(8,128)(2,1)S(1)} %bitcast.371, pred[208]{0:T(512)(128)(4,1)S(1)} %iota_compare_fusion.2), kind=kOutput, calls=%fused_computation.6 | convolution fusion | flops 7867072512 | bytes 17506512 | tf_op jit(solution)/shard_map/dot_general | solution.py:42
  195.9 3.6 all-to-all-start.3
  203.3 13.7 %bitcast_convert_fusion = bf16[3072,768]{1,0:T(8,128)(2,1)} fusion(bf16[8,208,3072]{2,1,0:T(8,128)(2,1)} %get-tuple-element.42, bf16[8,208,768]{2,1,0:T(8,128)(2,1)} %get-tuple-element.58), kind=kOutput, calls=%fused_computation.2 | convolution fusion | flops 7854096384 | bytes 17498112 | tf_op jit(solution)/shard_map/dot_general | solution.py:46
  218.2 13.2 %add_convert_fusion = bf16[1664,768]{1,0:T(8,128)(2,1)} fusion(bf16[1664,3072]{1,0:T(8,128)(2,1)} %bitcast.374, bf16[1,3072,768]{2,1,0:T(8,128)(2,1)} %param.26, f32[768]{0:T(1024)S(1)} %reduce), kind=kOutput, calls=%fused_computation.9 | convolution fusion | flops 7854292992 | bytes 17501184 | tf_op jit(solution)/shard_map/dot_general | solution.py:38
  234.2 4.1 all-to-all-start.2
  238.3 13.4 %row_grad.1 = (f32[784,768]{1,0:T(8,128)}, bf16[784,768]{1,0:T(8,128)(2,1)}, f32[8,768]{1,0:T(8,128)}, f32[8,768]{1,0:T(8,128)}) custom-call(s32[784,128]{1,0:T(8,128)} %get-tuple-element.36.kept_ref.col_ref, s32[8,784]{1,0:T(8,128)} %get-tuple-element.37.slot_ref, s32[2,784]{1,0:T(2,128)} %bitcast.367, f32[8,784]{1,0:T(8,128)} %get-tuple-element.38.probs_ref, ...), custom_call_target="tpu_custom_call" | custom-call | flops 5000000000 | bytes 12000000 | tf_op jit(solution)/shard_map/row_grad/pallas_call | solution.py:823
  251.7 10.1 %attend_back_a.1.refs_0_ = bf16[784,768]{1,0:T(8,128)(2,1)} custom-call(s32[1]{0:T(128)S(6)} %copy.167.kind_ref, bf16[784,768]{1,0:T(8,128)(2,1)} %get-tuple-element.46.up_ref, bf16[768,768]{1,0:T(8,128)(2,1)} %wo_ref.7, bf16[3,784,768]{2,1,0:T(8,128)(2,1)} %get-tuple-element.47.qkv_ref, bf16[784,768]{1,0:T(8,128)(2,1)} %get-tuple-element.48.mix_ref, ...), custom_call_target="tpu_custom_call" | custom-call | flops 8000000000 | bytes 6000000 | tf_op jit(solution)/shard_map/attend_back_a/pallas_call | solution.py:851
  261.8 10.0 %attend_back_b.1.refs_1_ = bf16[784,768]{1,0:T(8,128)(2,1)} custom-call(s32[1]{0:T(128)S(6)} %copy.167.kind_ref, bf16[784,768]{1,0:T(8,128)(2,1)} %get-tuple-element.46.up_ref, bf16[768,768]{1,0:T(8,128)(2,1)} %wo_ref.7, bf16[3,784,768]{2,1,0:T(8,128)(2,1)} %get-tuple-element.47.qkv_ref, bf16[784,768]{1,0:T(8,128)(2,1)} %get-tuple-element.48.mix_ref, ...), custom_call_target="tpu_custom_call" | custom-call | flops 8000000000 | bytes 6000000 | tf_op jit(solution)/shard_map/attend_back_b/pallas_call | solution.py:851
  271.8 10.2 %attend_back_c.1.refs_2_ = bf16[784,768]{1,0:T(8,128)(2,1)} custom-call(s32[1]{0:T(128)S(6)} %copy.167.kind_ref, bf16[784,768]{1,0:T(8,128)(2,1)} %get-tuple-element.46.up_ref, bf16[768,768]{1,0:T(8,128)(2,1)} %wo_ref.7, bf16[3,784,768]{2,1,0:T(8,128)(2,1)} %get-tuple-element.47.qkv_ref, bf16[784,768]{1,0:T(8,128)(2,1)} %get-tuple-element.48.mix_ref, ...), custom_call_target="tpu_custom_call" | custom-call | flops 8000000000 | bytes 6000000 | tf_op jit(solution)/shard_map/attend_back_c/pallas_call | solution.py:851
  282.0 10.6 %final.1 = (bf16[784,768]{1,0:T(8,128)(2,1)}, f32[8,768]{1,0:T(8,128)}) custom-call(bf16[784,768]{1,0:T(8,128)(2,1)} %attend_back_a.1.refs_0_, bf16[784,768]{1,0:T(8,128)(2,1)} %attend_back_b.1.refs_1_, bf16[784,768]{1,0:T(8,128)(2,1)} %attend_back_c.1.refs_2_, bf16[768,768]{1,0:T(8,128)(2,1)} %get-tuple-element.162.refs_3_, ...), custom_call_target="tpu_custom_call" | custom-call | flops 3000000000 | bytes 14000000 | tf_op jit(solution)/shard_map/final/pallas_call | solution.py:884
  292.6 4.8 %collective-permute-start = (f32[8,768]{1,0:T(8,128)}, f32[8,768]{1,0:T(8,128)}, u32[]{:S(2)}, u32[]{:S(2)}) collective-permute-start(f32[8,768]{1,0:T(8,128)} %get-tuple-element.52), channel_id=1, source_target_pairs={{0,1},{1,0},{2,3},{3,2},{4,5},{5,4},{6,7},{7,6},{8,9},{9,8},{10,11... | collective-permute-start | bytes 73736 | tf_op jit(solution)/shard_map/ppermute | solution.py:585
  297.4 3.1 convolution_convert_fusion.4
  313.1 9.0 %combine.1 = bf16[784,768]{1,0:T(8,128)(2,1)} custom-call(s32[784,128]{1,0:T(8,128)} %get-tuple-element.36.kept_ref.col_ref, f32[784,2]{1,0:T(8,128)} %bitcast_select_fusion.gates_ref, f32[784,768]{1,0:T(8,128)} %get-tuple-element.39.residual_ref, bf16[8,208,768]{2,1,0:T(8,128)(2,1)} %copy-done.1), custom_call_target="tpu_custom_call" | custom-call | flops 2000000000 | bytes 8000000 | tf_op jit(solution)/shard_map/combine/pallas_call | solution.py:894
  323.5 1.7 collective-permute-start.1
  327.3 1.7 collective-permute-start.2
  332.8 2.0 collective-permute-start.87
  335.8 1.8 collective-permute-done.3
  337.9 4.6 collective-permute-done.4
  342.5 2.4 collective-permute-start.89
  345.5 2.2 collective-permute-done.89
  352.4 2.0 collective-permute-start.16
  354.6 1.8 collective-permute-start.6
  357.5 1.8 collective-permute-start.56
  359.4 2.0 collective-permute-start.46
  361.5 1.8 collective-permute-done.36
  364.4 1.8 collective-permute-start.66
  371.2 1.7 collective-permute-start.57
  377.0 2.1 collective-permute-start.8
  379.2 2.1 collective-permute-start.28
  381.5 2.1 collective-permute-start.48
  383.8 2.1 collective-permute-start.68
  411.1 2.1 collective-permute-start.11
  413.4 2.1 collective-permute-start.31
  415.6 2.1 collective-permute-start.51
  417.9 2.1 collective-permute-start.71
  444.5 3.5 convert_element_type.651
  449.8 2.9 bitcast_convert_fusion.3
  452.7 2.8 bitcast_convert_fusion.2
  (457 shorter events, 105.2 us)
Async XLA Ops:
  15.1 43.3 %all-to-all-start.1 = ((bf16[8,208,768]{2,1,0:T(8,128)(2,1)}), bf16[8,208,768]{2,1,0:T(8,128)(2,1)S(1)}, u32[]{:S(2)}, u32[]{:S(2)}) async-start(bf16[8,208,768]{2,1,0:T(8,128)(2,1)} %get-tuple-element.41), calls=%async_computation.1 | async-start | bytes 5111808 | tf_op jit(solution)/shard_map/all_to_all | solution.py:682
  58.4 42.3 %all-to-all-start = ((bf16[8,208,768]{2,1,0:T(8,128)(2,1)}), bf16[8,208,768]{2,1,0:T(8,128)(2,1)}, u32[]{:S(2)}, u32[]{:S(2)}) async-start(bf16[8,208,768]{2,1,0:T(8,128)(2,1)} %get-tuple-element.40), calls=%async_computation | async-start | bytes 5111808 | tf_op jit(solution)/shard_map/all_to_all | solution.py:749
  69.0 380.8 %reduce-scatter.3.cloned.1.call-start = ((), (), s32[]{:S(2)}) async-start(), calls=%async_computation.6 | async-start | bytes 5898240 | tf_op jit(solution)/shard_map/reduce_scatter | solution.py:807
  195.9 36.9 %all-to-all-start.3 = ((bf16[8,208,768]{2,1,0:T(8,128)(2,1)}), bf16[8,208,768]{2,1,0:T(8,128)(2,1)S(1)}, u32[]{:S(2)}, u32[]{:S(2)}) async-start(bf16[8,208,768]{2,1,0:T(8,128)(2,1)} %fusion.1), calls=%async_computation.3 | async-start | bytes 5111808 | tf_op jit(solution)/shard_map/all_to_all | solution.py:802
  199.5 253.2 %reduce-scatter.5.cloned.1.call-start = ((), (), s32[]{:S(2)}) async-start(), calls=%async_computation.7 | async-start | bytes 5898240 | tf_op jit(solution)/shard_map/reduce_scatter | solution.py:805
  201.6 15.4 %collective-permute-start.90 = (f32[30,128]{1,0:T(8,128)S(1)}, f32[30,128]{1,0:T(8,128)S(1)}, u32[]{:S(2)}, u32[]{:S(2)}) collective-permute-start(f32[30,128]{1,0:T(8,128)S(1)} %maximum_bitcast_fusion), channel_id=1, source_target_pairs={{0,8},{8,0},{16,24},{24,16},{1,9},{9,1},{17,25},{25,17},{2,10},{10... | collective-permute-start | bytes 46088 | tf_op jit(solution)/shard_map/ppermute | solution.py:585
  217.0 14.4 %collective-permute-start.91 = (f32[30,128]{1,0:T(8,128)S(1)}, f32[30,128]{1,0:T(8,128)S(1)}, u32[]{:S(2)}, u32[]{:S(2)}) collective-permute-start(f32[30,128]{1,0:T(8,128)S(1)} %fusion.55), channel_id=1, source_target_pairs={{0,16},{8,24},{16,0},{24,8},{1,17},{9,25},{17,1},{25,9},{2,18},{10... | collective-permute-start | bytes 46088 | tf_op jit(solution)/shard_map/ppermute | solution.py:585
  234.2 77.4 %all-to-all-start.2 = ((bf16[8,208,768]{2,1,0:T(8,128)(2,1)}), bf16[8,208,768]{2,1,0:T(8,128)(2,1)S(1)}, u32[]{:S(2)}, u32[]{:S(2)}) async-start(bf16[8,208,768]{2,1,0:T(8,128)(2,1)} %bitcast.9), calls=%async_computation.2 | async-start | bytes 5111808 | tf_op jit(solution)/shard_map/all_to_all | solution.py:809
  292.6 30.1 %collective-permute-start = (f32[8,768]{1,0:T(8,128)}, f32[8,768]{1,0:T(8,128)}, u32[]{:S(2)}, u32[]{:S(2)}) collective-permute-start(f32[8,768]{1,0:T(8,128)} %get-tuple-element.52), channel_id=1, source_target_pairs={{0,1},{1,0},{2,3},{3,2},{4,5},{5,4},{6,7},{7,6},{8,9},{9,8},{10,11... | collective-permute-start | bytes 73736 | tf_op jit(solution)/shard_map/ppermute | solution.py:585
  301.5 47.5 %collective-permute-start.15 = (bf16[192,768]{1,0:T(8,128)(2,1)}, bf16[192,768]{1,0:T(8,128)(2,1)}, u32[]{:S(2)}, u32[]{:S(2)}) collective-permute-start(bf16[192,768]{1,0:T(8,128)(2,1)} %dynamic-slice_bitcast_fusion.6), channel_id=1, source_target_pairs={{0,1},{1,0},{2,3},{3,2},{4,5},{5,4},{6,7},{7,6},{8,9},{9,8},{10,11... | collective-permute-start | bytes 884744 | tf_op jit(solution)/shard_map/ppermute | solution.py:585
  302.3 49.5 %collective-permute-start.5 = (bf16[192,768]{1,0:T(8,128)(2,1)}, bf16[192,768]{1,0:T(8,128)(2,1)S(1)}, u32[]{:S(2)}, u32[]{:S(2)}) collective-permute-start(bf16[192,768]{1,0:T(8,128)(2,1)} %dynamic-slice_bitcast_fusion.7), channel_id=1, source_target_pairs={{0,1},{1,0},{2,3},{3,2},{4,5},{5,4},{6,7},{7,6},{8,9},{9,8},{10,11... | collective-permute-start | bytes 884744 | tf_op jit(solution)/shard_map/ppermute | solution.py:585
  306.0 44.6 %collective-permute-start.35 = (bf16[192,768]{1,0:T(8,128)(2,1)}, bf16[192,768]{1,0:T(8,128)(2,1)}, u32[]{:S(2)}, u32[]{:S(2)}) collective-permute-start(bf16[192,768]{1,0:T(8,128)(2,1)} %dynamic-slice_bitcast_fusion.4), channel_id=1, source_target_pairs={{0,1},{1,0},{2,3},{3,2},{4,5},{5,4},{6,7},{7,6},{8,9},{9,8},{10,11... | collective-permute-start | bytes 884744 | tf_op jit(solution)/shard_map/ppermute | solution.py:585
  342.5 10.0 %collective-permute-start.25 = (bf16[192,768]{1,0:T(8,128)(2,1)S(1)}, bf16[192,768]{1,0:T(8,128)(2,1)S(1)}, u32[]{:S(2)}, u32[]{:S(2)}) collective-permute-start(bf16[192,768]{1,0:T(8,128)(2,1)S(1)} %copy-done.15), channel_id=1, source_target_pairs={{0,1},{1,0},{2,3},{3,2},{4,5},{5,4},{6,7},{7,6},{8,9},{9,8},{10,11... | collective-permute-start | bytes 884744 | tf_op jit(solution)/shard_map/ppermute | solution.py:585
  347.7 6.9 %collective-permute-start.55 = (bf16[192,768]{1,0:T(8,128)(2,1)S(1)}, bf16[192,768]{1,0:T(8,128)(2,1)S(1)}, u32[]{:S(2)}, u32[]{:S(2)}) collective-permute-start(bf16[192,768]{1,0:T(8,128)(2,1)S(1)} %dynamic-slice_bitcast_fusion.2), channel_id=1, source_target_pairs={{0,1},{1,0},{2,3},{3,2},{4,5},{5,4},{6,7},{7,6},{8,9},{9,8},{10,11... | collective-permute-start | bytes 884744 | tf_op jit(solution)/shard_map/ppermute | solution.py:585
  349.0 7.6 %collective-permute-start.45 = (bf16[192,768]{1,0:T(8,128)(2,1)S(1)}, bf16[192,768]{1,0:T(8,128)(2,1)S(1)}, u32[]{:S(2)}, u32[]{:S(2)}) collective-permute-start(bf16[192,768]{1,0:T(8,128)(2,1)S(1)} %dynamic-slice_bitcast_fusion.3), channel_id=1, source_target_pairs={{0,1},{1,0},{2,3},{3,2},{4,5},{5,4},{6,7},{7,6},{8,9},{9,8},{10,11... | collective-permute-start | bytes 884744 | tf_op jit(solution)/shard_map/ppermute | solution.py:585
  350.6 6.7 %collective-permute-start.75 = (bf16[192,768]{1,0:T(8,128)(2,1)S(1)}, bf16[192,768]{1,0:T(8,128)(2,1)S(1)}, u32[]{:S(2)}, u32[]{:S(2)}) collective-permute-start(bf16[192,768]{1,0:T(8,128)(2,1)S(1)} %dynamic-slice_bitcast_fusion), channel_id=1, source_target_pairs={{0,1},{1,0},{2,3},{3,2},{4,5},{5,4},{6,7},{7,6},{8,9},{9,8},{10,11... | collective-permute-start | bytes 884744 | tf_op jit(solution)/shard_map/ppermute | solution.py:585
  352.4 7.0 %collective-permute-start.16 = (bf16[96,768]{1,0:T(8,128)(2,1)S(1)}, bf16[96,768]{1,0:T(8,128)(2,1)S(1)}, u32[]{:S(2)}, u32[]{:S(2)}) collective-permute-start(bf16[96,768]{1,0:T(8,128)(2,1)S(1)} %dynamic-slice_bitcast_fusion.14), channel_id=1, source_target_pairs={{0,4},{1,5},{2,6},{3,7},{4,0},{5,1},{6,2},{7,3},{8,12},{9,13},{10,... | collective-permute-start | bytes 442376 | tf_op jit(solution)/shard_map/ppermute | solution.py:585
  354.6 9.8 %collective-permute-start.6 = (bf16[96,768]{1,0:T(8,128)(2,1)S(1)}, bf16[96,768]{1,0:T(8,128)(2,1)S(1)}, u32[]{:S(2)}, u32[]{:S(2)}) collective-permute-start(bf16[96,768]{1,0:T(8,128)(2,1)S(1)} %dynamic-slice_bitcast_fusion.15), channel_id=1, source_target_pairs={{0,2},{1,3},{2,0},{3,1},{4,6},{5,7},{6,4},{7,5},{8,10},{9,11},{10,... | collective-permute-start | bytes 442376 | tf_op jit(solution)/shard_map/ppermute | solution.py:585
  356.5 6.8 %collective-permute-start.36 = (bf16[96,768]{1,0:T(8,128)(2,1)S(1)}, bf16[96,768]{1,0:T(8,128)(2,1)S(1)}, u32[]{:S(2)}, u32[]{:S(2)}) collective-permute-start(bf16[96,768]{1,0:T(8,128)(2,1)S(1)} %dynamic-slice_bitcast_fusion.12), channel_id=1, source_target_pairs={{0,4},{1,5},{2,6},{3,7},{4,0},{5,1},{6,2},{7,3},{8,12},{9,13},{10,... | collective-permute-start | bytes 442376 | tf_op jit(solution)/shard_map/ppermute | solution.py:585
  357.3 9.0 %collective-permute-start.26 = (bf16[96,768]{1,0:T(8,128)(2,1)S(1)}, bf16[96,768]{1,0:T(8,128)(2,1)S(1)}, u32[]{:S(2)}, u32[]{:S(2)}) collective-permute-start(bf16[96,768]{1,0:T(8,128)(2,1)S(1)} %dynamic-slice_bitcast_fusion.13), channel_id=1, source_target_pairs={{0,2},{1,3},{2,0},{3,1},{4,6},{5,7},{6,4},{7,5},{8,10},{9,11},{10,... | collective-permute-start | bytes 442376 | tf_op jit(solution)/shard_map/ppermute | solution.py:585
  357.5 9.2 %collective-permute-start.56 = (bf16[96,768]{1,0:T(8,128)(2,1)S(1)}, bf16[96,768]{1,0:T(8,128)(2,1)S(1)}, u32[]{:S(2)}, u32[]{:S(2)}) collective-permute-start(bf16[96,768]{1,0:T(8,128)(2,1)S(1)} %dynamic-slice_bitcast_fusion.10), channel_id=1, source_target_pairs={{0,4},{1,5},{2,6},{3,7},{4,0},{5,1},{6,2},{7,3},{8,12},{9,13},{10,... | collective-permute-start | bytes 442376 | tf_op jit(solution)/shard_map/ppermute | solution.py:585
  359.4 8.4 %collective-permute-start.46 = (bf16[96,768]{1,0:T(8,128)(2,1)S(1)}, bf16[96,768]{1,0:T(8,128)(2,1)S(1)}, u32[]{:S(2)}, u32[]{:S(2)}) collective-permute-start(bf16[96,768]{1,0:T(8,128)(2,1)S(1)} %dynamic-slice_bitcast_fusion.11), channel_id=1, source_target_pairs={{0,2},{1,3},{2,0},{3,1},{4,6},{5,7},{6,4},{7,5},{8,10},{9,11},{10,... | collective-permute-start | bytes 442376 | tf_op jit(solution)/shard_map/ppermute | solution.py:585
  364.4 6.8 %collective-permute-start.66 = (bf16[96,768]{1,0:T(8,128)(2,1)S(1)}, bf16[96,768]{1,0:T(8,128)(2,1)S(1)}, u32[]{:S(2)}, u32[]{:S(2)}) collective-permute-start(bf16[96,768]{1,0:T(8,128)(2,1)S(1)} %dynamic-slice_bitcast_fusion.9), channel_id=1, source_target_pairs={{0,2},{1,3},{2,0},{3,1},{4,6},{5,7},{6,4},{7,5},{8,10},{9,11},{10,... | collective-permute-start | bytes 442376 | tf_op jit(solution)/shard_map/ppermute | solution.py:585
  366.3 6.7 %collective-permute-start.17 = (bf16[48,768]{1,0:T(8,128)(2,1)S(1)}, bf16[48,768]{1,0:T(8,128)(2,1)S(1)}, u32[]{:S(2)}, u32[]{:S(2)}) collective-permute-start(bf16[48,768]{1,0:T(8,128)(2,1)S(1)} %dynamic-slice_bitcast_fusion.22), channel_id=1, source_target_pairs={{0,2},{1,3},{2,0},{3,1},{4,6},{5,7},{6,4},{7,5},{8,10},{9,11},{10,... | collective-permute-start | bytes 221192 | tf_op jit(solution)/shard_map/ppermute | solution.py:585
  366.7 7.0 %collective-permute-start.7 = (bf16[48,768]{1,0:T(8,128)(2,1)S(1)}, bf16[48,768]{1,0:T(8,128)(2,1)S(1)}, u32[]{:S(2)}, u32[]{:S(2)}) collective-permute-start(bf16[48,768]{1,0:T(8,128)(2,1)S(1)} %dynamic-slice_bitcast_fusion.23), channel_id=1, source_target_pairs={{0,4},{1,5},{2,6},{3,7},{4,0},{5,1},{6,2},{7,3},{8,12},{9,13},{10,... | collective-permute-start | bytes 221192 | tf_op jit(solution)/shard_map/ppermute | solution.py:585
  367.8 7.4 %collective-permute-start.37 = (bf16[48,768]{1,0:T(8,128)(2,1)S(1)}, bf16[48,768]{1,0:T(8,128)(2,1)S(1)}, u32[]{:S(2)}, u32[]{:S(2)}) collective-permute-start(bf16[48,768]{1,0:T(8,128)(2,1)S(1)} %dynamic-slice_bitcast_fusion.20), channel_id=1, source_target_pairs={{0,2},{1,3},{2,0},{3,1},{4,6},{5,7},{6,4},{7,5},{8,10},{9,11},{10,... | collective-permute-start | bytes 221192 | tf_op jit(solution)/shard_map/ppermute | solution.py:585
  369.5 7.3 %collective-permute-start.27 = (bf16[48,768]{1,0:T(8,128)(2,1)S(1)}, bf16[48,768]{1,0:T(8,128)(2,1)S(1)}, u32[]{:S(2)}, u32[]{:S(2)}) collective-permute-start(bf16[48,768]{1,0:T(8,128)(2,1)S(1)} %dynamic-slice_bitcast_fusion.21), channel_id=1, source_target_pairs={{0,4},{1,5},{2,6},{3,7},{4,0},{5,1},{6,2},{7,3},{8,12},{9,13},{10,... | collective-permute-start | bytes 221192 | tf_op jit(solution)/shard_map/ppermute | solution.py:585
  377.0 6.6 %collective-permute-start.8 = (bf16[24,768]{1,0:T(8,128)(2,1)S(1)}, bf16[24,768]{1,0:T(8,128)(2,1)S(1)}, u32[]{:S(2)}, u32[]{:S(2)}) collective-permute-start(bf16[24,768]{1,0:T(8,128)(2,1)S(1)} %dynamic-slice_bitcast_fusion.31), channel_id=1, source_target_pairs={{0,8},{8,0},{16,24},{24,16},{1,9},{9,1},{17,25},{25,17},{2,10},{10... | collective-permute-start | bytes 110600 | tf_op jit(solution)/shard_map/ppermute | solution.py:585
  379.2 6.7 %collective-permute-start.28 = (bf16[24,768]{1,0:T(8,128)(2,1)S(1)}, bf16[24,768]{1,0:T(8,128)(2,1)S(1)}, u32[]{:S(2)}, u32[]{:S(2)}) collective-permute-start(bf16[24,768]{1,0:T(8,128)(2,1)S(1)} %dynamic-slice_bitcast_fusion.29), channel_id=1, source_target_pairs={{0,8},{8,0},{16,24},{24,16},{1,9},{9,1},{17,25},{25,17},{2,10},{10... | collective-permute-start | bytes 110600 | tf_op jit(solution)/shard_map/ppermute | solution.py:585
  381.5 7.6 %collective-permute-start.48 = (bf16[24,768]{1,0:T(8,128)(2,1)S(1)}, bf16[24,768]{1,0:T(8,128)(2,1)S(1)}, u32[]{:S(2)}, u32[]{:S(2)}) collective-permute-start(bf16[24,768]{1,0:T(8,128)(2,1)S(1)} %dynamic-slice_bitcast_fusion.27), channel_id=1, source_target_pairs={{0,8},{8,0},{16,24},{24,16},{1,9},{9,1},{17,25},{25,17},{2,10},{10... | collective-permute-start | bytes 110600 | tf_op jit(solution)/shard_map/ppermute | solution.py:585
  383.6 7.0 %collective-permute-start.78 = (bf16[24,768]{1,0:T(8,128)(2,1)S(1)}, bf16[24,768]{1,0:T(8,128)(2,1)S(1)}, u32[]{:S(2)}, u32[]{:S(2)}) collective-permute-start(bf16[24,768]{1,0:T(8,128)(2,1)S(1)} %dynamic-slice_bitcast_fusion.24), channel_id=1, source_target_pairs={{0,8},{8,0},{16,24},{24,16},{1,9},{9,1},{17,25},{25,17},{2,10},{10... | collective-permute-start | bytes 110600 | tf_op jit(solution)/shard_map/ppermute | solution.py:585
  383.8 8.5 %collective-permute-start.68 = (bf16[24,768]{1,0:T(8,128)(2,1)S(1)}, bf16[24,768]{1,0:T(8,128)(2,1)S(1)}, u32[]{:S(2)}, u32[]{:S(2)}) collective-permute-start(bf16[24,768]{1,0:T(8,128)(2,1)S(1)} %dynamic-slice_bitcast_fusion.25), channel_id=1, source_target_pairs={{0,8},{8,0},{16,24},{24,16},{1,9},{9,1},{17,25},{25,17},{2,10},{10... | collective-permute-start | bytes 110600 | tf_op jit(solution)/shard_map/ppermute | solution.py:585
  385.9 7.9 %collective-permute-start.19 = (bf16[12,768]{1,0:T(8,128)(2,1)S(1)}, bf16[12,768]{1,0:T(8,128)(2,1)S(1)}, u32[]{:S(2)}, u32[]{:S(2)}) collective-permute-start(bf16[12,768]{1,0:T(8,128)(2,1)S(1)} %dynamic-slice_bitcast_fusion.38), channel_id=1, source_target_pairs={{0,16},{8,24},{16,0},{24,8},{1,17},{9,25},{17,1},{25,9},{2,18},{10... | collective-permute-start | bytes 55304 | tf_op jit(solution)/shard_map/ppermute | solution.py:585
  387.4 8.0 %collective-permute-start.9 = (bf16[12,768]{1,0:T(8,128)(2,1)S(1)}, bf16[12,768]{1,0:T(8,128)(2,1)S(1)}, u32[]{:S(2)}, u32[]{:S(2)}) collective-permute-start(bf16[12,768]{1,0:T(8,128)(2,1)S(1)} %dynamic-slice_bitcast_fusion.39), channel_id=1, source_target_pairs={{0,16},{8,24},{16,0},{24,8},{1,17},{9,25},{17,1},{25,9},{2,18},{10... | collective-permute-start | bytes 55304 | tf_op jit(solution)/shard_map/ppermute | solution.py:585
  389.1 7.8 %collective-permute-start.39 = (bf16[12,768]{1,0:T(8,128)(2,1)S(1)}, bf16[12,768]{1,0:T(8,128)(2,1)S(1)}, u32[]{:S(2)}, u32[]{:S(2)}) collective-permute-start(bf16[12,768]{1,0:T(8,128)(2,1)S(1)} %dynamic-slice_bitcast_fusion.36), channel_id=1, source_target_pairs={{0,16},{8,24},{16,0},{24,8},{1,17},{9,25},{17,1},{25,9},{2,18},{10... | collective-permute-start | bytes 55304 | tf_op jit(solution)/shard_map/ppermute | solution.py:585
  390.6 7.9 %collective-permute-start.29 = (bf16[12,768]{1,0:T(8,128)(2,1)S(1)}, bf16[12,768]{1,0:T(8,128)(2,1)S(1)}, u32[]{:S(2)}, u32[]{:S(2)}) collective-permute-start(bf16[12,768]{1,0:T(8,128)(2,1)S(1)} %dynamic-slice_bitcast_fusion.37), channel_id=1, source_target_pairs={{0,16},{8,24},{16,0},{24,8},{1,17},{9,25},{17,1},{25,9},{2,18},{10... | collective-permute-start | bytes 55304 | tf_op jit(solution)/shard_map/ppermute | solution.py:585
  392.3 7.7 %collective-permute-start.59 = (bf16[12,768]{1,0:T(8,128)(2,1)S(1)}, bf16[12,768]{1,0:T(8,128)(2,1)S(1)}, u32[]{:S(2)}, u32[]{:S(2)}) collective-permute-start(bf16[12,768]{1,0:T(8,128)(2,1)S(1)} %dynamic-slice_bitcast_fusion.34), channel_id=1, source_target_pairs={{0,16},{8,24},{16,0},{24,8},{1,17},{9,25},{17,1},{25,9},{2,18},{10... | collective-permute-start | bytes 55304 | tf_op jit(solution)/shard_map/ppermute | solution.py:585
  393.8 7.8 %collective-permute-start.49 = (bf16[12,768]{1,0:T(8,128)(2,1)S(1)}, bf16[12,768]{1,0:T(8,128)(2,1)S(1)}, u32[]{:S(2)}, u32[]{:S(2)}) collective-permute-start(bf16[12,768]{1,0:T(8,128)(2,1)S(1)} %dynamic-slice_bitcast_fusion.35), channel_id=1, source_target_pairs={{0,16},{8,24},{16,0},{24,8},{1,17},{9,25},{17,1},{25,9},{2,18},{10... | collective-permute-start | bytes 55304 | tf_op jit(solution)/shard_map/ppermute | solution.py:585
  395.5 7.7 %collective-permute-start.79 = (bf16[12,768]{1,0:T(8,128)(2,1)S(1)}, bf16[12,768]{1,0:T(8,128)(2,1)S(1)}, u32[]{:S(2)}, u32[]{:S(2)}) collective-permute-start(bf16[12,768]{1,0:T(8,128)(2,1)S(1)} %dynamic-slice_bitcast_fusion.32), channel_id=1, source_target_pairs={{0,16},{8,24},{16,0},{24,8},{1,17},{9,25},{17,1},{25,9},{2,18},{10... | collective-permute-start | bytes 55304 | tf_op jit(solution)/shard_map/ppermute | solution.py:585
  396.9 7.8 %collective-permute-start.69 = (bf16[12,768]{1,0:T(8,128)(2,1)S(1)}, bf16[12,768]{1,0:T(8,128)(2,1)S(1)}, u32[]{:S(2)}, u32[]{:S(2)}) collective-permute-start(bf16[12,768]{1,0:T(8,128)(2,1)S(1)} %dynamic-slice_bitcast_fusion.33), channel_id=1, source_target_pairs={{0,16},{8,24},{16,0},{24,8},{1,17},{9,25},{17,1},{25,9},{2,18},{10... | collective-permute-start | bytes 55304 | tf_op jit(solution)/shard_map/ppermute | solution.py:585
  398.6 7.7 %collective-permute-start.20 = (bf16[12,768]{1,0:T(8,128)(2,1)S(1)}, bf16[12,768]{1,0:T(8,128)(2,1)S(1)}, u32[]{:S(2)}, u32[]{:S(2)}) collective-permute-start(bf16[12,768]{1,0:T(8,128)(2,1)S(1)} %fusion.49), channel_id=1, source_target_pairs={{0,16},{8,24},{16,0},{24,8},{1,17},{9,25},{17,1},{25,9},{2,18},{10... | collective-permute-start | bytes 55304 | tf_op jit(solution)/shard_map/ppermute | solution.py:585
  400.0 7.8 %collective-permute-start.10 = (bf16[12,768]{1,0:T(8,128)(2,1)S(1)}, bf16[12,768]{1,0:T(8,128)(2,1)S(1)}, u32[]{:S(2)}, u32[]{:S(2)}) collective-permute-start(bf16[12,768]{1,0:T(8,128)(2,1)S(1)} %fusion.50), channel_id=1, source_target_pairs={{0,16},{8,24},{16,0},{24,8},{1,17},{9,25},{17,1},{25,9},{2,18},{10... | collective-permute-start | bytes 55304 | tf_op jit(solution)/shard_map/ppermute | solution.py:585
  401.7 7.7 %collective-permute-start.40 = (bf16[12,768]{1,0:T(8,128)(2,1)S(1)}, bf16[12,768]{1,0:T(8,128)(2,1)S(1)}, u32[]{:S(2)}, u32[]{:S(2)}) collective-permute-start(bf16[12,768]{1,0:T(8,128)(2,1)S(1)} %fusion.47), channel_id=1, source_target_pairs={{0,16},{8,24},{16,0},{24,8},{1,17},{9,25},{17,1},{25,9},{2,18},{10... | collective-permute-start | bytes 55304 | tf_op jit(solution)/shard_map/ppermute | solution.py:585
  403.1 7.9 %collective-permute-start.30 = (bf16[12,768]{1,0:T(8,128)(2,1)S(1)}, bf16[12,768]{1,0:T(8,128)(2,1)S(1)}, u32[]{:S(2)}, u32[]{:S(2)}) collective-permute-start(bf16[12,768]{1,0:T(8,128)(2,1)S(1)} %fusion.48), channel_id=1, source_target_pairs={{0,16},{8,24},{16,0},{24,8},{1,17},{9,25},{17,1},{25,9},{2,18},{10... | collective-permute-start | bytes 55304 | tf_op jit(solution)/shard_map/ppermute | solution.py:585
  406.2 7.0 %collective-permute-start.50 = (bf16[12,768]{1,0:T(8,128)(2,1)S(1)}, bf16[12,768]{1,0:T(8,128)(2,1)S(1)}, u32[]{:S(2)}, u32[]{:S(2)}) collective-permute-start(bf16[12,768]{1,0:T(8,128)(2,1)S(1)} %fusion.46), channel_id=1, source_target_pairs={{0,16},{8,24},{16,0},{24,8},{1,17},{9,25},{17,1},{25,9},{2,18},{10... | collective-permute-start | bytes 55304 | tf_op jit(solution)/shard_map/ppermute | solution.py:585
  413.4 6.6 %collective-permute-start.31 = (bf16[24,768]{1,0:T(8,128)(2,1)S(1)}, bf16[24,768]{1,0:T(8,128)(2,1)S(1)}, u32[]{:S(2)}, u32[]{:S(2)}) collective-permute-start(bf16[24,768]{1,0:T(8,128)(2,1)S(1)} %pad_maximum_fusion.32), channel_id=1, source_target_pairs={{0,8},{8,0},{16,24},{24,16},{1,9},{9,1},{17,25},{25,17},{2,10},{10... | collective-permute-start | bytes 110600 | tf_op jit(solution)/shard_map/ppermute | solution.py:585
  417.9 6.6 %collective-permute-start.71 = (bf16[24,768]{1,0:T(8,128)(2,1)S(1)}, bf16[24,768]{1,0:T(8,128)(2,1)S(1)}, u32[]{:S(2)}, u32[]{:S(2)}) collective-permute-start(bf16[24,768]{1,0:T(8,128)(2,1)S(1)} %pad_maximum_fusion.36), channel_id=1, source_target_pairs={{0,8},{8,0},{16,24},{24,16},{1,9},{9,1},{17,25},{25,17},{2,10},{10... | collective-permute-start | bytes 110600 | tf_op jit(solution)/shard_map/ppermute | solution.py:585
  420.7 6.7 %collective-permute-start.12 = (bf16[48,768]{1,0:T(8,128)(2,1)S(1)}, bf16[48,768]{1,0:T(8,128)(2,1)S(1)}, u32[]{:S(2)}, u32[]{:S(2)}) collective-permute-start(bf16[48,768]{1,0:T(8,128)(2,1)S(1)} %pad_maximum_fusion.22), channel_id=1, source_target_pairs={{0,4},{1,5},{2,6},{3,7},{4,0},{5,1},{6,2},{7,3},{8,12},{9,13},{10,... | collective-permute-start | bytes 221192 | tf_op jit(solution)/shard_map/ppermute | solution.py:585
  (82 other events, 505.6 us)
Sparse Core Ops, SparseCore 0:
  166.4 84.3 reduce-scatter.2
  253.1 86.3 reduce-scatter.4

commit v2 on v1

--- a/solution.py
+++ b/solution.py
@@ -50,23 +50,50 @@
     return lax.broadcasted_iota(jnp.int32, shape, dim)
 
 
-def call(body, out_shape, in_specs=None, out_specs=None, grid=None, scratch=(), cost=None, name=None):
+def call(
+    body, out_shape, in_specs=None, out_specs=None, grid=None, scratch=(), cost=None, name=None, after=()
+):
     args = dict(out_shape=out_shape, scratch_shapes=list(scratch), name=name)
     if grid is not None:
         args["grid"] = grid
-    if in_specs is not None:
-        args["in_specs"] = in_specs
     if out_specs is not None:
         args["out_specs"] = out_specs
     if cost is not None:
         args["cost_estimate"] = pl.CostEstimate(
             flops=int(cost[0]), bytes_accessed=int(cost[1]), transcendentals=int(cost[2])
         )
+
+    def run(*operands):
+        count = len(operands)
+        specs = in_specs or [pl.BlockSpec(memory_space=pltpu.VMEM)] * count
+        specs = list(specs) + [pl.BlockSpec(memory_space=pl.ANY)] * len(after)
+
+        def inner(*refs):
+            body(*refs[:count], *refs[count + len(after) :])
+
+        return pl.pallas_call(
+            inner,
+            in_specs=specs,
+            compiler_params=pltpu.CompilerParams(vmem_limit_bytes=60 * 1024 * 1024),
+            **args,
+        )(*operands, *after)
+
+    return run
+
+
+def hold(values, after):
+    def nothing(*refs):
+        pass
+
+    any_spec = pl.BlockSpec(memory_space=pl.ANY)
     return pl.pallas_call(
-        body,
-        compiler_params=pltpu.CompilerParams(vmem_limit_bytes=60 * 1024 * 1024),
-        **args,
-    )
+        nothing,
+        out_shape=jax.ShapeDtypeStruct(values.shape, values.dtype),
+        in_specs=[any_spec] * (1 + len(after)),
+        out_specs=any_spec,
+        input_output_aliases={0: 0},
+        name="hold",
+    )(values, *after)
 
 
 def whole(shape, memory_space=None):
@@ -403,22 +430,38 @@
         lax.fori_loop(0, blocks, last, 0)
 
 
-def combine_body(experts, kept_ref, gates_ref, residual_ref, back_ref, result_ref):
+def produce_body(hidden_ref, w_ref, bias_ref, out_ref):
+    out_ref[...] = (dot_nn(hidden_ref[...], w_ref[...]) + bias_ref[...]).astype(BF16)
+
+
+def combine_body(
+    experts, kept_ref, slot_ref, routes_ref, probs_ref, residual_ref, back_ref, result_ref
+):
     blocks, cap_pad, width = back_ref.shape
     toks = residual_ref.shape[0]
     chunk = row_chunk(toks)
     flat = back_ref[...].reshape(blocks * cap_pad, width)
-
-    def rows(i, carry):
+    labels = iota((experts, toks), 0)
+    probs = probs_ref[...]
+
+    def gate(k):
+        return jnp.sum(jnp.where(labels == routes_ref[k : k + 1, :], probs, 0.0), axis=0, keepdims=True)
+
+    gate_one, gate_two = gate(0), gate(1)
+
+    def columns(i, carry):
         spot = pl.ds(pl.multiple_of(i * chunk, 16), chunk)
+        eye = iota((chunk, toks), 0) + i * chunk == iota((chunk, toks), 1)
+        col_one = jnp.sum(jnp.where(eye, gate_one, 0.0), axis=1, keepdims=True)
+        col_two = jnp.sum(jnp.where(eye, gate_two, 0.0), axis=1, keepdims=True)
         spots = iota((chunk, blocks * cap_pad), 1)
-        hot = jnp.where(spots == kept_ref[spot, 0:1], gates_ref[spot, 0:1], 0.0) + jnp.where(
-            spots == kept_ref[spot, 1:2], gates_ref[spot, 1:2], 0.0
+        hot = jnp.where(spots == kept_ref[spot, 0:1], col_one, 0.0) + jnp.where(
+            spots == kept_ref[spot, 1:2], col_two, 0.0
         )
         result_ref[spot, :] = (residual_ref[spot, :] + dot_nn(hot.astype(BF16), flat)).astype(BF16)
         return carry
 
-    lax.fori_loop(0, toks // chunk, rows, 0)
+    lax.fori_loop(0, toks // chunk, columns, 0)
 
 
 def row_grad_body(
@@ -581,63 +624,104 @@
     lax.fori_loop(0, toks // chunk, rows, 0)
 
 
-def swap(values, axis, bit, size):
-    return lax.ppermute(values, axis, [(j, j ^ bit) for j in range(size)])
-
-
-def add_pair(a, b):
-    return (a.astype(F32) + b.astype(F32)).astype(a.dtype)
-
-
-def halve(values, axis, bit, size):
-    mine = (lax.axis_index(axis) // bit) % 2
-    halves = values.reshape((2, values.shape[0] // 2) + values.shape[1:])
-    keep = lax.dynamic_index_in_dim(halves, mine, 0, keepdims=False)
-    send = lax.dynamic_index_in_dim(halves, 1 - mine, 0, keepdims=False)
-    return add_pair(keep, swap(send, axis, bit, size))
-
-
-def unhalve(values, axis, bit, size):
-    mine = (lax.axis_index(axis) // bit) % 2
-    other = swap(values, axis, bit, size)
-    return jnp.concatenate(
-        [jnp.where(mine == 0, values, other), jnp.where(mine == 0, other, values)], axis=0
-    )
-
-
-def axis_bits(axis, size):
-    bits = []
-    bit = 1
-    while bit < size:
-        bits.append((axis, bit, size))
+def place_body(core_ref, own_one, other_one, own_two, other_two, out_ref):
+    zero = core_ref[0] == 0
+    parts = (
+        jnp.where(zero, other_one[...], own_one[...]),
+        jnp.where(zero, own_two[...], other_two[...]),
+        jnp.where(zero, other_two[...], own_two[...]),
+    )
+    for k, part in enumerate(parts):
+        for p in range(3):
+            at = (p * 3 + k) * LANES
+            out_ref[:, at : at + LANES] = part[:, p * LANES : (p + 1) * LANES].astype(F32)
+
+
+def place_qkv(pairs, core):
+    rows, cols = pairs[0][0].shape
+    tile = rows // 3
+    return call(
+        place_body,
+        jax.ShapeDtypeStruct((rows, 3 * cols), F32),
+        in_specs=[pl.BlockSpec(memory_space=pltpu.SMEM)]
+        + [pl.BlockSpec((tile, cols), lambda i: (i, 0)) for _ in range(4)],
+        out_specs=pl.BlockSpec((tile, 3 * cols), lambda i: (i, 0)),
+        grid=(3,),
+        name="place_qkv",
+        cost=(1e6, 20 * rows * cols, 0),
+    )(core.astype(jnp.int32).reshape(1), *[part for pair in pairs for part in pair])
+
+
+def bits_below(count):
+    bits, bit = [], 1
+    while bit < count:
+        bits.append(bit)
         bit *= 2
     return bits
 
 
-def sum_all(values, sizes):
-    inner = axis_bits("ex", sizes["ex"])
-    outer = axis_bits("rep", sizes["rep"])
-    core, plane = inner[:1], inner[1:]
-    shape = values.shape
-    if shape[0] % (2 * sizes["ex"] * sizes["rep"]):
-        values = values.reshape(-1, 128)
-    half = values.shape[0] // 2
-    done = []
-    for part, order in (
-        (values[:half], core + plane + outer),
-        (values[half:], core + plane[::-1] + outer),
-    ):
-        for hop in order:
-            part = halve(part, *hop)
-        for hop in order[::-1]:
-            part = unhalve(part, *hop)
-        done.append(part)
-    return jnp.concatenate(done, axis=0).reshape(shape)
-
-
-def sum_small(values, bits):
-    for hop in bits:
-        values = values + swap(values, *hop)
+def send_xor(values, axis, size, distance):
+    return lax.ppermute(values, axis, [(j, j ^ distance) for j in range(size)])
+
+
+def trade_sum(parts, axis, size, stride, mine):
+    total = lax.dynamic_index_in_dim(parts, mine, 0, keepdims=False).astype(F32)
+    for d in range(1, parts.shape[0]):
+        sent = lax.dynamic_index_in_dim(parts, mine ^ d, 0, keepdims=False)
+        total = total + send_xor(sent, axis, size, d * stride).astype(F32)
+    return total.astype(parts.dtype)
+
+
+def gather_group(values, axis, size, stride, count, mine):
+    got = [values] + [send_xor(values, axis, size, d * stride) for d in range(1, count)]
+    for bit in bits_below(count):
+        flip = (mine & bit) != 0
+        got = [jnp.where(flip, got[k ^ bit], got[k]) for k in range(count)]
+    return jnp.concatenate(got, axis=0)
+
+
+class PairSum:
+    def __init__(self, first, second, sizes):
+        self.width = first.shape[1]
+        self.wide, self.reps = sizes["ex"], sizes["rep"]
+        place = lax.axis_index("ex")
+        self.core, self.chip = place % 2, place // 2
+        self.rep = lax.axis_index("rep")
+        self.keep = jnp.where(self.core == 0, first, second)
+        self.value = jnp.where(self.core == 0, second, first)
+        self.stage = 0
+
+    def split(self, values, count):
+        return values.reshape(count, -1, self.width)
+
+    def step(self):
+        v = self.value
+        chips = self.wide // 2
+        if self.stage == 0:
+            other = send_xor(v, "ex", self.wide, 1)
+            v = (self.keep.astype(F32) + other.astype(F32)).astype(v.dtype)
+        elif self.stage == 1:
+            v = trade_sum(self.split(v, chips), "ex", self.wide, 2, self.chip)
+        elif self.stage == 2:
+            v = trade_sum(self.split(v, self.reps), "rep", self.reps, 1, self.rep)
+        elif self.stage == 3:
+            v = gather_group(v, "rep", self.reps, 1, self.reps, self.rep)
+        elif self.stage == 4:
+            v = gather_group(v, "ex", self.wide, 2, chips, self.chip)
+        self.stage += 1
+        self.value = v
+        return v
+
+    def finish(self):
+        while self.stage < 5:
+            self.step()
+        return self.value, send_xor(self.value, "ex", self.wide, 1)
+
+
+def sum_small(values, axes):
+    for axis, size in axes:
+        for bit in bits_below(size):
+            values = values + send_xor(values, axis, size, bit)
     return values
 
 
@@ -796,23 +880,39 @@
     gate_high = gate_row.astype(BF16).astype(F32)
     gate_rows = jnp.concatenate([gate_high, gate_row - gate_high], axis=1)
     gate_rows = jnp.pad(gate_rows, ((0, 0), (cap_pad - 2, 0), (0, width - wide)))
+    first_grad = dot_tn(flat_rows, flat_pre).astype(BF16)
+    first_out = lax.psum_scatter(first_grad, "rep", scatter_dimension=0, tiled=True).astype(F32)
+    flat_pre = hold(flat_pre, [first_grad])
     grad_rows = dot_nt(flat_pre, first_w).reshape(blocks, cap_pad, width)
     tail = lax.broadcasted_iota(jnp.int32, (blocks, cap_pad, width), 1) >= cap_pad - 2
     grad_rows = jnp.where(tail, gate_rows, grad_rows).astype(BF16)
     grad_back = lax.all_to_all(grad_rows, "ex", split_axis=0, concat_axis=0, tiled=True)
 
+    flat_slots = hold(flat_slots, [first_grad, grad_rows])
     second_grad = dot_tn(flat_hidden, flat_slots).astype(BF16)
-    second_out = lax.psum_scatter(second_grad, "rep", scatter_dimension=0, tiled=True)
-    first_grad = dot_tn(flat_rows, flat_pre).astype(BF16)
-    first_out = lax.psum_scatter(first_grad, "rep", scatter_dimension=0, tiled=True)
-    produced = (dot_nn(flat_hidden, second_w) + bias_back).astype(BF16)
+    second_out = lax.psum_scatter(second_grad, "rep", scatter_dimension=0, tiled=True).astype(F32)
+    flat_hidden = hold(flat_hidden, [second_grad])
+    tall = blocks * cap_pad // 4
+    produced = call(
+        produce_body,
+        sds((blocks * cap_pad, width), BF16),
+        in_specs=[
+            pl.BlockSpec((tall, hidden_units), lambda i: (i, 0)),
+            whole((hidden_units, width)),
+            whole((1, width)),
+        ],
+        out_specs=pl.BlockSpec((tall, width), lambda i: (i, 0)),
+        grid=(4,),
+        cost=(1, 1, 0),
+        name="produce",
+    )(flat_hidden, second_w, bias_back)
     returned = lax.all_to_all(
         produced.reshape(blocks, cap_pad, width), "ex", split_axis=0, concat_axis=0, tiled=True
     )
 
     reps = sizes["rep"]
     bias_sum = sum_small(
-        jnp.concatenate([bin_sum[0], bback_sum[0]]).reshape(-1, 128), axis_bits("rep", reps)
+        jnp.concatenate([bin_sum[0], bback_sum[0]]).reshape(-1, 128), [("rep", reps)]
     ).reshape(-1)
     rank = lax.axis_index("rep")
     bin_out = lax.dynamic_slice_in_dim(bias_sum, rank * (hidden_units // reps), hidden_units // reps)
@@ -829,8 +929,9 @@
             sds((experts, width), F32),
         ),
         scratch=[pltpu.VMEM((toks, width), F32)],
-        cost=(5e9, 12e6, 0),
+        cost=(1, 1, 0),
         name="row_grad",
+        after=[first_grad, second_grad, produced],
     )(
         slot_col,
         slots,
@@ -843,11 +944,18 @@
         router_row,
         grad_back,
     )
-    out_grad = sum_all(dot_tn(mix, grad_branch).astype(BF16), sizes)
+    out_part = dot_tn(mix, grad_branch).astype(BF16)
+    sums = []
+
+    def advance():
+        return [s.step() for s in sums]
 
     packed_grads = []
-    qkv_sums = []
+    parts = [out_part]
+    waiting = [out_part]
     for g in range(groups):
+        if g == 1:
+            waiting.append(returned)
         packed = call(
             functools.partial(backward_body, g),
             sds((toks, 3 * LANES), BF16),
@@ -868,11 +976,19 @@
                 pltpu.VMEM((toks, LANES), F32),
                 pltpu.VMEM((toks, LANES), F32),
             ],
-            cost=(8e9, 6e6, 2e6),
+            cost=(1, 1, 0),
             name="attend_back_" + "abcdef"[g],
+            after=waiting,
         )(image_kind, grad_branch, w_out, qkv, mix, logsum)
         packed_grads.append(packed)
-        qkv_sums.append(sum_all(dot_tn(low_one, packed).astype(BF16), sizes))
+        waiting = advance()
+        parts.append(dot_tn(low_one, packed).astype(BF16))
+        if len(parts) == 2:
+            sums.append(PairSum(*parts, sizes))
+            parts = []
+            waiting.append(sums[-1].value)
+        else:
+            waiting.append(parts[-1])
 
     w_groups = [
         jnp.concatenate(
@@ -885,43 +1001,45 @@
         functools.partial(final_body, groups),
         (sds((toks, width), BF16), sds((8, width), F32)),
         scratch=[pltpu.VMEM((toks, width), F32)],
-        cost=(3e9, 14e6, 0),
+        cost=(1, 1, 0),
         name="final",
+        after=waiting,
     )(*packed_grads, *w_groups, tokens, gains[0], grad_residual)
-
-    gates = jnp.take_along_axis(probs, routes_row, axis=0)
-    gates = gates.T
+    last = sums[1]
+
     result = call(
         functools.partial(combine_body, experts),
         sds((toks, width), BF16),
-        cost=(2e9, 8e6, 0),
+        cost=(1, 1, 0),
         name="combine",
-    )(slot_col, gates, residual, returned)
-
-    everyone = axis_bits("ex", sizes["ex"]) + axis_bits("rep", reps)
-    small_two = sum_small(jnp.concatenate([small_two, route_grad], axis=0), everyone)
-    small_one = sum_small(small_one, everyone)
-    qkv_grad = jnp.concatenate(
-        [
-            qkv_sums[g][:, p * LANES : (p + 1) * LANES]
-            for p in range(3)
-            for g in range(groups)
-        ],
-        axis=1,
-    ).astype(F32)
+        after=[last.step()],
+    )(slot_col, slots, routes_row, probs, residual, returned)
+    last.step()
+    last.value = hold(last.value, [result])
+    last.step()
+    last.step()
+
+    small = sum_small(
+        jnp.concatenate([small_one[0:2], small_two[0:2], route_grad], axis=0),
+        [("ex", sizes["ex"]), ("rep", reps)],
+    )
+    pairs = [s.finish() for s in sums]
+    core = lax.axis_index("ex") % 2
+    out_grad = jnp.where(core == 0, *pairs[0]).astype(F32)
+    qkv_grad = place_qkv(pairs, core)
     return (
         result,
         grad_tokens,
-        small_one[0],
-        small_one[1],
+        small[0],
+        small[1],
         qkv_grad,
-        out_grad.astype(F32),
-        small_two[0],
-        small_two[1],
-        small_two[8:].T,
-        first_out.astype(F32)[None],
+        out_grad,
+        small[2],
+        small[3],
+        small[4:].T,
+        first_out[None],
         bin_out[None],
-        second_out.astype(F32)[None],
+        second_out[None],
         bback_out[None],
     )
 

time: 470 us -> 447 us (0.951)
  starting transfers between devices: 125 us -> 69 us
  waiting for transfers between devices: 34.5 us -> 68.6 us
  Pallas kernels: 158 us -> 177 us
  local copies, waits for them, and re-layouts: 33.1 us -> 14.2 us
    ppermute x92 -> x35, starting transfers between devices: 101 us -> 45.3 us  [send_xor(): return lax.ppermute(values, axis, [(j, j ^ distance) for j in range(size)])]
    ppermute x92 -> x35, waiting for transfers between devices: 15.7 us -> 44.5 us  [send_xor(): return lax.ppermute(values, axis, [(j, j ^ distance) for j in range(size)])]
    pallas_call x9 -> x15, Pallas kernels: 158 us -> 177 us  [the longest x11 177 us: run(): pl.pallas_call(inner, in_specs=specs, compiler_params=pltpu.CompilerParam...]
    dot_general x1 -> x0, matrix products: 13.2 us -> none  [dot_nn(): lax.dot_general(a, b, (((1,), (0,)), ((), ())), preferred_element_type=F32)]
    dot_general x6, matrix products: 35.1 us -> 44.7 us  [dot_tn(): lax.dot_general(a, b, (((0,), (0,)), ((), ())), preferred_element_type=F32)]
    gather x4 -> x0, local copies, waits for them, and re-layouts: 9.54 us -> none  [local(): gates = jnp.take_along_axis(probs, routes_row, axis=0)]
    squeeze x40 -> x4, local copies, waits for them, and re-layouts: 6.42 us -> 1.12 us  [trade_sum(): sent = lax.dynamic_index_in_dim(parts, mine ^ d, 0, keepdims=False)]
    all_to_all x1, waiting for transfers between devices: 0.01 us -> 5.06 us  [local(): lax.all_to_all(grad_rows, 'ex', split_axis=0, concat_axis=0, tiled=True)]
  transfers between devices with their start and end apart: 98 -> 41, of which waited for: 12 -> 19; matrix products, arithmetic and copies ran while one was open for 23% -> 21% of each run, Pallas kernels for 21% -> 27%
where the time goes in v2:
time: 447 us; the launch traced here: 441 us
  Pallas kernels  177 us (40%)
  matrix products  70.7 us (16%)
  starting transfers between devices  69 us (15%)
  waiting for transfers between devices  68.6 us (15%)
  other arithmetic  26.1 us (6%)
  between operations  15.6 us (3%)
  local copies, waits for them, and re-layouts  14.2 us (3%)
    pallas_call x11, Pallas kernels, run(): pl.pallas_call(inner, in_specs=specs, compiler_params=pltpu.CompilerParam...  177 us
    ppermute x35, starting transfers between devices, send_xor(): return lax.ppermute(values, axis, [(j, j ^ distance) for j in range(size)])  45.3 us
    dot_general x6, matrix products, dot_tn(): lax.dot_general(a, b, (((0,), (0,)), ((), ())), preferred_element_type=F32)  44.7 us
    ppermute x35, waiting for transfers between devices, send_xor(): return lax.ppermute(values, axis, [(j, j ^ distance) for j in range(size)])  44.5 us
    dot_general x2, matrix products, dot_nt(): lax.dot_general(a, b, (((1,), (1,)), ((), ())), preferred_element_type=F32)  26 us
    all_to_all x1, waiting for transfers between devices, local(): lax.all_to_all(sent, 'ex', split_axis=0, concat_axis=0, tiled=True)  18.3 us
    all_to_all x1, starting transfers between devices, local(): lax.all_to_all(sent, 'ex', split_axis=0, concat_axis=0, tiled=True)  10.4 us
  transfers between devices with their start and end apart: 41, of which 19 were waited for; matrix products, arithmetic and copies ran while one was open for 21% of the time, Pallas kernels for 27%

profile of v2, /device:TPU:0, one launch (start us, length us, event | category | flops | bytes accessed | tf_op | source)
XLA Modules:
  0.0 440.8 jit_solution(8969779181219286790)
XLA Ops:
  7.2 7.8 %prep.1 = (s32[8,784]{1,0:T(8,128)}, s32[784,128]{1,0:T(8,128)}, bf16[8,208,768]{2,1,0:T(8,128)(2,1)}) custom-call(s32[2,784]{1,0:T(2,128)} %bitcast.112, s32[1,784]{1,0:T(1,128)} %refs_1_.2, bf16[784,768]{1,0:T(8,128)(2,1)} %refs_6_.4), custom_call_target="tpu_custom_call" | custom-call | flops 4000000000 | bytes 6000000 | tf_op jit(solution)/shard_map/prep/pallas_call | solution.py:74
  15.0 5.3 %all-to-all-start.1 = ((bf16[8,208,768]{2,1,0:T(8,128)(2,1)}), bf16[8,208,768]{2,1,0:T(8,128)(2,1)S(1)}, u32[]{:S(2)}, u32[]{:S(2)}) async-start(bf16[8,208,768]{2,1,0:T(8,128)(2,1)} %get-tuple-element.41), calls=%async_computation.1 | async-start | bytes 5111808 | tf_op jit(solution)/shard_map/all_to_all | solution.py:766
  23.4 34.9 %attend.1 = (bf16[3,784,768]{2,1,0:T(8,128)(2,1)}, bf16[784,768]{1,0:T(8,128)(2,1)}, f32[16,784]{1,0:T(8,128)}, bf16[784,768]{1,0:T(8,128)(2,1)}, f32[784,768]{1...) custom-call(s32[1]{0:T(128)S(6)} %copy.37.refs_0_, ...), custom_call_target="tpu_custom_call" | custom-call | flops 10000000000 | bytes 20000000 | tf_op jit(solution)/shard_map/attend/pallas_call | solution.py:74
  58.3 10.4 %all-to-all-start = ((bf16[8,208,768]{2,1,0:T(8,128)(2,1)}), bf16[8,208,768]{2,1,0:T(8,128)(2,1)}, u32[]{:S(2)}, u32[]{:S(2)}) async-start(bf16[8,208,768]{2,1,0:T(8,128)(2,1)} %get-tuple-element.40), calls=%async_computation | async-start | bytes 5111808 | tf_op jit(solution)/shard_map/all_to_all | solution.py:833
  69.3 12.8 %convolution_convert_fusion = bf16[1664,3072]{1,0:T(8,128)(2,1)} fusion(bf16[1664,768]{1,0:T(8,128)(2,1)S(1)} %bitcast.108, bf16[1,3072,768]{2,1,0:T(8,128)(2,1)} %param.26), kind=kOutput, calls=%fused_computation | convolution fusion | flops 7856848896 | bytes 17498112 | tf_op jit(solution)/shard_map/dot_general | solution.py:42
  82.1 18.3 %all-to-all-done.refs_0_ = bf16[8,208,768]{2,1,0:T(8,128)(2,1)} async-done(((bf16[8,208,768]{2,1,0:T(8,128)(2,1)}), bf16[8,208,768]{2,1,0:T(8,128)(2,1)}, u32[]{:S(2)}, u32[]{:S(2)}) %all-to-all-start) | async-done | bytes 2555936 | tf_op jit(solution)/shard_map/all_to_all | solution.py:833
  100.4 51.6 %expert.1 = (bf16[8,208,3072]{2,1,0:T(8,128)(2,1)}, bf16[8,208,3072]{2,1,0:T(8,128)(2,1)}, bf16[8,208,768]{2,1,0:T(8,128)(2,1)}, f32[8,8,256]{2,1,0:T(8,128)}, f32[8,3072]{1,0:T(8,128)}, /*index=5*/f32[8,768]{1,0:T(8,128)}) custom-call(bf16[8,208,768]{2,1,0:T(8,128)(2,1)} %all-to-all-done.refs_0_, bf16[8,208,768]{2,1,0:T(8,128)(2,1)} %copy-done.15, ...), custom_call_target="tpu_custom_call" | custom-call | flops 8000000000 | bytes 40000000 | tf_op jit(solution)/shard_map/expert/pallas_call | solution.py:74
  152.1 13.7 %bitcast_convert_fusion.refs_1_.refs_10_ = bf16[768,3072]{1,0:T(8,128)(2,1)} fusion(bf16[8,208,768]{2,1,0:T(8,128)(2,1)} %all-to-all-done.refs_0_, bf16[8,208,3072]{2,1,0:T(8,128)(2,1)} %get-tuple-element.44), kind=kOutput, calls=%fused_computation.1 | convolution fusion | flops 7854096384 | bytes 17498112 | tf_op jit(solution)/shard_map/dot_general | solution.py:46
  166.8 13.3 %fusion.1.refs_2_ = bf16[8,208,768]{2,1,0:T(8,128)(2,1)} fusion(bf16[8,1,256]{2,1,0:T(2,128)(2,1)S(1)} %get-tuple-element.99, bf16[8,1,256]{2,1,0:T(2,128)(2,1)S(1)} %get-tuple-element.98, bf16[8,208,3072]{2,1,0:T(8,128)(2,1)} %bitcast.101, bf16[1,768,3072]{2,1,0:T(8,128)(2,1)} %param.24, pred[208]{0:T(512)(128)(4,1)S(1)} %iota_compare_fusion.2), kind=kOutput, calls=%fused_computation.4 | convolution fusion | flops 7867072512 | bytes 17506512 | tf_op jit(solution)/shard_map/dot_general | solution.py:42
  180.1 3.8 all-to-all-start.3
  183.9 13.7 %convolution_convert_fusion.1.refs_1_.refs_11_ = bf16[3072,768]{1,0:T(8,128)(2,1)} fusion(bf16[1664,3072]{1,0:T(8,128)(2,1)} %bitcast.93, bf16[1664,768]{1,0:T(8,128)(2,1)} %hold.5), kind=kOutput, calls=%fused_computation.7 | convolution fusion | flops 7854096384 | bytes 17498112 | tf_op jit(solution)/shard_map/dot_general | solution.py:46
  197.6 12.7 %produce.1.refs_12_ = bf16[1664,768]{1,0:T(8,128)(2,1)} custom-call(bf16[1664,3072]{1,0:T(8,128)(2,1)} %hold.6.refs_0_, bf16[3072,768]{1,0:T(8,128)(2,1)} %bitcast.102, f32[1,768]{1,0:T(1,128)} %refs_2_.6), custom_call_target="tpu_custom_call" | custom-call | flops 1 | bytes 1 | tf_op jit(solution)/shard_map/produce/pallas_call | solution.py:74
  210.3 5.1 %all-to-all-done.3.refs_9_ = bf16[8,208,768]{2,1,0:T(8,128)(2,1)S(1)} async-done(((bf16[8,208,768]{2,1,0:T(8,128)(2,1)}), bf16[8,208,768]{2,1,0:T(8,128)(2,1)S(1)}, u32[]{:S(2)}, u32[]{:S(2)}) %all-to-all-start.3) | async-done | bytes 2555936 | tf_op jit(solution)/shard_map/all_to_all | solution.py:889
  216.8 3.6 all-to-all-start.2
  221.1 13.4 %row_grad.1 = (f32[784,768]{1,0:T(8,128)}, bf16[784,768]{1,0:T(8,128)(2,1)}, f32[8,768]{1,0:T(8,128)}, f32[8,768]{1,0:T(8,128)}) custom-call(s32[784,128]{1,0:T(8,128)} %get-tuple-element.36.refs_0_, s32[8,784]{1,0:T(8,128)} %get-tuple-element.37.refs_12_.refs_1_, s32[2,784]{1,0:T(2,128)} %bitcast.114, f32[8,784]{1,0:T(8,128)} %get-tuple-element.38.refs_3_, ...), custom_call_target="tpu_custom_call" | custom-call | flops 1 | bytes 1 | tf_op jit(solution)/shard_map/row_grad/pallas_call | solution.py:74
  234.6 4.1 convolution_convert_fusion.5.refs_6_
  238.7 10.2 %attend_back_a.1.refs_0_ = bf16[784,768]{1,0:T(8,128)(2,1)} custom-call(s32[1]{0:T(128)S(6)} %copy.37.refs_0_, bf16[784,768]{1,0:T(8,128)(2,1)} %get-tuple-element.48.refs_1_, bf16[768,768]{1,0:T(8,128)(2,1)} %refs_2_.9, bf16[3,784,768]{2,1,0:T(8,128)(2,1)} %get-tuple-element.49.refs_3_, bf16[784,768]{1,0:T(8,128)(2,1)} %get-tuple-element.50.refs_4_, ...), custom_call_target="tpu_custom_call" | custom-call | flops 1 | bytes 1 | tf_op jit(solution)/shard_map/attend_back_a/pallas_call | solution.py:74
  248.8 4.5 %broadcast_select_fusion.1 = (bf16[768,768]{1,0:T(8,128)(2,1)}, bf16[768,768]{1,0:T(8,128)(2,1)}) fusion(bf16[768,768]{1,0:T(8,128)(2,1)} %convolution_convert_fusion.5.refs_6_, pred[]{:T(512)S(6)} %eq.6, bf16[784,768]{1,0:T(8,128)(2,1)} %get-tuple-element.46, bf16[784,768]{1,0:T(8,128)(2,1)} %attend_back_a.1.refs_0_), kind=kOutput, calls=%fused_computation.25 | convolution fusion | flops 926023680 | bytes 5947393 | tf_op jit(solution)/shard_map/dot_general | solution.py:46
  253.4 2.2 collective-permute-start
  257.0 10.0 %attend_back_b.1.refs_1_ = bf16[784,768]{1,0:T(8,128)(2,1)} custom-call(s32[1]{0:T(128)S(6)} %copy.37.refs_0_, bf16[784,768]{1,0:T(8,128)(2,1)} %get-tuple-element.48.refs_1_, bf16[768,768]{1,0:T(8,128)(2,1)} %refs_2_.9, bf16[3,784,768]{2,1,0:T(8,128)(2,1)} %get-tuple-element.49.refs_3_, bf16[784,768]{1,0:T(8,128)(2,1)} %get-tuple-element.50.refs_4_, ...), custom_call_target="tpu_custom_call" | custom-call | flops 1 | bytes 1 | tf_op jit(solution)/shard_map/attend_back_b/pallas_call | solution.py:74
  267.0 4.3 convolution_convert_fusion.3.refs_7_
  271.2 2.8 add_convert_fusion.1.refs_6_
  274.1 10.4 %attend_back_c.1.refs_2_ = bf16[784,768]{1,0:T(8,128)(2,1)} custom-call(s32[1]{0:T(128)S(6)} %copy.37.refs_0_, bf16[784,768]{1,0:T(8,128)(2,1)} %get-tuple-element.48.refs_1_, bf16[768,768]{1,0:T(8,128)(2,1)} %refs_2_.9, bf16[3,784,768]{2,1,0:T(8,128)(2,1)} %get-tuple-element.49.refs_3_, bf16[784,768]{1,0:T(8,128)(2,1)} %get-tuple-element.50.refs_4_, ...), custom_call_target="tpu_custom_call" | custom-call | flops 1 | bytes 1 | tf_op jit(solution)/shard_map/attend_back_c/pallas_call | solution.py:74
  284.5 4.3 broadcast_select_fusion
  288.7 2.9 collective-permute-start.1
  293.2 2.7 collective-permute-start.4
  296.7 2.4 pad_maximum_fusion.2.refs_5_
  304.1 5.9 %collective-permute-done.3 = bf16[192,768]{1,0:T(8,128)(2,1)S(1)} collective-permute-done((bf16[192,768]{1,0:T(8,128)(2,1)S(1)}, bf16[192,768]{1,0:T(8,128)(2,1)S(1)}, u32[]{:S(2)}, u32[]{:S(2)}) %collective-permute-start.3) | collective-permute-done | bytes 294944 | tf_op jit(solution)/shard_map/ppermute | solution.py:664
  311.0 10.7 %final.1 = (bf16[784,768]{1,0:T(8,128)(2,1)}, f32[8,768]{1,0:T(8,128)}) custom-call(bf16[784,768]{1,0:T(8,128)(2,1)} %attend_back_a.1.refs_0_, bf16[784,768]{1,0:T(8,128)(2,1)} %attend_back_b.1.refs_1_, bf16[784,768]{1,0:T(8,128)(2,1)} %attend_back_c.1.refs_2_, bf16[768,768]{1,0:T(8,128)(2,1)} %get-tuple-element.104.refs_3_, ...), custom_call_target="tpu_custom_call" | custom-call | flops 1 | bytes 1 | tf_op jit(solution)/shard_map/final/pallas_call | solution.py:74
  322.5 3.6 collective-permute-start.12
  327.0 4.0 collective-permute-done.12
  331.1 11.7 %collective-permute-done.11 = bf16[48,768]{1,0:T(8,128)(2,1)S(1)} collective-permute-done((bf16[48,768]{1,0:T(8,128)(2,1)S(1)}, bf16[48,768]{1,0:T(8,128)(2,1)S(1)}, u32[]{:S(2)}, u32[]{:S(2)}) %collective-permute-start.11) | collective-permute-done | bytes 73760 | tf_op jit(solution)/shard_map/ppermute | solution.py:664
  342.8 2.3 collective-permute-start.13
  345.1 2.2 collective-permute-start.15
  354.3 9.3 %combine.1.refs_1_ = bf16[784,768]{1,0:T(8,128)(2,1)} custom-call(s32[784,128]{1,0:T(8,128)} %get-tuple-element.36.refs_0_, s32[8,784]{1,0:T(8,128)} %get-tuple-element.37.refs_12_.refs_1_, s32[2,784]{1,0:T(2,128)} %bitcast.115, f32[8,784]{1,0:T(8,128)} %get-tuple-element.38.refs_3_, f32[784,768]{1,0:T(8,128)} %get-tuple-element.39.refs_5_.refs_4_, ...), custom_call_target="tpu_custom_call" | custom-call | flops 1 | bytes 1 | tf_op jit(solution)/shard_map/combine/pallas_call | solution.py:74
  364.3 1.8 fusion.8.refs_0_
  368.5 2.2 collective-permute-start.16
  373.4 1.8 collective-permute-start.23
  379.1 2.7 collective-permute-start.26
  383.7 2.6 collective-permute-start.28
  386.6 1.8 collective-permute-done.27
  388.9 1.8 collective-permute-start.30
  392.8 9.1 %collective-permute-done.30 = bf16[192,768]{1,0:T(8,128)(2,1)S(1)} collective-permute-done((bf16[192,768]{1,0:T(8,128)(2,1)S(1)}, bf16[192,768]{1,0:T(8,128)(2,1)S(1)}, u32[]{:S(2)}, u32[]{:S(2)}) %collective-permute-start.30) | collective-permute-done | bytes 294944 | tf_op jit(solution)/shard_map/ppermute | solution.py:664
  403.7 2.4 collective-permute-start.33
  418.7 3.3 select_convert_fusion
  422.1 5.7 %place_qkv.1 = f32[768,2304]{1,0:T(8,128)} custom-call(s32[1]{0:T(128)} %bitcast.18.refs_0_, bf16[768,768]{1,0:T(8,128)(2,1)} %copy-done.6, bf16[768,768]{1,0:T(8,128)(2,1)} %copy-done.5, bf16[768,768]{1,0:T(8,128)(2,1)} %copy-done.7, bf16[768,768]{1,0:T(8,128)(2,1)} %collective-permute-done.32.refs_4_), custom_call_target="tpu_custom_call" | custom-call | flops 1000000 | bytes 11796480 | tf_op jit(solution)/shard_map/place_qkv/pallas_call | solution.py:74
  427.8 2.9 bitcast_convert_fusion.2
  430.7 2.8 bitcast_convert_fusion.1
  (169 shorter events, 53.4 us)
Async XLA Ops:
  15.0 43.3 %all-to-all-start.1 = ((bf16[8,208,768]{2,1,0:T(8,128)(2,1)}), bf16[8,208,768]{2,1,0:T(8,128)(2,1)S(1)}, u32[]{:S(2)}, u32[]{:S(2)}) async-start(bf16[8,208,768]{2,1,0:T(8,128)(2,1)} %get-tuple-element.41), calls=%async_computation.1 | async-start | bytes 5111808 | tf_op jit(solution)/shard_map/all_to_all | solution.py:766
  58.3 11.0 %copy-start.15 = (bf16[8,208,768]{2,1,0:T(8,128)(2,1)}, bf16[8,208,768]{2,1,0:T(8,128)(2,1)S(1)}, u32[]{:S(2)}) copy-start(bf16[8,208,768]{2,1,0:T(8,128)(2,1)S(1)} %all-to-all-done.1.refs_1_) | copy-start | bytes 7667716
  58.3 42.1 %all-to-all-start = ((bf16[8,208,768]{2,1,0:T(8,128)(2,1)}), bf16[8,208,768]{2,1,0:T(8,128)(2,1)}, u32[]{:S(2)}, u32[]{:S(2)}) async-start(bf16[8,208,768]{2,1,0:T(8,128)(2,1)} %get-tuple-element.40), calls=%async_computation | async-start | bytes 5111808 | tf_op jit(solution)/shard_map/all_to_all | solution.py:833
  68.8 359.0 %reduce-scatter.3.cloned.1.call-start = ((), (), s32[]{:S(2)}) async-start(), calls=%async_computation.6 | async-start | bytes 5898240 | tf_op jit(solution)/shard_map/reduce_scatter | solution.py:884
  180.1 35.3 %all-to-all-start.3 = ((bf16[8,208,768]{2,1,0:T(8,128)(2,1)}), bf16[8,208,768]{2,1,0:T(8,128)(2,1)S(1)}, u32[]{:S(2)}, u32[]{:S(2)}) async-start(bf16[8,208,768]{2,1,0:T(8,128)(2,1)} %fusion.1.refs_2_), calls=%async_computation.3 | async-start | bytes 5111808 | tf_op jit(solution)/shard_map/all_to_all | solution.py:889
  216.8 38.8 %all-to-all-start.2 = ((bf16[8,208,768]{2,1,0:T(8,128)(2,1)}), bf16[8,208,768]{2,1,0:T(8,128)(2,1)S(1)}, u32[]{:S(2)}, u32[]{:S(2)}) async-start(bf16[8,208,768]{2,1,0:T(8,128)(2,1)} %bitcast.95), calls=%async_computation.2 | async-start | bytes 5111808 | tf_op jit(solution)/shard_map/all_to_all | solution.py:909
  220.4 210.3 %reduce-scatter.5.cloned.1.call-start = ((), (), s32[]{:S(2)}) async-start(), calls=%async_computation.7 | async-start | bytes 5898240 | tf_op jit(solution)/shard_map/reduce_scatter | solution.py:893
  253.4 17.9 %collective-permute-start = (bf16[768,768]{1,0:T(8,128)(2,1)}, bf16[768,768]{1,0:T(8,128)(2,1)}, u32[]{:S(2)}, u32[]{:S(2)}) collective-permute-start(bf16[768,768]{1,0:T(8,128)(2,1)} %get-tuple-element.100.refs_6_), channel_id=1, source_target_pairs={{0,1},{1,0},{2,3},{3,2},{4,5},{5,4},{6,7},{7,6},{8,9},{9,8},{10,11... | collective-permute-start | bytes 3538952 | tf_op jit(solution)/shard_map/ppermute | solution.py:664
  288.7 58.5 %collective-permute-start.1 = (bf16[768,768]{1,0:T(8,128)(2,1)}, bf16[768,768]{1,0:T(8,128)(2,1)}, u32[]{:S(2)}, u32[]{:S(2)}) collective-permute-start(bf16[768,768]{1,0:T(8,128)(2,1)} %get-tuple-element.102.refs_10_), channel_id=1, source_target_pairs={{0,1},{1,0},{2,3},{3,2},{4,5},{5,4},{6,7},{7,6},{8,9},{9,8},{10,11... | collective-permute-start | bytes 3538952 | tf_op jit(solution)/shard_map/ppermute | solution.py:664
  293.2 10.9 %collective-permute-start.4 = (bf16[192,768]{1,0:T(8,128)(2,1)S(1)}, bf16[192,768]{1,0:T(8,128)(2,1)S(1)}, u32[]{:S(2)}, u32[]{:S(2)}) collective-permute-start(bf16[192,768]{1,0:T(8,128)(2,1)S(1)} %get-tuple-element.82), channel_id=1, source_target_pairs={{0,6},{1,7},{2,4},{3,5},{4,2},{5,3},{6,0},{7,1},{8,14},{9,15},{10,... | collective-permute-start | bytes 884744 | tf_op jit(solution)/shard_map/ppermute | solution.py:664
  295.9 14.1 %collective-permute-start.3 = (bf16[192,768]{1,0:T(8,128)(2,1)S(1)}, bf16[192,768]{1,0:T(8,128)(2,1)S(1)}, u32[]{:S(2)}, u32[]{:S(2)}) collective-permute-start(bf16[192,768]{1,0:T(8,128)(2,1)S(1)} %get-tuple-element.83), channel_id=1, source_target_pairs={{0,4},{1,5},{2,6},{3,7},{4,0},{5,1},{6,2},{7,3},{8,12},{9,13},{10,... | collective-permute-start | bytes 884744 | tf_op jit(solution)/shard_map/ppermute | solution.py:664
  296.5 13.7 %collective-permute-start.2 = (bf16[192,768]{1,0:T(8,128)(2,1)S(1)}, bf16[192,768]{1,0:T(8,128)(2,1)S(1)}, u32[]{:S(2)}, u32[]{:S(2)}) collective-permute-start(bf16[192,768]{1,0:T(8,128)(2,1)S(1)} %get-tuple-element.81), channel_id=1, source_target_pairs={{0,2},{1,3},{2,0},{3,1},{4,6},{5,7},{6,4},{7,5},{8,10},{9,11},{10,... | collective-permute-start | bytes 884744 | tf_op jit(solution)/shard_map/ppermute | solution.py:664
  302.3 24.6 %copy-start.23 = (f32[2,768]{1,0:T(2,128)}, f32[2,768]{1,0:T(2,128)S(1)}, u32[]{:S(2)}) copy-start(f32[2,768]{1,0:T(2,128)S(1)} %slice.68) | copy-start | bytes 18436
  311.0 11.4 %copy-start.14 = (bf16[192,768]{1,0:T(8,128)(2,1)S(1)}, bf16[192,768]{1,0:T(8,128)(2,1)}, u32[]{:S(2)}) copy-start(bf16[192,768]{1,0:T(8,128)(2,1)} %fusion.11.refs_9_) | copy-start | bytes 884740
  311.0 15.9 %copy-start.21 = (f32[8,768]{1,0:T(8,128)S(1)}, f32[8,768]{1,0:T(8,128)}, u32[]{:S(2)}) copy-start(f32[8,768]{1,0:T(8,128)} %get-tuple-element.56) | copy-start | bytes 73732
  311.0 36.2 %copy-start.19 = (bf16[768,768]{1,0:T(8,128)(2,1)S(1)}, bf16[768,768]{1,0:T(8,128)(2,1)}, u32[]{:S(2)}) copy-start(bf16[768,768]{1,0:T(8,128)(2,1)} %get-tuple-element.103) | copy-start | bytes 3538948
  322.5 8.6 %collective-permute-start.12 = (bf16[48,768]{1,0:T(8,128)(2,1)S(1)}, bf16[48,768]{1,0:T(8,128)(2,1)S(1)}, u32[]{:S(2)}, u32[]{:S(2)}) collective-permute-start(bf16[48,768]{1,0:T(8,128)(2,1)S(1)} %get-tuple-element.96), channel_id=1, source_target_pairs={{0,24},{8,16},{16,8},{24,0},{1,25},{9,17},{17,9},{25,1},{2,26},{10... | collective-permute-start | bytes 221192 | tf_op jit(solution)/shard_map/ppermute | solution.py:664
  326.1 16.7 %collective-permute-start.11 = (bf16[48,768]{1,0:T(8,128)(2,1)S(1)}, bf16[48,768]{1,0:T(8,128)(2,1)S(1)}, u32[]{:S(2)}, u32[]{:S(2)}) collective-permute-start(bf16[48,768]{1,0:T(8,128)(2,1)S(1)} %get-tuple-element.97), channel_id=1, source_target_pairs={{0,16},{8,24},{16,0},{24,8},{1,17},{9,25},{17,1},{25,9},{2,18},{10... | collective-permute-start | bytes 221192 | tf_op jit(solution)/shard_map/ppermute | solution.py:664
  326.1 16.7 %collective-permute-start.10 = (bf16[48,768]{1,0:T(8,128)(2,1)S(1)}, bf16[48,768]{1,0:T(8,128)(2,1)S(1)}, u32[]{:S(2)}, u32[]{:S(2)}) collective-permute-start(bf16[48,768]{1,0:T(8,128)(2,1)S(1)} %get-tuple-element.95), channel_id=1, source_target_pairs={{0,8},{8,0},{16,24},{24,16},{1,9},{9,1},{17,25},{25,17},{2,10},{10... | collective-permute-start | bytes 221192 | tf_op jit(solution)/shard_map/ppermute | solution.py:664
  327.0 23.6 %collective-permute-start.5 = (f32[12,768]{1,0:T(8,128)S(1)}, f32[12,768]{1,0:T(8,128)S(1)}, u32[]{:S(2)}, u32[]{:S(2)}) collective-permute-start(f32[12,768]{1,0:T(8,128)S(1)} %pad_maximum_fusion.7), channel_id=1, source_target_pairs={{0,1},{1,0},{2,3},{3,2},{4,5},{5,4},{6,7},{7,6},{8,9},{9,8},{10,11... | collective-permute-start | bytes 110600 | tf_op jit(solution)/shard_map/ppermute | solution.py:664
  342.8 9.3 %collective-permute-start.13 = (bf16[48,768]{1,0:T(8,128)(2,1)S(1)}, bf16[48,768]{1,0:T(8,128)(2,1)S(1)}, u32[]{:S(2)}, u32[]{:S(2)}) collective-permute-start(bf16[48,768]{1,0:T(8,128)(2,1)S(1)} %fusion.17), channel_id=1, source_target_pairs={{0,24},{8,16},{16,8},{24,0},{1,25},{9,17},{17,9},{25,1},{2,26},{10... | collective-permute-start | bytes 221192 | tf_op jit(solution)/shard_map/ppermute | solution.py:664
  345.1 7.6 %collective-permute-start.14 = (bf16[48,768]{1,0:T(8,128)(2,1)S(1)}, bf16[48,768]{1,0:T(8,128)(2,1)S(1)}, u32[]{:S(2)}, u32[]{:S(2)}) collective-permute-start(bf16[48,768]{1,0:T(8,128)(2,1)S(1)} %fusion.17), channel_id=1, source_target_pairs={{0,16},{8,24},{16,0},{24,8},{1,17},{9,25},{17,1},{25,9},{2,18},{10... | collective-permute-start | bytes 221192 | tf_op jit(solution)/shard_map/ppermute | solution.py:664
  345.1 9.2 %collective-permute-start.15 = (bf16[48,768]{1,0:T(8,128)(2,1)S(1)}, bf16[48,768]{1,0:T(8,128)(2,1)S(1)}, u32[]{:S(2)}, u32[]{:S(2)}) collective-permute-start(bf16[48,768]{1,0:T(8,128)(2,1)S(1)} %fusion.17), channel_id=1, source_target_pairs={{0,8},{8,0},{16,24},{24,16},{1,9},{9,1},{17,25},{25,17},{2,10},{10... | collective-permute-start | bytes 221192 | tf_op jit(solution)/shard_map/ppermute | solution.py:664
  349.1 14.5 %collective-permute-start.22 = (bf16[192,768]{1,0:T(8,128)(2,1)S(1)}, bf16[192,768]{1,0:T(8,128)(2,1)S(1)}, u32[]{:S(2)}, u32[]{:S(2)}) collective-permute-start(bf16[192,768]{1,0:T(8,128)(2,1)S(1)} %get-tuple-element.76), channel_id=1, source_target_pairs={{0,6},{1,7},{2,4},{3,5},{4,2},{5,3},{6,0},{7,1},{8,14},{9,15},{10,... | collective-permute-start | bytes 884744 | tf_op jit(solution)/shard_map/ppermute | solution.py:664
  350.5 13.0 %collective-permute-start.21 = (bf16[192,768]{1,0:T(8,128)(2,1)S(1)}, bf16[192,768]{1,0:T(8,128)(2,1)S(1)}, u32[]{:S(2)}, u32[]{:S(2)}) collective-permute-start(bf16[192,768]{1,0:T(8,128)(2,1)S(1)} %get-tuple-element.77), channel_id=1, source_target_pairs={{0,4},{1,5},{2,6},{3,7},{4,0},{5,1},{6,2},{7,3},{8,12},{9,13},{10,... | collective-permute-start | bytes 884744 | tf_op jit(solution)/shard_map/ppermute | solution.py:664
  352.1 12.2 %collective-permute-start.20 = (bf16[192,768]{1,0:T(8,128)(2,1)S(1)}, bf16[192,768]{1,0:T(8,128)(2,1)S(1)}, u32[]{:S(2)}, u32[]{:S(2)}) collective-permute-start(bf16[192,768]{1,0:T(8,128)(2,1)S(1)} %get-tuple-element.75), channel_id=1, source_target_pairs={{0,2},{1,3},{2,0},{3,1},{4,6},{5,7},{6,4},{7,5},{8,10},{9,11},{10,... | collective-permute-start | bytes 884744 | tf_op jit(solution)/shard_map/ppermute | solution.py:664
  352.7 18.5 %collective-permute-start.6 = (f32[12,768]{1,0:T(8,128)S(1)}, f32[12,768]{1,0:T(8,128)S(1)}, u32[]{:S(2)}, u32[]{:S(2)}) collective-permute-start(f32[12,768]{1,0:T(8,128)S(1)} %fusion.20), channel_id=1, source_target_pairs={{0,2},{1,3},{2,0},{3,1},{4,6},{5,7},{6,4},{7,5},{8,10},{9,11},{10,... | collective-permute-start | bytes 110600 | tf_op jit(solution)/shard_map/ppermute | solution.py:664
  367.1 6.3 %collective-permute-start.25 = (bf16[48,768]{1,0:T(8,128)(2,1)S(1)}, bf16[48,768]{1,0:T(8,128)(2,1)S(1)}, u32[]{:S(2)}, u32[]{:S(2)}) collective-permute-start(bf16[48,768]{1,0:T(8,128)(2,1)S(1)} %get-tuple-element.89), channel_id=1, source_target_pairs={{0,24},{8,16},{16,8},{24,0},{1,25},{9,17},{17,9},{25,1},{2,26},{10... | collective-permute-start | bytes 221192 | tf_op jit(solution)/shard_map/ppermute | solution.py:664
  367.6 14.7 %collective-permute-start.17 = (bf16[192,768]{1,0:T(8,128)(2,1)S(1)}, bf16[192,768]{1,0:T(8,128)(2,1)S(1)}, u32[]{:S(2)}, u32[]{:S(2)}) collective-permute-start(bf16[192,768]{1,0:T(8,128)(2,1)S(1)} %pad_maximum_fusion.5), channel_id=1, source_target_pairs={{0,4},{1,5},{2,6},{3,7},{4,0},{5,1},{6,2},{7,3},{8,12},{9,13},{10,... | collective-permute-start | bytes 884744 | tf_op jit(solution)/shard_map/ppermute | solution.py:664
  368.5 15.1 %collective-permute-start.16 = (bf16[192,768]{1,0:T(8,128)(2,1)S(1)}, bf16[192,768]{1,0:T(8,128)(2,1)S(1)}, u32[]{:S(2)}, u32[]{:S(2)}) collective-permute-start(bf16[192,768]{1,0:T(8,128)(2,1)S(1)} %pad_maximum_fusion.5), channel_id=1, source_target_pairs={{0,6},{1,7},{2,4},{3,5},{4,2},{5,3},{6,0},{7,1},{8,14},{9,15},{10,... | collective-permute-start | bytes 884744 | tf_op jit(solution)/shard_map/ppermute | solution.py:664
  370.7 15.6 %collective-permute-start.18 = (bf16[192,768]{1,0:T(8,128)(2,1)S(1)}, bf16[192,768]{1,0:T(8,128)(2,1)S(1)}, u32[]{:S(2)}, u32[]{:S(2)}) collective-permute-start(bf16[192,768]{1,0:T(8,128)(2,1)S(1)} %pad_maximum_fusion.5), channel_id=1, source_target_pairs={{0,2},{1,3},{2,0},{3,1},{4,6},{5,7},{6,4},{7,5},{8,10},{9,11},{10,... | collective-permute-start | bytes 884744 | tf_op jit(solution)/shard_map/ppermute | solution.py:664
  371.1 6.1 %collective-permute-start.24 = (bf16[48,768]{1,0:T(8,128)(2,1)S(1)}, bf16[48,768]{1,0:T(8,128)(2,1)S(1)}, u32[]{:S(2)}, u32[]{:S(2)}) collective-permute-start(bf16[48,768]{1,0:T(8,128)(2,1)S(1)} %get-tuple-element.90), channel_id=1, source_target_pairs={{0,16},{8,24},{16,0},{24,8},{1,17},{9,25},{17,1},{25,9},{2,18},{10... | collective-permute-start | bytes 221192 | tf_op jit(solution)/shard_map/ppermute | solution.py:664
  373.4 4.8 %collective-permute-start.23 = (bf16[48,768]{1,0:T(8,128)(2,1)S(1)}, bf16[48,768]{1,0:T(8,128)(2,1)S(1)}, u32[]{:S(2)}, u32[]{:S(2)}) collective-permute-start(bf16[48,768]{1,0:T(8,128)(2,1)S(1)} %get-tuple-element.88), channel_id=1, source_target_pairs={{0,8},{8,0},{16,24},{24,16},{1,9},{9,1},{17,25},{25,17},{2,10},{10... | collective-permute-start | bytes 221192 | tf_op jit(solution)/shard_map/ppermute | solution.py:664
  377.3 28.8 %collective-permute-start.7 = (f32[12,768]{1,0:T(8,128)S(1)}, f32[12,768]{1,0:T(8,128)S(1)}, u32[]{:S(2)}, u32[]{:S(2)}) collective-permute-start(f32[12,768]{1,0:T(8,128)S(1)} %add.129), channel_id=1, source_target_pairs={{0,4},{1,5},{2,6},{3,7},{4,0},{5,1},{6,2},{7,3},{8,12},{9,13},{10,... | collective-permute-start | bytes 110600 | tf_op jit(solution)/shard_map/ppermute | solution.py:664
  379.1 7.5 %collective-permute-start.26 = (bf16[48,768]{1,0:T(8,128)(2,1)S(1)}, bf16[48,768]{1,0:T(8,128)(2,1)S(1)}, u32[]{:S(2)}, u32[]{:S(2)}) collective-permute-start(bf16[48,768]{1,0:T(8,128)(2,1)S(1)} %fusion.14), channel_id=1, source_target_pairs={{0,24},{8,16},{16,8},{24,0},{1,25},{9,17},{17,9},{25,1},{2,26},{10... | collective-permute-start | bytes 221192 | tf_op jit(solution)/shard_map/ppermute | solution.py:664
  382.3 6.1 %collective-permute-start.27 = (bf16[48,768]{1,0:T(8,128)(2,1)S(1)}, bf16[48,768]{1,0:T(8,128)(2,1)S(1)}, u32[]{:S(2)}, u32[]{:S(2)}) collective-permute-start(bf16[48,768]{1,0:T(8,128)(2,1)S(1)} %fusion.14), channel_id=1, source_target_pairs={{0,16},{8,24},{16,0},{24,8},{1,17},{9,25},{17,1},{25,9},{2,18},{10... | collective-permute-start | bytes 221192 | tf_op jit(solution)/shard_map/ppermute | solution.py:664
  383.7 5.1 %collective-permute-start.28 = (bf16[48,768]{1,0:T(8,128)(2,1)S(1)}, bf16[48,768]{1,0:T(8,128)(2,1)S(1)}, u32[]{:S(2)}, u32[]{:S(2)}) collective-permute-start(bf16[48,768]{1,0:T(8,128)(2,1)S(1)} %fusion.14), channel_id=1, source_target_pairs={{0,8},{8,0},{16,24},{24,16},{1,9},{9,1},{17,25},{25,17},{2,10},{10... | collective-permute-start | bytes 221192 | tf_op jit(solution)/shard_map/ppermute | solution.py:664
  388.9 13.0 %collective-permute-start.30 = (bf16[192,768]{1,0:T(8,128)(2,1)S(1)}, bf16[192,768]{1,0:T(8,128)(2,1)S(1)}, u32[]{:S(2)}, u32[]{:S(2)}) collective-permute-start(bf16[192,768]{1,0:T(8,128)(2,1)S(1)} %pad_maximum_fusion.6), channel_id=1, source_target_pairs={{0,4},{1,5},{2,6},{3,7},{4,0},{5,1},{6,2},{7,3},{8,12},{9,13},{10,... | collective-permute-start | bytes 884744 | tf_op jit(solution)/shard_map/ppermute | solution.py:664
  390.7 11.2 %collective-permute-start.29 = (bf16[192,768]{1,0:T(8,128)(2,1)S(1)}, bf16[192,768]{1,0:T(8,128)(2,1)S(1)}, u32[]{:S(2)}, u32[]{:S(2)}) collective-permute-start(bf16[192,768]{1,0:T(8,128)(2,1)S(1)} %pad_maximum_fusion.6), channel_id=1, source_target_pairs={{0,6},{1,7},{2,4},{3,5},{4,2},{5,3},{6,0},{7,1},{8,14},{9,15},{10,... | collective-permute-start | bytes 884744 | tf_op jit(solution)/shard_map/ppermute | solution.py:664
  392.1 11.0 %collective-permute-start.31 = (bf16[192,768]{1,0:T(8,128)(2,1)S(1)}, bf16[192,768]{1,0:T(8,128)(2,1)S(1)}, u32[]{:S(2)}, u32[]{:S(2)}) collective-permute-start(bf16[192,768]{1,0:T(8,128)(2,1)S(1)} %pad_maximum_fusion.6), channel_id=1, source_target_pairs={{0,2},{1,3},{2,0},{3,1},{4,6},{5,7},{6,4},{7,5},{8,10},{9,11},{10,... | collective-permute-start | bytes 884744 | tf_op jit(solution)/shard_map/ppermute | solution.py:664
  392.6 10.9 %copy-start.13 = (bf16[192,768]{1,0:T(8,128)(2,1)}, bf16[192,768]{1,0:T(8,128)(2,1)S(1)}, u32[]{:S(2)}) copy-start(bf16[192,768]{1,0:T(8,128)(2,1)S(1)} %broadcast_select_fusion.14) | copy-start | bytes 884740
  392.7 26.0 %collective-permute-start.19 = (bf16[768,768]{1,0:T(8,128)(2,1)S(1)}, bf16[768,768]{1,0:T(8,128)(2,1)S(1)}, u32[]{:S(2)}, u32[]{:S(2)}) collective-permute-start(bf16[768,768]{1,0:T(8,128)(2,1)S(1)} %pad_maximum_fusion.3.refs_1_), channel_id=1, source_target_pairs={{0,1},{1,0},{2,3},{3,2},{4,5},{5,4},{6,7},{7,6},{8,9},{9,8},{10,11... | collective-permute-start | bytes 3538952 | tf_op jit(solution)/shard_map/ppermute | solution.py:664
  403.6 18.4 %copy-start.7 = (bf16[768,768]{1,0:T(8,128)(2,1)}, bf16[768,768]{1,0:T(8,128)(2,1)S(1)}, u32[]{:S(2)}) copy-start(bf16[768,768]{1,0:T(8,128)(2,1)S(1)} %pad_maximum_fusion.4.refs_3_) | copy-start | bytes 3538948
  403.6 18.4 %collective-permute-start.32 = (bf16[768,768]{1,0:T(8,128)(2,1)S(1)}, bf16[768,768]{1,0:T(8,128)(2,1)}, u32[]{:S(2)}, u32[]{:S(2)}) collective-permute-start(bf16[768,768]{1,0:T(8,128)(2,1)S(1)} %pad_maximum_fusion.4.refs_3_), channel_id=1, source_target_pairs={{0,1},{1,0},{2,3},{3,2},{4,5},{5,4},{6,7},{7,6},{8,9},{9,8},{10,11... | collective-permute-start | bytes 3538952 | tf_op jit(solution)/shard_map/ppermute | solution.py:664
  403.7 4.1 collective-permute-start.33
  406.7 4.4 collective-permute-start.8
  409.0 5.0 %collective-permute-start.34 = (f32[30,128]{1,0:T(8,128)}, f32[30,128]{1,0:T(8,128)}, u32[]{:S(2)}, u32[]{:S(2)}) collective-permute-start(f32[30,128]{1,0:T(8,128)} %fusion.19), channel_id=1, source_target_pairs={{0,16},{8,24},{16,0},{24,8},{1,17},{9,25},{17,1},{25,9},{2,18},{10... | collective-permute-start | bytes 46088 | tf_op jit(solution)/shard_map/ppermute | solution.py:664
  412.0 5.5 %collective-permute-start.9 = (f32[12,768]{1,0:T(8,128)S(1)}, f32[12,768]{1,0:T(8,128)S(1)}, u32[]{:S(2)}, u32[]{:S(2)}) collective-permute-start(f32[12,768]{1,0:T(8,128)S(1)} %add.131), channel_id=1, source_target_pairs={{0,16},{8,24},{16,0},{24,8},{1,17},{9,25},{17,1},{25,9},{2,18},{10... | collective-permute-start | bytes 110600 | tf_op jit(solution)/shard_map/ppermute | solution.py:664
  (23 other events, 133.2 us)
Sparse Core Ops, SparseCore 0:
  166.0 84.8 reduce-scatter.2
  253.1 90.3 reduce-scatter.4

commit v3 on v2

--- a/solution.py
+++ b/solution.py
@@ -664,11 +664,17 @@
     return lax.ppermute(values, axis, [(j, j ^ distance) for j in range(size)])
 
 
-def trade_sum(parts, axis, size, stride, mine):
-    total = lax.dynamic_index_in_dim(parts, mine, 0, keepdims=False).astype(F32)
+def trade_sum(parts, axis, size, stride, mine, extra, after):
+    def pick(place):
+        part = lax.dynamic_index_in_dim(parts, place, 0, keepdims=False)
+        return part if extra is None else jnp.concatenate([part, extra], axis=0)
+
+    own = pick(mine)
+    if after:
+        own = hold(own, after)
+    total = own.astype(F32)
     for d in range(1, parts.shape[0]):
-        sent = lax.dynamic_index_in_dim(parts, mine ^ d, 0, keepdims=False)
-        total = total + send_xor(sent, axis, size, d * stride).astype(F32)
+        total = total + send_xor(pick(mine ^ d), axis, size, d * stride).astype(F32)
     return total.astype(parts.dtype)
 
 
@@ -681,48 +687,49 @@
 
 
 class PairSum:
-    def __init__(self, first, second, sizes):
+    def __init__(self, first, second, wide, plan):
         self.width = first.shape[1]
-        self.wide, self.reps = sizes["ex"], sizes["rep"]
-        place = lax.axis_index("ex")
-        self.core, self.chip = place % 2, place // 2
-        self.rep = lax.axis_index("rep")
+        self.wide = wide
+        self.plan = plan
+        self.core = lax.axis_index("ex") % 2
         self.keep = jnp.where(self.core == 0, first, second)
         self.value = jnp.where(self.core == 0, second, first)
+        self.extra = None
         self.stage = 0
 
-    def split(self, values, count):
-        return values.reshape(count, -1, self.width)
-
-    def step(self):
+    def step(self, after=()):
         v = self.value
-        chips = self.wide // 2
+        deep = len(self.plan)
         if self.stage == 0:
             other = send_xor(v, "ex", self.wide, 1)
-            v = (self.keep.astype(F32) + other.astype(F32)).astype(v.dtype)
-        elif self.stage == 1:
-            v = trade_sum(self.split(v, chips), "ex", self.wide, 2, self.chip)
-        elif self.stage == 2:
-            v = trade_sum(self.split(v, self.reps), "rep", self.reps, 1, self.rep)
-        elif self.stage == 3:
-            v = gather_group(v, "rep", self.reps, 1, self.reps, self.rep)
-        elif self.stage == 4:
-            v = gather_group(v, "ex", self.wide, 2, chips, self.chip)
+            keep = hold(self.keep, after) if after else self.keep
+            v = (keep.astype(F32) + other.astype(F32)).astype(v.dtype)
+        elif self.stage <= deep:
+            axis, size, stride, count = self.plan[self.stage - 1]
+            mine = (lax.axis_index(axis) // stride) % count
+            parts = v.reshape(count, -1, self.width)
+            v = trade_sum(parts, axis, size, stride, mine, self.extra, after)
+            if self.extra is not None:
+                rows = parts.shape[1]
+                self.extra = v[rows:]
+                v = v[:rows]
+        else:
+            axis, size, stride, count = self.plan[2 * deep - self.stage]
+            mine = (lax.axis_index(axis) // stride) % count
+            v = gather_group(v, axis, size, stride, count, mine)
+            if after:
+                v = hold(v, after)
         self.stage += 1
         self.value = v
         return v
 
+    def left(self):
+        return 2 * len(self.plan) + 1 - self.stage
+
     def finish(self):
-        while self.stage < 5:
+        while self.left():
             self.step()
         return self.value, send_xor(self.value, "ex", self.wide, 1)
-
-
-def sum_small(values, axes):
-    for axis, size in axes:
-        for bit in bits_below(size):
-            values = values + send_xor(values, axis, size, bit)
-    return values
 
 
 def local(
@@ -911,15 +918,6 @@
     )
 
     reps = sizes["rep"]
-    bias_sum = sum_small(
-        jnp.concatenate([bin_sum[0], bback_sum[0]]).reshape(-1, 128), [("rep", reps)]
-    ).reshape(-1)
-    rank = lax.axis_index("rep")
-    bin_out = lax.dynamic_slice_in_dim(bias_sum, rank * (hidden_units // reps), hidden_units // reps)
-    bback_out = lax.dynamic_slice_in_dim(
-        bias_sum, hidden_units + rank * (width // reps), width // reps
-    )
-
     grad_residual, grad_branch, small_two, route_grad = call(
         functools.partial(row_grad_body, experts),
         (
@@ -950,6 +948,9 @@
     def advance():
         return [s.step() for s in sums]
 
+    reps = sizes["rep"]
+    plane_hops = [("ex", sizes["ex"], bit, 2) for bit in bits_below(sizes["ex"])[1:]]
+    rep_hops = [("rep", reps, bit, 2) for bit in bits_below(reps)]
     packed_grads = []
     parts = [out_part]
     waiting = [out_part]
@@ -976,7 +977,7 @@
                 pltpu.VMEM((toks, LANES), F32),
                 pltpu.VMEM((toks, LANES), F32),
             ],
-            cost=(1, 1, 0),
+            cost=(8e9, 6e6, 2e6),
             name="attend_back_" + "abcdef"[g],
             after=waiting,
         )(image_kind, grad_branch, w_out, qkv, mix, logsum)
@@ -984,7 +985,8 @@
         waiting = advance()
         parts.append(dot_tn(low_one, packed).astype(BF16))
         if len(parts) == 2:
-            sums.append(PairSum(*parts, sizes))
+            order = plane_hops[:: 1 if g == 0 else -1]
+            sums.append(PairSum(*parts, sizes["ex"], order + rep_hops))
             parts = []
             waiting.append(sums[-1].value)
         else:
@@ -1001,29 +1003,46 @@
         functools.partial(final_body, groups),
         (sds((toks, width), BF16), sds((8, width), F32)),
         scratch=[pltpu.VMEM((toks, width), F32)],
-        cost=(1, 1, 0),
+        cost=(3e9, 14e6, 0),
         name="final",
-        after=waiting,
+        after=[sums[1].value],
     )(*packed_grads, *w_groups, tokens, gains[0], grad_residual)
-    last = sums[1]
-
+    ahead, last = sums
+    small = jnp.concatenate([small_one[0:2], small_two[0:2], route_grad], axis=0)
+    small_rows = small.shape[0]
+    added = last.step([small_one])
+    last.extra = jnp.pad(small, ((0, -small_rows % 16), (0, 0))).astype(BF16)
     result = call(
         functools.partial(combine_body, experts),
         sds((toks, width), BF16),
-        cost=(1, 1, 0),
+        cost=(2e9, 8e6, 0),
         name="combine",
-        after=[last.step()],
+        after=[added, ahead.value, first_out],
     )(slot_col, slots, routes_row, probs, residual, returned)
+    ahead.step([result])
+    last.step([result])
+    bin_sum = hold(bin_sum, [result])
+    while ahead.stage < len(plane_hops) + 1:
+        ahead.step()
+        last.step()
+    bias_rows = jnp.concatenate([bin_sum[0].reshape(-1, width), bback_sum[0:1]], axis=0)
+    bias_rows = jnp.pad(bias_rows, ((0, -bias_rows.shape[0] % 16), (0, 0))).astype(BF16)
+    ahead.extra = bias_rows
+    while last.left() > 1:
+        if ahead.left():
+            ahead.step([second_out] if ahead.left() == 1 else ())
+        last.step()
     last.step()
-    last.value = hold(last.value, [result])
-    last.step()
-    last.step()
-
-    small = sum_small(
-        jnp.concatenate([small_one[0:2], small_two[0:2], route_grad], axis=0),
-        [("ex", sizes["ex"]), ("rep", reps)],
-    )
-    pairs = [s.finish() for s in sums]
+    pairs = [ahead.finish(), last.finish()]
+    rank = lax.axis_index("rep")
+    bias_sum = ahead.extra.astype(F32)
+    bin_out = bias_sum[: hidden_units // width].reshape(-1)
+    bin_out = lax.dynamic_slice_in_dim(bin_out, rank * (hidden_units // reps), hidden_units // reps)
+    bback_out = lax.dynamic_slice_in_dim(
+        bias_sum[hidden_units // width], rank * (width // reps), width // reps
+    )
+    small = last.extra.astype(F32)
+    small = small + send_xor(small, "ex", sizes["ex"], 1)
     core = lax.axis_index("ex") % 2
     out_grad = jnp.where(core == 0, *pairs[0]).astype(F32)
     qkv_grad = place_qkv(pairs, core)
@@ -1036,7 +1055,7 @@
         out_grad,
         small[2],
         small[3],
-        small[4:].T,
+        small[4:small_rows].T,
         first_out[None],
         bin_out[None],
         second_out[None],

time: 447 us -> 424 us (0.949)
  starting transfers between devices: 69 us -> 40.7 us
  waiting for transfers between devices: 68.6 us -> 57.1 us
  Pallas kernels: 177 us -> 187 us
    ppermute x35 -> x21, starting transfers between devices: 45.3 us -> 23 us  [send_xor(): return lax.ppermute(values, axis, [(j, j ^ distance) for j in range(size)])]
    pallas_call x11, Pallas kernels: 177 us -> 187 us  [run(): pl.pallas_call(inner, in_specs=specs, compiler_params=pltpu.CompilerParam...]
    ppermute x35 -> x21, waiting for transfers between devices: 44.5 us -> 34.2 us  [send_xor(): return lax.ppermute(values, axis, [(j, j ^ distance) for j in range(size)])]
    all_to_all x1, starting transfers between devices: 10.4 us -> 4.4 us  [local(): lax.all_to_all(sent, 'ex', split_axis=0, concat_axis=0, tiled=True)]
  transfers between devices with their start and end apart: 41 -> 27, of which waited for: 19 -> 13; matrix products, arithmetic and copies ran while one was open for 21% -> 24% of each run, Pallas kernels for 27% -> 29%
where the time goes in v3:
time: 424 us; the launch traced here: 417 us
  Pallas kernels  187 us (44%)
  matrix products  71.8 us (17%)
  waiting for transfers between devices  57.1 us (13%)
  starting transfers between devices  40.7 us (10%)
  other arithmetic  27.9 us (7%)
  local copies, waits for them, and re-layouts  16.6 us (4%)
  between operations  15.7 us (4%)
    pallas_call x11, Pallas kernels, run(): pl.pallas_call(inner, in_specs=specs, compiler_params=pltpu.CompilerParam...  187 us
    dot_general x6, matrix products, dot_tn(): lax.dot_general(a, b, (((0,), (0,)), ((), ())), preferred_element_type=F32)  45.7 us
    ppermute x21, waiting for transfers between devices, send_xor(): return lax.ppermute(values, axis, [(j, j ^ distance) for j in range(size)])  34.2 us
    dot_general x2, matrix products, dot_nt(): lax.dot_general(a, b, (((1,), (1,)), ((), ())), preferred_element_type=F32)  26.1 us
    ppermute x21, starting transfers between devices, send_xor(): return lax.ppermute(values, axis, [(j, j ^ distance) for j in range(size)])  23 us
    all_to_all x1, waiting for transfers between devices, local(): lax.all_to_all(sent, 'ex', split_axis=0, concat_axis=0, tiled=True)  18.2 us
  transfers between devices with their start and end apart: 27, of which 13 were waited for; matrix products, arithmetic and copies ran while one was open for 24% of the time, Pallas kernels for 29%

profile of v3, /device:TPU:0, one launch (start us, length us, event | category | flops | bytes accessed | tf_op | source)
XLA Modules:
  0.0 417.1 jit_solution(11312365667364222499)
XLA Ops:
  7.2 7.9 %prep.1 = (s32[8,784]{1,0:T(8,128)}, s32[784,128]{1,0:T(8,128)}, bf16[8,208,768]{2,1,0:T(8,128)(2,1)}) custom-call(s32[2,784]{1,0:T(2,128)} %bitcast.99, s32[1,784]{1,0:T(1,128)} %refs_1_.2, bf16[784,768]{1,0:T(8,128)(2,1)} %refs_6_.4), custom_call_target="tpu_custom_call" | custom-call | flops 4000000000 | bytes 6000000 | tf_op jit(solution)/shard_map/prep/pallas_call | solution.py:74
  15.0 5.3 %all-to-all-start.1 = ((bf16[8,208,768]{2,1,0:T(8,128)(2,1)}), bf16[8,208,768]{2,1,0:T(8,128)(2,1)S(1)}, u32[]{:S(2)}, u32[]{:S(2)}) async-start(bf16[8,208,768]{2,1,0:T(8,128)(2,1)} %get-tuple-element.41), calls=%async_computation.1 | async-start | bytes 5111808 | tf_op jit(solution)/shard_map/all_to_all | solution.py:773
  23.4 41.2 %attend.1 = (bf16[3,784,768]{2,1,0:T(8,128)(2,1)}, bf16[784,768]{1,0:T(8,128)(2,1)}, f32[16,784]{1,0:T(8,128)}, bf16[784,768]{1,0:T(8,128)(2,1)}, f32[784,768]{1...) custom-call(s32[1]{0:T(128)S(6)} %copy.45.refs_0_, ...), custom_call_target="tpu_custom_call" | custom-call | flops 10000000000 | bytes 20000000 | tf_op jit(solution)/shard_map/attend/pallas_call | solution.py:74
  64.7 4.4 %all-to-all-start = ((bf16[8,208,768]{2,1,0:T(8,128)(2,1)}), bf16[8,208,768]{2,1,0:T(8,128)(2,1)}, u32[]{:S(2)}, u32[]{:S(2)}) async-start(bf16[8,208,768]{2,1,0:T(8,128)(2,1)} %get-tuple-element.40), calls=%async_computation | async-start | bytes 5111808 | tf_op jit(solution)/shard_map/all_to_all | solution.py:840
  69.6 12.8 %convolution_convert_fusion = bf16[1664,3072]{1,0:T(8,128)(2,1)} fusion(bf16[1664,768]{1,0:T(8,128)(2,1)S(1)} %bitcast.93, bf16[1,3072,768]{2,1,0:T(8,128)(2,1)} %param.26), kind=kOutput, calls=%fused_computation | convolution fusion | flops 7856848896 | bytes 17498112 | tf_op jit(solution)/shard_map/dot_general | solution.py:42
  82.4 18.2 %all-to-all-done.refs_0_ = bf16[8,208,768]{2,1,0:T(8,128)(2,1)} async-done(((bf16[8,208,768]{2,1,0:T(8,128)(2,1)}), bf16[8,208,768]{2,1,0:T(8,128)(2,1)}, u32[]{:S(2)}, u32[]{:S(2)}) %all-to-all-start) | async-done | bytes 2555936 | tf_op jit(solution)/shard_map/all_to_all | solution.py:840
  100.6 51.7 %expert.1 = (bf16[8,208,3072]{2,1,0:T(8,128)(2,1)}, bf16[8,208,3072]{2,1,0:T(8,128)(2,1)}, bf16[8,208,768]{2,1,0:T(8,128)(2,1)}, f32[8,8,256]{2,1,0:T(8,128)}, f32[8,3072]{1,0:T(8,128)}, /*index=5*/f32[8,768]{1,0:T(8,128)}) custom-call(bf16[8,208,768]{2,1,0:T(8,128)(2,1)} %all-to-all-done.refs_0_, bf16[8,208,768]{2,1,0:T(8,128)(2,1)} %copy-done.10, ...), custom_call_target="tpu_custom_call" | custom-call | flops 8000000000 | bytes 40000000 | tf_op jit(solution)/shard_map/expert/pallas_call | solution.py:74
  152.3 13.7 %bitcast_convert_fusion.refs_1_.refs_10_ = bf16[768,3072]{1,0:T(8,128)(2,1)} fusion(bf16[8,208,768]{2,1,0:T(8,128)(2,1)} %all-to-all-done.refs_0_, bf16[8,208,3072]{2,1,0:T(8,128)(2,1)} %get-tuple-element.44), kind=kOutput, calls=%fused_computation.1 | convolution fusion | flops 7854096384 | bytes 17498112 | tf_op jit(solution)/shard_map/dot_general | solution.py:46
  167.0 13.3 %fusion.1.refs_2_ = bf16[8,208,768]{2,1,0:T(8,128)(2,1)} fusion(bf16[8,1,256]{2,1,0:T(2,128)(2,1)S(1)} %get-tuple-element.109, bf16[8,1,256]{2,1,0:T(2,128)(2,1)S(1)} %get-tuple-element.108, bf16[8,208,3072]{2,1,0:T(8,128)(2,1)} %bitcast.87, bf16[1,768,3072]{2,1,0:T(8,128)(2,1)} %param.24, pred[208]{0:T(512)(128)(4,1)S(1)} %iota_compare_fusion.4), kind=kOutput, calls=%fused_computation.4 | convolution fusion | flops 7867072512 | bytes 17506512 | tf_op jit(solution)/shard_map/dot_general | solution.py:42
  180.3 3.6 all-to-all-start.3
  184.1 13.8 %convolution_convert_fusion.1.refs_1_.refs_11_ = bf16[3072,768]{1,0:T(8,128)(2,1)} fusion(bf16[1664,3072]{1,0:T(8,128)(2,1)} %bitcast.82, bf16[1664,768]{1,0:T(8,128)(2,1)} %hold.9), kind=kOutput, calls=%fused_computation.7 | convolution fusion | flops 7854096384 | bytes 17498112 | tf_op jit(solution)/shard_map/dot_general | solution.py:46
  197.9 12.7 %produce.1.refs_12_ = bf16[1664,768]{1,0:T(8,128)(2,1)} custom-call(bf16[1664,3072]{1,0:T(8,128)(2,1)} %hold.10.refs_0_, bf16[3072,768]{1,0:T(8,128)(2,1)} %bitcast.89, f32[1,768]{1,0:T(1,128)} %refs_2_.6), custom_call_target="tpu_custom_call" | custom-call | flops 1 | bytes 1 | tf_op jit(solution)/shard_map/produce/pallas_call | solution.py:74
  210.6 4.7 %all-to-all-done.3.refs_9_ = bf16[8,208,768]{2,1,0:T(8,128)(2,1)S(1)} async-done(((bf16[8,208,768]{2,1,0:T(8,128)(2,1)}), bf16[8,208,768]{2,1,0:T(8,128)(2,1)S(1)}, u32[]{:S(2)}, u32[]{:S(2)}) %all-to-all-start.3) | async-done | bytes 2555936 | tf_op jit(solution)/shard_map/all_to_all | solution.py:896
  216.8 3.6 all-to-all-start.2
  220.4 13.4 %row_grad.1 = (f32[784,768]{1,0:T(8,128)}, bf16[784,768]{1,0:T(8,128)(2,1)}, f32[8,768]{1,0:T(8,128)}, f32[8,768]{1,0:T(8,128)}) custom-call(s32[784,128]{1,0:T(8,128)} %get-tuple-element.36.refs_0_, s32[8,784]{1,0:T(8,128)} %get-tuple-element.37.refs_12_.refs_1_, s32[2,784]{1,0:T(2,128)} %bitcast.101, f32[8,784]{1,0:T(8,128)} %get-tuple-element.38.refs_3_, ...), custom_call_target="tpu_custom_call" | custom-call | flops 1 | bytes 1 | tf_op jit(solution)/shard_map/row_grad/pallas_call | solution.py:74
  233.9 4.1 convolution_convert_fusion.5.refs_6_
  238.0 11.6 %attend_back_a.1.refs_0_ = bf16[784,768]{1,0:T(8,128)(2,1)} custom-call(s32[1]{0:T(128)S(6)} %copy.45.refs_0_, bf16[784,768]{1,0:T(8,128)(2,1)} %get-tuple-element.48.refs_1_, bf16[768,768]{1,0:T(8,128)(2,1)} %refs_2_.9, bf16[3,784,768]{2,1,0:T(8,128)(2,1)} %get-tuple-element.49.refs_3_, bf16[784,768]{1,0:T(8,128)(2,1)} %get-tuple-element.50.refs_4_, ...), custom_call_target="tpu_custom_call" | custom-call | flops 8000000000 | bytes 6000000 | tf_op jit(solution)/shard_map/attend_back_a/pallas_call | solution.py:74
  249.6 4.8 %broadcast_select_fusion.2 = (bf16[768,768]{1,0:T(8,128)(2,1)}, bf16[768,768]{1,0:T(8,128)(2,1)}) fusion(bf16[768,768]{1,0:T(8,128)(2,1)} %convolution_convert_fusion.5.refs_6_, pred[]{:T(512)S(6)} %eq.27, bf16[784,768]{1,0:T(8,128)(2,1)} %get-tuple-element.46, bf16[784,768]{1,0:T(8,128)(2,1)} %attend_back_a.1.refs_0_), kind=kOutput, calls=%fused_computation.27 | convolution fusion | flops 926023680 | bytes 5947393 | tf_op jit(solution)/shard_map/dot_general | solution.py:46
  257.4 11.4 %attend_back_b.1.refs_1_ = bf16[784,768]{1,0:T(8,128)(2,1)} custom-call(s32[1]{0:T(128)S(6)} %copy.45.refs_0_, bf16[784,768]{1,0:T(8,128)(2,1)} %get-tuple-element.48.refs_1_, bf16[768,768]{1,0:T(8,128)(2,1)} %refs_2_.9, bf16[3,784,768]{2,1,0:T(8,128)(2,1)} %get-tuple-element.49.refs_3_, bf16[784,768]{1,0:T(8,128)(2,1)} %get-tuple-element.50.refs_4_, ...), custom_call_target="tpu_custom_call" | custom-call | flops 8000000000 | bytes 6000000 | tf_op jit(solution)/shard_map/attend_back_b/pallas_call | solution.py:74
  268.8 4.4 %convolution_convert_fusion.3.refs_7_ = bf16[768,768]{1,0:T(8,128)(2,1)} fusion(bf16[784,768]{1,0:T(8,128)(2,1)} %get-tuple-element.46, bf16[784,768]{1,0:T(8,128)(2,1)} %attend_back_b.1.refs_1_), kind=kOutput, calls=%fused_computation.13 | convolution fusion | flops 925433856 | bytes 3588096 | tf_op jit(solution)/shard_map/dot_general | solution.py:46
  273.2 2.8 add_convert_fusion.1.refs_6_
  276.0 11.7 %attend_back_c.1.refs_2_ = bf16[784,768]{1,0:T(8,128)(2,1)} custom-call(s32[1]{0:T(128)S(6)} %copy.45.refs_0_, bf16[784,768]{1,0:T(8,128)(2,1)} %get-tuple-element.48.refs_1_, bf16[768,768]{1,0:T(8,128)(2,1)} %refs_2_.9, bf16[3,784,768]{2,1,0:T(8,128)(2,1)} %get-tuple-element.49.refs_3_, bf16[784,768]{1,0:T(8,128)(2,1)} %get-tuple-element.50.refs_4_, ...), custom_call_target="tpu_custom_call" | custom-call | flops 8000000000 | bytes 6000000 | tf_op jit(solution)/shard_map/attend_back_c/pallas_call | solution.py:74
  287.6 4.9 %broadcast_select_fusion.1 = (bf16[768,768]{1,0:T(8,128)(2,1)}, bf16[768,768]{1,0:T(8,128)(2,1)}) fusion(bf16[768,768]{1,0:T(8,128)(2,1)} %convolution_convert_fusion.3.refs_7_, pred[]{:T(512)S(6)} %eq.27, bf16[784,768]{1,0:T(8,128)(2,1)} %get-tuple-element.46, bf16[784,768]{1,0:T(8,128)(2,1)} %attend_back_c.1.refs_2_), kind=kOutput, calls=%fused_computation.26 | convolution fusion | flops 926613504 | bytes 5947393 | tf_op jit(solution)/shard_map/dot_general | solution.py:46
  293.6 2.4 collective-permute-start.2
  297.6 2.6 pad_maximum_fusion
  301.7 10.6 %final.1 = (bf16[784,768]{1,0:T(8,128)(2,1)}, f32[8,768]{1,0:T(8,128)}) custom-call(bf16[784,768]{1,0:T(8,128)(2,1)} %attend_back_a.1.refs_0_, bf16[784,768]{1,0:T(8,128)(2,1)} %attend_back_b.1.refs_1_, bf16[784,768]{1,0:T(8,128)(2,1)} %attend_back_c.1.refs_2_, bf16[768,768]{1,0:T(8,128)(2,1)} %get-tuple-element.114.refs_3_, ...), custom_call_target="tpu_custom_call" | custom-call | flops 3000000000 | bytes 14000000 | tf_op jit(solution)/shard_map/final/pallas_call | solution.py:74
  316.6 1.6 add_convert_fusion.refs_6_
  320.2 4.0 convert_bitcast_fusion.1
  324.2 9.3 %combine.1.refs_1_ = bf16[784,768]{1,0:T(8,128)(2,1)} custom-call(s32[784,128]{1,0:T(8,128)} %get-tuple-element.36.refs_0_, s32[8,784]{1,0:T(8,128)} %get-tuple-element.37.refs_12_.refs_1_, s32[2,784]{1,0:T(2,128)} %bitcast.102, f32[8,784]{1,0:T(8,128)} %get-tuple-element.38.refs_3_, f32[784,768]{1,0:T(8,128)} %get-tuple-element.39.refs_5_.refs_4_, ...), custom_call_target="tpu_custom_call" | custom-call | flops 2000000000 | bytes 8000000 | tf_op jit(solution)/shard_map/combine/pallas_call | solution.py:74
  333.5 4.1 collective-permute-done.3
  341.3 1.7 collective-permute-start.9
  343.0 3.8 convert_bitcast_fusion
  347.1 2.2 collective-permute-start.10
  350.2 2.6 collective-permute-done.10
  352.8 2.5 collective-permute-start.11
  355.5 2.1 collective-permute-start.6
  357.6 2.8 collective-permute-done.11
  360.4 2.4 collective-permute-done.6
  363.4 2.3 collective-permute-start.12
  365.7 3.0 collective-permute-done.16
  370.6 1.7 collective-permute-start.13
  372.3 1.7 collective-permute-done.17
  374.1 1.8 collective-permute-start.18
  375.8 2.6 collective-permute-done.13
  379.4 3.6 collective-permute-done.18
  383.8 9.7 %collective-permute-done.14 = bf16[384,768]{1,0:T(8,128)(2,1)S(1)} collective-permute-done((bf16[384,768]{1,0:T(8,128)(2,1)S(1)}, bf16[384,768]{1,0:T(8,128)(2,1)S(1)}, u32[]{:S(2)}, u32[]{:S(2)}) %collective-permute-start.14) | collective-permute-done | bytes 589856 | tf_op jit(solution)/shard_map/ppermute | solution.py:664
  402.3 1.7 select_convert_fusion
  404.1 5.7 %place_qkv.1 = f32[768,2304]{1,0:T(8,128)} custom-call(s32[1]{0:T(128)} %bitcast.28.refs_0_, bf16[768,768]{1,0:T(8,128)(2,1)} %hold.15.refs_1_, bf16[768,768]{1,0:T(8,128)(2,1)} %copy-done.5, bf16[768,768]{1,0:T(8,128)(2,1)} %copy-done.6, bf16[768,768]{1,0:T(8,128)(2,1)} %collective-permute-done.20.refs_4_), custom_call_target="tpu_custom_call" | custom-call | flops 1000000 | bytes 11796480 | tf_op jit(solution)/shard_map/place_qkv/pallas_call | solution.py:74
  (169 shorter events, 36.7 us)
Async XLA Ops:
  15.0 6.0 %copy-start.22 = (f32[768]{0:T(1024)S(1)}, f32[768]{0:T(1024)}, u32[]{:S(2)}) copy-start(f32[768]{0:T(1024)} %param.17) | copy-start | bytes 9220
  15.0 6.6 %copy-start.23 = (f32[768]{0:T(1024)S(1)}, f32[768]{0:T(1024)}, u32[]{:S(2)}) copy-start(f32[768]{0:T(1024)} %param.18) | copy-start | bytes 9220
  15.0 7.2 %copy-start.24 = (f32[768]{0:T(1024)S(1)}, f32[768]{0:T(1024)}, u32[]{:S(2)}) copy-start(f32[768]{0:T(1024)} %param.21) | copy-start | bytes 9220
  15.0 7.8 %copy-start.25 = (f32[768]{0:T(1024)S(1)}, f32[768]{0:T(1024)}, u32[]{:S(2)}) copy-start(f32[768]{0:T(1024)} %param.22) | copy-start | bytes 9220
  15.0 49.6 %all-to-all-start.1 = ((bf16[8,208,768]{2,1,0:T(8,128)(2,1)}), bf16[8,208,768]{2,1,0:T(8,128)(2,1)S(1)}, u32[]{:S(2)}, u32[]{:S(2)}) async-start(bf16[8,208,768]{2,1,0:T(8,128)(2,1)} %get-tuple-element.41), calls=%async_computation.1 | async-start | bytes 5111808 | tf_op jit(solution)/shard_map/all_to_all | solution.py:773
  64.7 4.9 %copy-start.10 = (bf16[8,208,768]{2,1,0:T(8,128)(2,1)}, bf16[8,208,768]{2,1,0:T(8,128)(2,1)S(1)}, u32[]{:S(2)}) copy-start(bf16[8,208,768]{2,1,0:T(8,128)(2,1)S(1)} %all-to-all-done.1.refs_1_) | copy-start | bytes 7667716
  64.7 36.0 %all-to-all-start = ((bf16[8,208,768]{2,1,0:T(8,128)(2,1)}), bf16[8,208,768]{2,1,0:T(8,128)(2,1)}, u32[]{:S(2)}, u32[]{:S(2)}) async-start(bf16[8,208,768]{2,1,0:T(8,128)(2,1)} %get-tuple-element.40), calls=%async_computation | async-start | bytes 5111808 | tf_op jit(solution)/shard_map/all_to_all | solution.py:840
  69.1 251.1 %reduce-scatter.3.cloned.1.call-start = ((), (), s32[]{:S(2)}) async-start(), calls=%async_computation.6 | async-start | bytes 5898240 | tf_op jit(solution)/shard_map/reduce_scatter | solution.py:891
  180.3 35.1 %all-to-all-start.3 = ((bf16[8,208,768]{2,1,0:T(8,128)(2,1)}), bf16[8,208,768]{2,1,0:T(8,128)(2,1)S(1)}, u32[]{:S(2)}, u32[]{:S(2)}) async-start(bf16[8,208,768]{2,1,0:T(8,128)(2,1)} %fusion.1.refs_2_), calls=%async_computation.3 | async-start | bytes 5111808 | tf_op jit(solution)/shard_map/all_to_all | solution.py:896
  183.9 159.2 %reduce-scatter.5.cloned.1.call-start = ((), (), s32[]{:S(2)}) async-start(), calls=%async_computation.7 | async-start | bytes 5898240 | tf_op jit(solution)/shard_map/reduce_scatter | solution.py:900
  216.8 39.2 %all-to-all-start.2 = ((bf16[8,208,768]{2,1,0:T(8,128)(2,1)}), bf16[8,208,768]{2,1,0:T(8,128)(2,1)S(1)}, u32[]{:S(2)}, u32[]{:S(2)}) async-start(bf16[8,208,768]{2,1,0:T(8,128)(2,1)} %bitcast.84), calls=%async_computation.2 | async-start | bytes 5111808 | tf_op jit(solution)/shard_map/all_to_all | solution.py:916
  249.6 4.8 %copy-start.9 = (bf16[768,2304]{1,0:T(8,128)(2,1)S(1)}, bf16[768,2304]{1,0:T(8,128)(2,1)}, u32[]{:S(2)}) copy-start(bf16[768,2304]{1,0:T(8,128)(2,1)} %refs_6_.3) | copy-start | bytes 10616836
  254.4 18.8 %collective-permute-start = (bf16[768,768]{1,0:T(8,128)(2,1)}, bf16[768,768]{1,0:T(8,128)(2,1)}, u32[]{:S(2)}, u32[]{:S(2)}) collective-permute-start(bf16[768,768]{1,0:T(8,128)(2,1)} %get-tuple-element.112.refs_6_), channel_id=1, source_target_pairs={{0,1},{1,0},{2,3},{3,2},{4,5},{5,4},{6,7},{7,6},{8,9},{9,8},{10,11... | collective-permute-start | bytes 3538952 | tf_op jit(solution)/shard_map/ppermute | solution.py:664
  268.8 4.4 %copy-start.17 = (bf16[768,768]{1,0:T(8,128)(2,1)S(1)}, bf16[768,768]{1,0:T(8,128)(2,1)}, u32[]{:S(2)}) copy-start(bf16[768,768]{1,0:T(8,128)(2,1)} %convolution_convert_fusion.5.refs_6_) | copy-start | bytes 3538948
  268.8 4.4 %copy-start.18 = (bf16[768,768]{1,0:T(8,128)(2,1)S(1)}, bf16[768,768]{1,0:T(8,128)(2,1)}, u32[]{:S(2)}) copy-start(bf16[768,768]{1,0:T(8,128)(2,1)} %get-tuple-element.113) | copy-start | bytes 3538948
  287.6 5.0 %copy-start.7 = (bf16[768,768]{1,0:T(8,128)(2,1)S(1)}, bf16[768,768]{1,0:T(8,128)(2,1)}, u32[]{:S(2)}) copy-start(bf16[768,768]{1,0:T(8,128)(2,1)} %add_convert_fusion.1.refs_6_) | copy-start | bytes 3538948
  292.6 3.4 copy-start.14
  292.6 3.4 copy-start.15
  292.6 3.4 copy-start.16
  292.6 24.0 %collective-permute-start.1 = (bf16[768,768]{1,0:T(8,128)(2,1)}, bf16[768,768]{1,0:T(8,128)(2,1)}, u32[]{:S(2)}, u32[]{:S(2)}) collective-permute-start(bf16[768,768]{1,0:T(8,128)(2,1)} %get-tuple-element.73.refs_9_), channel_id=1, source_target_pairs={{0,1},{1,0},{2,3},{3,2},{4,5},{5,4},{6,7},{7,6},{8,9},{9,8},{10,11... | collective-permute-start | bytes 3538952 | tf_op jit(solution)/shard_map/ppermute | solution.py:664
  293.6 19.6 %collective-permute-start.2 = (bf16[384,768]{1,0:T(8,128)(2,1)}, bf16[384,768]{1,0:T(8,128)(2,1)}, u32[]{:S(2)}, u32[]{:S(2)}) collective-permute-start(bf16[384,768]{1,0:T(8,128)(2,1)} %dynamic-slice_bitcast_fusion.2), channel_id=1, source_target_pairs={{0,2},{1,3},{2,0},{3,1},{4,6},{5,7},{6,4},{7,5},{8,10},{9,11},{10,... | collective-permute-start | bytes 1769480 | tf_op jit(solution)/shard_map/ppermute | solution.py:664
  297.6 3.3 copy-start.21
  313.1 3.4 copy-start.8
  314.5 3.7 copy-start.4
  315.3 24.9 %collective-permute-start.8 = (bf16[192,768]{1,0:T(8,128)(2,1)S(1)}, bf16[192,768]{1,0:T(8,128)(2,1)S(1)}, u32[]{:S(2)}, u32[]{:S(2)}) collective-permute-start(bf16[192,768]{1,0:T(8,128)(2,1)S(1)} %get-tuple-element.89), channel_id=1, source_target_pairs={{0,4},{1,5},{2,6},{3,7},{4,0},{5,1},{6,2},{7,3},{8,12},{9,13},{10,... | collective-permute-start | bytes 884744 | tf_op jit(solution)/shard_map/ppermute | solution.py:664
  319.4 18.2 %collective-permute-start.3 = (bf16[400,768]{1,0:T(8,128)(2,1)S(1)}, bf16[400,768]{1,0:T(8,128)(2,1)S(1)}, u32[]{:S(2)}, u32[]{:S(2)}) collective-permute-start(bf16[400,768]{1,0:T(8,128)(2,1)S(1)} %get-tuple-element.111), channel_id=1, source_target_pairs={{0,4},{1,5},{2,6},{3,7},{4,0},{5,1},{6,2},{7,3},{8,12},{9,13},{10,... | collective-permute-start | bytes 1843208 | tf_op jit(solution)/shard_map/ppermute | solution.py:664
  339.0 10.3 %collective-permute-start.4 = (bf16[208,768]{1,0:T(8,128)(2,1)S(1)}, bf16[208,768]{1,0:T(8,128)(2,1)S(1)}, u32[]{:S(2)}, u32[]{:S(2)}) collective-permute-start(bf16[208,768]{1,0:T(8,128)(2,1)S(1)} %pad_maximum_fusion.9), channel_id=1, source_target_pairs={{0,2},{1,3},{2,0},{3,1},{4,6},{5,7},{6,4},{7,5},{8,10},{9,11},{10,... | collective-permute-start | bytes 958472 | tf_op jit(solution)/shard_map/ppermute | solution.py:664
  341.3 5.7 %collective-permute-start.9 = (bf16[112,768]{1,0:T(8,128)(2,1)S(1)}, bf16[112,768]{1,0:T(8,128)(2,1)S(1)}, u32[]{:S(2)}, u32[]{:S(2)}) collective-permute-start(bf16[112,768]{1,0:T(8,128)(2,1)S(1)} %pad_maximum_fusion.15), channel_id=1, source_target_pairs={{0,8},{8,0},{16,24},{24,16},{1,9},{9,1},{17,25},{25,17},{2,10},{10... | collective-permute-start | bytes 516104 | tf_op jit(solution)/shard_map/ppermute | solution.py:664
  347.1 5.7 %collective-permute-start.10 = (bf16[64,768]{1,0:T(8,128)(2,1)S(1)}, bf16[64,768]{1,0:T(8,128)(2,1)S(1)}, u32[]{:S(2)}, u32[]{:S(2)}) collective-permute-start(bf16[64,768]{1,0:T(8,128)(2,1)S(1)} %pad_maximum_fusion.21), channel_id=1, source_target_pairs={{0,16},{8,24},{16,0},{24,8},{1,17},{9,25},{17,1},{25,9},{2,18},{10... | collective-permute-start | bytes 294920 | tf_op jit(solution)/shard_map/ppermute | solution.py:664
  349.5 5.9 %collective-permute-start.5 = (bf16[112,768]{1,0:T(8,128)(2,1)S(1)}, bf16[112,768]{1,0:T(8,128)(2,1)S(1)}, u32[]{:S(2)}, u32[]{:S(2)}) collective-permute-start(bf16[112,768]{1,0:T(8,128)(2,1)S(1)} %pad_maximum_fusion.13), channel_id=1, source_target_pairs={{0,8},{8,0},{16,24},{24,16},{1,9},{9,1},{17,25},{25,17},{2,10},{10... | collective-permute-start | bytes 516104 | tf_op jit(solution)/shard_map/ppermute | solution.py:664
  352.8 7.5 %collective-permute-start.11 = (bf16[48,768]{1,0:T(8,128)(2,1)S(1)}, bf16[48,768]{1,0:T(8,128)(2,1)S(1)}, u32[]{:S(2)}, u32[]{:S(2)}) collective-permute-start(bf16[48,768]{1,0:T(8,128)(2,1)S(1)} %slice.151), channel_id=1, source_target_pairs={{0,16},{8,24},{16,0},{24,8},{1,17},{9,25},{17,1},{25,9},{2,18},{10... | collective-permute-start | bytes 221192 | tf_op jit(solution)/shard_map/ppermute | solution.py:664
  355.5 7.3 %collective-permute-start.6 = (bf16[64,768]{1,0:T(8,128)(2,1)S(1)}, bf16[64,768]{1,0:T(8,128)(2,1)S(1)}, u32[]{:S(2)}, u32[]{:S(2)}) collective-permute-start(bf16[64,768]{1,0:T(8,128)(2,1)S(1)} %pad_maximum_fusion.19), channel_id=1, source_target_pairs={{0,16},{8,24},{16,0},{24,8},{1,17},{9,25},{17,1},{25,9},{2,18},{10... | collective-permute-start | bytes 294920 | tf_op jit(solution)/shard_map/ppermute | solution.py:664
  362.8 6.3 %copy-start.19 = (bf16[64,768]{1,0:T(8,128)(2,1)}, bf16[64,768]{1,0:T(8,128)(2,1)S(1)}, u32[]{:S(2)}) copy-start(bf16[64,768]{1,0:T(8,128)(2,1)S(1)} %add_convert_fusion.8) | copy-start | bytes 294916
  362.8 5.9 %collective-permute-start.16 = (bf16[48,768]{1,0:T(8,128)(2,1)S(1)}, bf16[48,768]{1,0:T(8,128)(2,1)S(1)}, u32[]{:S(2)}, u32[]{:S(2)}) collective-permute-start(bf16[48,768]{1,0:T(8,128)(2,1)S(1)} %slice.152), channel_id=1, source_target_pairs={{0,16},{8,24},{16,0},{24,8},{1,17},{9,25},{17,1},{25,9},{2,18},{10... | collective-permute-start | bytes 221192 | tf_op jit(solution)/shard_map/ppermute | solution.py:664
  363.4 7.2 %collective-permute-start.12 = (bf16[96,768]{1,0:T(8,128)(2,1)S(1)}, bf16[96,768]{1,0:T(8,128)(2,1)S(1)}, u32[]{:S(2)}, u32[]{:S(2)}) collective-permute-start(bf16[96,768]{1,0:T(8,128)(2,1)S(1)} %pad_maximum_fusion.17), channel_id=1, source_target_pairs={{0,8},{8,0},{16,24},{24,16},{1,9},{9,1},{17,25},{25,17},{2,10},{10... | collective-permute-start | bytes 442376 | tf_op jit(solution)/shard_map/ppermute | solution.py:664
  368.8 5.2 %collective-permute-start.17 = (bf16[96,768]{1,0:T(8,128)(2,1)S(1)}, bf16[96,768]{1,0:T(8,128)(2,1)S(1)}, u32[]{:S(2)}, u32[]{:S(2)}) collective-permute-start(bf16[96,768]{1,0:T(8,128)(2,1)S(1)} %pad_maximum_fusion.18), channel_id=1, source_target_pairs={{0,8},{8,0},{16,24},{24,16},{1,9},{9,1},{17,25},{25,17},{2,10},{10... | collective-permute-start | bytes 442376 | tf_op jit(solution)/shard_map/ppermute | solution.py:664
  370.6 7.9 %collective-permute-start.13 = (bf16[192,768]{1,0:T(8,128)(2,1)S(1)}, bf16[192,768]{1,0:T(8,128)(2,1)S(1)}, u32[]{:S(2)}, u32[]{:S(2)}) collective-permute-start(bf16[192,768]{1,0:T(8,128)(2,1)S(1)} %pad_maximum_fusion.11), channel_id=1, source_target_pairs={{0,4},{1,5},{2,6},{3,7},{4,0},{5,1},{6,2},{7,3},{8,12},{9,13},{10,... | collective-permute-start | bytes 884744 | tf_op jit(solution)/shard_map/ppermute | solution.py:664
  374.1 9.0 %collective-permute-start.18 = (bf16[192,768]{1,0:T(8,128)(2,1)S(1)}, bf16[192,768]{1,0:T(8,128)(2,1)S(1)}, u32[]{:S(2)}, u32[]{:S(2)}) collective-permute-start(bf16[192,768]{1,0:T(8,128)(2,1)S(1)} %pad_maximum_fusion.12), channel_id=1, source_target_pairs={{0,2},{1,3},{2,0},{3,1},{4,6},{5,7},{6,4},{7,5},{8,10},{9,11},{10,... | collective-permute-start | bytes 884744 | tf_op jit(solution)/shard_map/ppermute | solution.py:664
  378.6 14.9 %collective-permute-start.14 = (bf16[384,768]{1,0:T(8,128)(2,1)S(1)}, bf16[384,768]{1,0:T(8,128)(2,1)S(1)}, u32[]{:S(2)}, u32[]{:S(2)}) collective-permute-start(bf16[384,768]{1,0:T(8,128)(2,1)S(1)} %pad_maximum_fusion.7), channel_id=1, source_target_pairs={{0,2},{1,3},{2,0},{3,1},{4,6},{5,7},{6,4},{7,5},{8,10},{9,11},{10,... | collective-permute-start | bytes 1769480 | tf_op jit(solution)/shard_map/ppermute | solution.py:664
  383.2 11.7 %collective-permute-start.19 = (bf16[384,768]{1,0:T(8,128)(2,1)S(1)}, bf16[384,768]{1,0:T(8,128)(2,1)S(1)}, u32[]{:S(2)}, u32[]{:S(2)}) collective-permute-start(bf16[384,768]{1,0:T(8,128)(2,1)S(1)} %pad_maximum_fusion.8), channel_id=1, source_target_pairs={{0,4},{1,5},{2,6},{3,7},{4,0},{5,1},{6,2},{7,3},{8,12},{9,13},{10,... | collective-permute-start | bytes 1769480 | tf_op jit(solution)/shard_map/ppermute | solution.py:664
  383.8 11.1 %copy-start.20 = (f32[16,768]{1,0:T(8,128)}, f32[16,768]{1,0:T(8,128)S(1)}, u32[]{:S(2)}) copy-start(f32[16,768]{1,0:T(8,128)S(1)} %slice_convert_fusion) | copy-start | bytes 147460
  394.8 7.5 %collective-permute-start.15 = (bf16[768,768]{1,0:T(8,128)(2,1)}, bf16[768,768]{1,0:T(8,128)(2,1)S(1)}, u32[]{:S(2)}, u32[]{:S(2)}) collective-permute-start(bf16[768,768]{1,0:T(8,128)(2,1)} %hold.15.refs_1_), channel_id=1, source_target_pairs={{0,1},{1,0},{2,3},{3,2},{4,5},{5,4},{6,7},{7,6},{8,9},{9,8},{10,11... | collective-permute-start | bytes 3538952 | tf_op jit(solution)/shard_map/ppermute | solution.py:664
  395.1 3.2 slice-start
  395.1 7.2 %copy-start = (bf16[768,768]{1,0:T(8,128)(2,1)S(1)}, bf16[768,768]{1,0:T(8,128)(2,1)}, u32[]{:S(2)}) copy-start(bf16[768,768]{1,0:T(8,128)(2,1)} %hold.15.refs_1_) | copy-start | bytes 3538948
  395.2 8.8 %copy-start.6 = (bf16[768,768]{1,0:T(8,128)(2,1)}, bf16[768,768]{1,0:T(8,128)(2,1)S(1)}, u32[]{:S(2)}) copy-start(bf16[768,768]{1,0:T(8,128)(2,1)S(1)} %pad_maximum_fusion.4.refs_3_) | copy-start | bytes 3538948
  395.2 8.9 %collective-permute-start.20 = (bf16[768,768]{1,0:T(8,128)(2,1)S(1)}, bf16[768,768]{1,0:T(8,128)(2,1)}, u32[]{:S(2)}, u32[]{:S(2)}) collective-permute-start(bf16[768,768]{1,0:T(8,128)(2,1)S(1)} %pad_maximum_fusion.4.refs_3_), channel_id=1, source_target_pairs={{0,1},{1,0},{2,3},{3,2},{4,5},{5,4},{6,7},{7,6},{8,9},{9,8},{10,11... | collective-permute-start | bytes 3538952 | tf_op jit(solution)/shard_map/ppermute | solution.py:664
  397.2 3.0 collective-permute-start.7
  402.3 1.8 copy-start.5
  (6 other events, 8.3 us)
Sparse Core Ops, SparseCore 0:
  166.1 84.6 reduce-scatter.2
  253.1 85.7 reduce-scatter.4

commit v4 on v3

--- a/solution.py
+++ b/solution.py
@@ -19,16 +19,15 @@
 SCALE = HEAD_DIM ** (-0.5)
 LOG2E = 1.4426950408889634
 INV_ROOT_TAU = 0.3989422804014327
-PHI_RATE = 0.3
+PHI_RATE = 0.36
 PHI_FIT = (
-    0.11962929778234231,
-    0.1207539739440115,
-    0.09991336806177473,
-    0.1285620774229096,
-    -0.05368457415108751,
-    0.20635459820469867,
-    -0.1572037608415104,
-    0.03567494667893269,
+    0.14371304535439455,
+    0.14177245494035942,
+    0.1397192591115954,
+    0.026549327576509053,
+    0.18095403137785818,
+    -0.17976471959279186,
+    0.047056297922502474,
 )
 F32 = jnp.float32
 BF16 = jnp.bfloat16
@@ -195,14 +194,11 @@
     cap_pad,
     kind_ref,
     x_ref,
-    gain_one_ref,
-    shift_one_ref,
+    gains_ref,
     wq_ref,
     wk_ref,
     wv_ref,
     wo_ref,
-    gain_two_ref,
-    shift_two_ref,
     router_ref,
     routes_ref,
     slot_ref,
@@ -229,7 +225,7 @@
         def rows(i, carry):
             spot = pl.ds(pl.multiple_of(i * chunk, 16), chunk)
             scaled, _ = norm_stats(x_ref[spot, :].astype(F32))
-            low_ref[spot, :] = (scaled * gain_one_ref[...] + shift_one_ref[...]).astype(BF16)
+            low_ref[spot, :] = (scaled * gains_ref[0:1, :] + gains_ref[1:2, :]).astype(BF16)
             return carry
 
         lax.fori_loop(0, toks // chunk, rows, 0)
@@ -295,7 +291,7 @@
             residual = acc_ref[spot, :]
             residual_ref[spot, :] = residual
             scaled, _ = norm_stats(residual)
-            lowered_ref[spot, :] = (scaled * gain_two_ref[...] + shift_two_ref[...]).astype(BF16)
+            lowered_ref[spot, :] = (scaled * gains_ref[2:3, :] + gains_ref[3:4, :]).astype(BF16)
             return carry
 
         lax.fori_loop(0, toks // chunk, rows, 0)
@@ -344,7 +340,7 @@
 
 def phi_parts(v):
     a = jnp.abs(v)
-    bell = jnp.exp(-0.5 * (v * v))
+    bell = jnp.exp2((-0.5 * LOG2E) * (v * v))
     t = 1.0 / (1.0 + PHI_RATE * a)
     poly = PHI_FIT[-1] * t
     for part in PHI_FIT[-2::-1]:
@@ -368,6 +364,8 @@
     bback_ref,
     gate_scr,
     acc_scr,
+    even_ref,
+    odd_ref,
 ):
     step = pl.program_id(0)
     blocks, cap_pad, width = x_ref.shape
@@ -399,13 +397,13 @@
 
     bin_ref[...] = jnp.zeros_like(bin_ref)
 
-    def block(b, carry):
-        pre = dot_nn(x_ref[b], w_ref[...]) + bias_ref[...]
+    def work(b, pre_ref):
+        pre = pre_ref[...] + bias_ref[...]
         cdf, bell = phi_parts(pre)
-        hidden = (pre * cdf).astype(BF16)
-        hidden_ref[b] = hidden
+        hidden = pre * cdf
+        hidden_ref[b] = hidden.astype(BF16)
         z = z_ref[b].astype(F32)
-        part = hidden.astype(F32) * z
+        part = hidden * z
         total = acc_scr[b]
         for i in range(tile // 128):
             total = total + part[:, i * 128 : (i + 1) * 128]
@@ -415,9 +413,18 @@
         grad = (gate * z * slope).astype(BF16)
         grad_ref[b] = grad
         bin_ref[0:1, :] += jnp.sum(grad.astype(F32), axis=0, keepdims=True)
+
+    even_ref[...] = dot_nn(x_ref[0], w_ref[...])
+
+    def pair(i, carry):
+        b = 2 * i
+        odd_ref[...] = dot_nn(x_ref[b + 1], w_ref[...])
+        work(b, even_ref)
+        even_ref[...] = dot_nn(x_ref[jnp.minimum(b + 2, blocks - 1)], w_ref[...])
+        work(b + 1, odd_ref)
         return carry
 
-    lax.fori_loop(0, blocks, block, 0)
+    lax.fori_loop(0, blocks // 2, pair, 0)
 
     @pl.when(step == pl.num_programs(0) - 1)
     def _():
@@ -524,7 +531,7 @@
         scaled, inverse = norm_stats(residual_ref[spot, :])
         small_ref[0:1, :] += jnp.sum(grad * scaled, axis=0, keepdims=True)
         small_ref[1:2, :] += jnp.sum(grad, axis=0, keepdims=True)
-        total = cot_ref[spot, :].astype(F32) + norm_grad(grad, scaled, inverse, gain_ref[...])
+        total = cot_ref[spot, :].astype(F32) + norm_grad(grad, scaled, inverse, gain_ref[2:3, :])
         grad_ref[spot, :] = total
         low_ref[spot, :] = total.astype(BF16)
         return carry
@@ -617,7 +624,7 @@
         small_ref[0:1, :] += jnp.sum(grad * scaled, axis=0, keepdims=True)
         small_ref[1:2, :] += jnp.sum(grad, axis=0, keepdims=True)
         out_ref[spot, :] = (
-            up_ref[spot, :] + norm_grad(grad, scaled, inverse, gain_ref[...])
+            up_ref[spot, :] + norm_grad(grad, scaled, inverse, gain_ref[0:1, :])
         ).astype(BF16)
         return carry
 
@@ -772,7 +779,7 @@
     )(routes_row, priority, cotangent)
     up_in = lax.all_to_all(up_rows, "ex", split_axis=0, concat_axis=0, tiled=True)
 
-    gains = [a.reshape(1, width) for a in (gain_one, shift_one, gain_two, shift_two)]
+    gains = jnp.stack([gain_one, shift_one, gain_two, shift_two])
     col = lambda offset: pl.BlockSpec((width, LANES), lambda g: (0, offset * groups + g))
     smem = pl.BlockSpec(memory_space=pltpu.SMEM)
     per_group = lambda: pl.BlockSpec((1, toks, 3 * LANES), lambda g: (g, 0, 0))
@@ -791,14 +798,11 @@
         in_specs=[
             smem,
             whole((toks, width)),
-            whole((1, width)),
-            whole((1, width)),
+            whole((4, width)),
             col(0),
             col(1),
             col(2),
             pl.BlockSpec((LANES, width), lambda g: (g, 0)),
-            whole((1, width)),
-            whole((1, width)),
             whole((experts, width)),
             whole((2, toks)),
             whole((8, toks)),
@@ -825,14 +829,11 @@
     )(
         image_kind,
         tokens,
-        gains[0],
-        gains[1],
+        gains,
         w_qkv,
         w_qkv,
         w_qkv,
         w_out,
-        gains[2],
-        gains[3],
         router_row,
         routes_row,
         slots,
@@ -874,6 +875,8 @@
         scratch=[
             pltpu.VMEM((blocks, cap_pad, 128), F32),
             pltpu.VMEM((blocks, cap_pad, 128), F32),
+            pltpu.VMEM((cap_pad, tile), F32),
+            pltpu.VMEM((cap_pad, tile), F32),
         ],
         cost=(8e9, 40e6, 10e6),
         name="expert",
@@ -938,7 +941,7 @@
         lowered,
         residual,
         cotangent,
-        gains[2],
+        gains,
         router_row,
         grad_back,
     )
@@ -1006,7 +1009,7 @@
         cost=(3e9, 14e6, 0),
         name="final",
         after=[sums[1].value],
-    )(*packed_grads, *w_groups, tokens, gains[0], grad_residual)
+    )(*packed_grads, *w_groups, tokens, gains, grad_residual)
     ahead, last = sums
     small = jnp.concatenate([small_one[0:2], small_two[0:2], route_grad], axis=0)
     small_rows = small.shape[0]

time: 424 us -> 416 us (0.981)
  Pallas kernels: 187 us -> 180 us
    pallas_call x11, Pallas kernels: 187 us -> 180 us  [run(): pl.pallas_call(inner, in_specs=specs, compiler_params=pltpu.CompilerParam...]
  transfers between devices with their start and end apart: 27 -> 27, of which waited for: 13 -> 15; matrix products, arithmetic and copies ran while one was open for 24% -> 24% of each run, Pallas kernels for 29% -> 30%
where the time goes in v4:
time: 416 us; the launch traced here: 409 us
  Pallas kernels  180 us (43%)
  matrix products  71.7 us (17%)
  waiting for transfers between devices  55.1 us (13%)
  starting transfers between devices  42.8 us (10%)
  other arithmetic  28.9 us (7%)
  between operations  15.8 us (4%)
  local copies, waits for them, and re-layouts  14.3 us (3%)
    pallas_call x11, Pallas kernels, run(): pl.pallas_call(inner, in_specs=specs, compiler_params=pltpu.CompilerParam...  180 us
    dot_general x6, matrix products, dot_tn(): lax.dot_general(a, b, (((0,), (0,)), ((), ())), preferred_element_type=F32)  45.7 us
    ppermute x21, waiting for transfers between devices, send_xor(): return lax.ppermute(values, axis, [(j, j ^ distance) for j in range(size)])  32.1 us
    dot_general x2, matrix products, dot_nt(): lax.dot_general(a, b, (((1,), (1,)), ((), ())), preferred_element_type=F32)  26.1 us
    ppermute x21, starting transfers between devices, send_xor(): return lax.ppermute(values, axis, [(j, j ^ distance) for j in range(size)])  25.1 us
    all_to_all x1, waiting for transfers between devices, local(): lax.all_to_all(sent, 'ex', split_axis=0, concat_axis=0, tiled=True)  18.2 us
  transfers between devices with their start and end apart: 27, of which 15 were waited for; matrix products, arithmetic and copies ran while one was open for 24% of the time, Pallas kernels for 30%

profile of v4, /device:TPU:0, one launch (start us, length us, event | category | flops | bytes accessed | tf_op | source)
XLA Modules:
  0.0 408.6 jit_solution(13111691591072434969)
XLA Ops:
  7.2 7.9 %prep.1 = (s32[8,784]{1,0:T(8,128)}, s32[784,128]{1,0:T(8,128)}, bf16[8,208,768]{2,1,0:T(8,128)(2,1)}) custom-call(s32[2,784]{1,0:T(2,128)} %bitcast.99, s32[1,784]{1,0:T(1,128)} %refs_1_.2, bf16[784,768]{1,0:T(8,128)(2,1)} %refs_6_.4), custom_call_target="tpu_custom_call" | custom-call | flops 4000000000 | bytes 6000000 | tf_op jit(solution)/shard_map/prep/pallas_call | solution.py:73
  15.0 5.3 %all-to-all-start.1 = ((bf16[8,208,768]{2,1,0:T(8,128)(2,1)}), bf16[8,208,768]{2,1,0:T(8,128)(2,1)S(1)}, u32[]{:S(2)}, u32[]{:S(2)}) async-start(bf16[8,208,768]{2,1,0:T(8,128)(2,1)} %get-tuple-element.41), calls=%async_computation.1 | async-start | bytes 5111808 | tf_op jit(solution)/shard_map/all_to_all | solution.py:780
  21.8 41.2 %attend.1 = (bf16[3,784,768]{2,1,0:T(8,128)(2,1)}, bf16[784,768]{1,0:T(8,128)(2,1)}, f32[16,784]{1,0:T(8,128)}, bf16[784,768]{1,0:T(8,128)(2,1)}, f32[784,768]{1...) custom-call(s32[1]{0:T(128)S(6)} %copy.45.refs_0_, ...), custom_call_target="tpu_custom_call" | custom-call | flops 10000000000 | bytes 20000000 | tf_op jit(solution)/shard_map/attend/pallas_call | solution.py:73
  63.0 4.4 %all-to-all-start = ((bf16[8,208,768]{2,1,0:T(8,128)(2,1)}), bf16[8,208,768]{2,1,0:T(8,128)(2,1)}, u32[]{:S(2)}, u32[]{:S(2)}) async-start(bf16[8,208,768]{2,1,0:T(8,128)(2,1)} %get-tuple-element.40), calls=%async_computation | async-start | bytes 5111808 | tf_op jit(solution)/shard_map/all_to_all | solution.py:841
  67.9 12.8 %convolution_convert_fusion = bf16[1664,3072]{1,0:T(8,128)(2,1)} fusion(bf16[1664,768]{1,0:T(8,128)(2,1)S(1)} %bitcast.93, bf16[1,3072,768]{2,1,0:T(8,128)(2,1)} %param.26), kind=kOutput, calls=%fused_computation | convolution fusion | flops 7856848896 | bytes 17498112 | tf_op jit(solution)/shard_map/dot_general | solution.py:41
  80.7 18.2 %all-to-all-done.refs_0_ = bf16[8,208,768]{2,1,0:T(8,128)(2,1)} async-done(((bf16[8,208,768]{2,1,0:T(8,128)(2,1)}), bf16[8,208,768]{2,1,0:T(8,128)(2,1)}, u32[]{:S(2)}, u32[]{:S(2)}) %all-to-all-start) | async-done | bytes 2555936 | tf_op jit(solution)/shard_map/all_to_all | solution.py:841
  98.9 44.5 %expert.1 = (bf16[8,208,3072]{2,1,0:T(8,128)(2,1)}, bf16[8,208,3072]{2,1,0:T(8,128)(2,1)}, bf16[8,208,768]{2,1,0:T(8,128)(2,1)}, f32[8,8,256]{2,1,0:T(8,128)}, f32[8,3072]{1,0:T(8,128)}, /*index=5*/f32[8,768]{1,0:T(8,128)}) custom-call(bf16[8,208,768]{2,1,0:T(8,128)(2,1)} %all-to-all-done.refs_0_, bf16[8,208,768]{2,1,0:T(8,128)(2,1)} %copy-done.10, ...), custom_call_target="tpu_custom_call" | custom-call | flops 8000000000 | bytes 40000000 | tf_op jit(solution)/shard_map/expert/pallas_call | solution.py:73
  143.5 13.7 %bitcast_convert_fusion.refs_1_.refs_10_ = bf16[768,3072]{1,0:T(8,128)(2,1)} fusion(bf16[8,208,768]{2,1,0:T(8,128)(2,1)} %all-to-all-done.refs_0_, bf16[8,208,3072]{2,1,0:T(8,128)(2,1)} %get-tuple-element.44), kind=kOutput, calls=%fused_computation.1 | convolution fusion | flops 7854096384 | bytes 17498112 | tf_op jit(solution)/shard_map/dot_general | solution.py:45
  158.1 13.3 %fusion.1.refs_2_ = bf16[8,208,768]{2,1,0:T(8,128)(2,1)} fusion(bf16[8,1,256]{2,1,0:T(2,128)(2,1)S(1)} %get-tuple-element.109, bf16[8,1,256]{2,1,0:T(2,128)(2,1)S(1)} %get-tuple-element.108, bf16[8,208,3072]{2,1,0:T(8,128)(2,1)} %bitcast.87, bf16[1,768,3072]{2,1,0:T(8,128)(2,1)} %param.24, pred[208]{0:T(512)(128)(4,1)S(1)} %iota_compare_fusion.4), kind=kOutput, calls=%fused_computation.4 | convolution fusion | flops 7867072512 | bytes 17506512 | tf_op jit(solution)/shard_map/dot_general | solution.py:41
  171.4 3.6 all-to-all-start.3
  175.3 13.8 %convolution_convert_fusion.1.refs_1_.refs_11_ = bf16[3072,768]{1,0:T(8,128)(2,1)} fusion(bf16[1664,3072]{1,0:T(8,128)(2,1)} %bitcast.82, bf16[1664,768]{1,0:T(8,128)(2,1)} %hold.9), kind=kOutput, calls=%fused_computation.7 | convolution fusion | flops 7854096384 | bytes 17498112 | tf_op jit(solution)/shard_map/dot_general | solution.py:45
  189.1 12.7 %produce.1.refs_12_ = bf16[1664,768]{1,0:T(8,128)(2,1)} custom-call(bf16[1664,3072]{1,0:T(8,128)(2,1)} %hold.10.refs_0_, bf16[3072,768]{1,0:T(8,128)(2,1)} %bitcast.89, f32[1,768]{1,0:T(1,128)} %refs_2_.6), custom_call_target="tpu_custom_call" | custom-call | flops 1 | bytes 1 | tf_op jit(solution)/shard_map/produce/pallas_call | solution.py:73
  201.8 4.7 %all-to-all-done.3.refs_9_ = bf16[8,208,768]{2,1,0:T(8,128)(2,1)S(1)} async-done(((bf16[8,208,768]{2,1,0:T(8,128)(2,1)}), bf16[8,208,768]{2,1,0:T(8,128)(2,1)S(1)}, u32[]{:S(2)}, u32[]{:S(2)}) %all-to-all-start.3) | async-done | bytes 2555936 | tf_op jit(solution)/shard_map/all_to_all | solution.py:899
  207.9 3.6 all-to-all-start.2
  211.6 13.4 %row_grad.1 = (f32[784,768]{1,0:T(8,128)}, bf16[784,768]{1,0:T(8,128)(2,1)}, f32[8,768]{1,0:T(8,128)}, f32[8,768]{1,0:T(8,128)}) custom-call(s32[784,128]{1,0:T(8,128)} %get-tuple-element.36.refs_0_, s32[8,784]{1,0:T(8,128)} %get-tuple-element.37.refs_9_.refs_1_, s32[2,784]{1,0:T(2,128)} %bitcast.101, f32[8,784]{1,0:T(8,128)} %get-tuple-element.38.refs_3_, ...), custom_call_target="tpu_custom_call" | custom-call | flops 1 | bytes 1 | tf_op jit(solution)/shard_map/row_grad/pallas_call | solution.py:73
  225.0 4.1 %convolution_convert_fusion.5.refs_6_ = bf16[768,768]{1,0:T(8,128)(2,1)} fusion(bf16[784,768]{1,0:T(8,128)(2,1)} %get-tuple-element.50.refs_4_, bf16[784,768]{1,0:T(8,128)(2,1)} %get-tuple-element.48.refs_1_), kind=kOutput, calls=%fused_computation.15 | convolution fusion | flops 925433856 | bytes 3588096 | tf_op jit(solution)/shard_map/dot_general | solution.py:45
  229.1 11.6 %attend_back_a.1.refs_0_ = bf16[784,768]{1,0:T(8,128)(2,1)} custom-call(s32[1]{0:T(128)S(6)} %copy.45.refs_0_, bf16[784,768]{1,0:T(8,128)(2,1)} %get-tuple-element.48.refs_1_, bf16[768,768]{1,0:T(8,128)(2,1)} %refs_2_.9, bf16[3,784,768]{2,1,0:T(8,128)(2,1)} %get-tuple-element.49.refs_3_, bf16[784,768]{1,0:T(8,128)(2,1)} %get-tuple-element.50.refs_4_, ...), custom_call_target="tpu_custom_call" | custom-call | flops 8000000000 | bytes 6000000 | tf_op jit(solution)/shard_map/attend_back_a/pallas_call | solution.py:73
  240.8 4.8 %broadcast_select_fusion.2 = (bf16[768,768]{1,0:T(8,128)(2,1)}, bf16[768,768]{1,0:T(8,128)(2,1)}) fusion(bf16[768,768]{1,0:T(8,128)(2,1)} %convolution_convert_fusion.5.refs_6_, pred[]{:T(512)S(6)} %eq.27, bf16[784,768]{1,0:T(8,128)(2,1)} %get-tuple-element.46, bf16[784,768]{1,0:T(8,128)(2,1)} %attend_back_a.1.refs_0_), kind=kOutput, calls=%fused_computation.27 | convolution fusion | flops 926023680 | bytes 5947393 | tf_op jit(solution)/shard_map/dot_general | solution.py:45
  248.5 11.4 %attend_back_b.1.refs_1_ = bf16[784,768]{1,0:T(8,128)(2,1)} custom-call(s32[1]{0:T(128)S(6)} %copy.45.refs_0_, bf16[784,768]{1,0:T(8,128)(2,1)} %get-tuple-element.48.refs_1_, bf16[768,768]{1,0:T(8,128)(2,1)} %refs_2_.9, bf16[3,784,768]{2,1,0:T(8,128)(2,1)} %get-tuple-element.49.refs_3_, bf16[784,768]{1,0:T(8,128)(2,1)} %get-tuple-element.50.refs_4_, ...), custom_call_target="tpu_custom_call" | custom-call | flops 8000000000 | bytes 6000000 | tf_op jit(solution)/shard_map/attend_back_b/pallas_call | solution.py:73
  259.9 4.4 %convolution_convert_fusion.3.refs_7_ = bf16[768,768]{1,0:T(8,128)(2,1)} fusion(bf16[784,768]{1,0:T(8,128)(2,1)} %get-tuple-element.46, bf16[784,768]{1,0:T(8,128)(2,1)} %attend_back_b.1.refs_1_), kind=kOutput, calls=%fused_computation.13 | convolution fusion | flops 925433856 | bytes 3588096 | tf_op jit(solution)/shard_map/dot_general | solution.py:45
  264.3 2.8 add_convert_fusion.1.refs_6_
  267.1 11.7 %attend_back_c.1.refs_2_ = bf16[784,768]{1,0:T(8,128)(2,1)} custom-call(s32[1]{0:T(128)S(6)} %copy.45.refs_0_, bf16[784,768]{1,0:T(8,128)(2,1)} %get-tuple-element.48.refs_1_, bf16[768,768]{1,0:T(8,128)(2,1)} %refs_2_.9, bf16[3,784,768]{2,1,0:T(8,128)(2,1)} %get-tuple-element.49.refs_3_, bf16[784,768]{1,0:T(8,128)(2,1)} %get-tuple-element.50.refs_4_, ...), custom_call_target="tpu_custom_call" | custom-call | flops 8000000000 | bytes 6000000 | tf_op jit(solution)/shard_map/attend_back_c/pallas_call | solution.py:73
  278.8 4.9 %broadcast_select_fusion.1 = (bf16[768,768]{1,0:T(8,128)(2,1)}, bf16[768,768]{1,0:T(8,128)(2,1)}) fusion(bf16[768,768]{1,0:T(8,128)(2,1)} %convolution_convert_fusion.3.refs_7_, pred[]{:T(512)S(6)} %eq.27, bf16[784,768]{1,0:T(8,128)(2,1)} %get-tuple-element.46, bf16[784,768]{1,0:T(8,128)(2,1)} %attend_back_c.1.refs_2_), kind=kOutput, calls=%fused_computation.26 | convolution fusion | flops 926613504 | bytes 5947393 | tf_op jit(solution)/shard_map/dot_general | solution.py:45
  284.7 2.4 collective-permute-start.2
  288.8 2.6 pad_maximum_fusion
  292.9 10.7 %final.1 = (bf16[784,768]{1,0:T(8,128)(2,1)}, f32[8,768]{1,0:T(8,128)}) custom-call(bf16[784,768]{1,0:T(8,128)(2,1)} %attend_back_a.1.refs_0_, bf16[784,768]{1,0:T(8,128)(2,1)} %attend_back_b.1.refs_1_, bf16[784,768]{1,0:T(8,128)(2,1)} %attend_back_c.1.refs_2_, bf16[768,768]{1,0:T(8,128)(2,1)} %get-tuple-element.114.refs_3_, ...), custom_call_target="tpu_custom_call" | custom-call | flops 3000000000 | bytes 14000000 | tf_op jit(solution)/shard_map/final/pallas_call | solution.py:73
  307.8 1.6 add_convert_fusion.refs_6_
  311.4 4.0 convert_bitcast_fusion.1
  315.4 9.3 %combine.1.refs_1_ = bf16[784,768]{1,0:T(8,128)(2,1)} custom-call(s32[784,128]{1,0:T(8,128)} %get-tuple-element.36.refs_0_, s32[8,784]{1,0:T(8,128)} %get-tuple-element.37.refs_9_.refs_1_, s32[2,784]{1,0:T(2,128)} %bitcast.102, f32[8,784]{1,0:T(8,128)} %get-tuple-element.38.refs_3_, f32[784,768]{1,0:T(8,128)} %get-tuple-element.39.refs_5_.refs_4_, ...), custom_call_target="tpu_custom_call" | custom-call | flops 2000000000 | bytes 8000000 | tf_op jit(solution)/shard_map/combine/pallas_call | solution.py:73
  324.7 4.1 %collective-permute-done.3 = bf16[400,768]{1,0:T(8,128)(2,1)S(1)} collective-permute-done((bf16[400,768]{1,0:T(8,128)(2,1)S(1)}, bf16[400,768]{1,0:T(8,128)(2,1)S(1)}, u32[]{:S(2)}, u32[]{:S(2)}) %collective-permute-start.3) | collective-permute-done | bytes 614432 | tf_op jit(solution)/shard_map/ppermute | solution.py:671
  332.5 1.7 collective-permute-start.9
  334.3 3.8 convert_bitcast_fusion
  338.3 2.9 collective-permute-start.10
  341.4 1.7 collective-permute-start.5
  344.4 3.4 collective-permute-start.11
  348.5 3.7 collective-permute-done.11
  352.2 3.0 collective-permute-done.6
  355.4 2.6 collective-permute-start.12
  358.0 3.4 collective-permute-done.16
  362.9 1.9 collective-permute-start.13
  364.8 1.8 collective-permute-done.17
  369.9 1.9 collective-permute-start.14
  371.8 4.9 %collective-permute-done.18 = bf16[192,768]{1,0:T(8,128)(2,1)S(1)} collective-permute-done((bf16[192,768]{1,0:T(8,128)(2,1)S(1)}, bf16[192,768]{1,0:T(8,128)(2,1)S(1)}, u32[]{:S(2)}, u32[]{:S(2)}) %collective-permute-start.18) | collective-permute-done | bytes 294944 | tf_op jit(solution)/shard_map/ppermute | solution.py:671
  376.8 1.7 collective-permute-start.19
  378.5 6.5 %collective-permute-done.14 = bf16[384,768]{1,0:T(8,128)(2,1)S(1)} collective-permute-done((bf16[384,768]{1,0:T(8,128)(2,1)S(1)}, bf16[384,768]{1,0:T(8,128)(2,1)S(1)}, u32[]{:S(2)}, u32[]{:S(2)}) %collective-permute-start.14) | collective-permute-done | bytes 589856 | tf_op jit(solution)/shard_map/ppermute | solution.py:671
  387.2 1.8 slice_convert_fusion.1
  393.9 1.7 select_convert_fusion
  395.6 5.7 %place_qkv.1 = f32[768,2304]{1,0:T(8,128)} custom-call(s32[1]{0:T(128)} %bitcast.28.refs_0_, bf16[768,768]{1,0:T(8,128)(2,1)} %hold.15.refs_1_, bf16[768,768]{1,0:T(8,128)(2,1)} %copy-done.5, bf16[768,768]{1,0:T(8,128)(2,1)} %copy-done.6, bf16[768,768]{1,0:T(8,128)(2,1)} %collective-permute-done.20.refs_4_), custom_call_target="tpu_custom_call" | custom-call | flops 1000000 | bytes 11796480 | tf_op jit(solution)/shard_map/place_qkv/pallas_call | solution.py:73
  (170 shorter events, 35.3 us)
Async XLA Ops:
  15.0 6.0 %copy-start.22 = (f32[768]{0:T(1024)S(1)}, f32[768]{0:T(1024)}, u32[]{:S(2)}) copy-start(f32[768]{0:T(1024)} %param.22) | copy-start | bytes 9220
  15.0 6.0 %copy-start.23 = (f32[768]{0:T(1024)S(1)}, f32[768]{0:T(1024)}, u32[]{:S(2)}) copy-start(f32[768]{0:T(1024)} %param.21) | copy-start | bytes 9220
  15.0 6.1 %copy-start.24 = (f32[768]{0:T(1024)S(1)}, f32[768]{0:T(1024)}, u32[]{:S(2)}) copy-start(f32[768]{0:T(1024)} %param.18) | copy-start | bytes 9220
  15.0 6.1 %copy-start.25 = (f32[768]{0:T(1024)S(1)}, f32[768]{0:T(1024)}, u32[]{:S(2)}) copy-start(f32[768]{0:T(1024)} %param.17) | copy-start | bytes 9220
  15.0 47.9 %all-to-all-start.1 = ((bf16[8,208,768]{2,1,0:T(8,128)(2,1)}), bf16[8,208,768]{2,1,0:T(8,128)(2,1)S(1)}, u32[]{:S(2)}, u32[]{:S(2)}) async-start(bf16[8,208,768]{2,1,0:T(8,128)(2,1)} %get-tuple-element.41), calls=%async_computation.1 | async-start | bytes 5111808 | tf_op jit(solution)/shard_map/all_to_all | solution.py:780
  63.0 4.9 %copy-start.10 = (bf16[8,208,768]{2,1,0:T(8,128)(2,1)}, bf16[8,208,768]{2,1,0:T(8,128)(2,1)S(1)}, u32[]{:S(2)}) copy-start(bf16[8,208,768]{2,1,0:T(8,128)(2,1)S(1)} %all-to-all-done.1.refs_1_) | copy-start | bytes 7667716
  63.0 36.0 %all-to-all-start = ((bf16[8,208,768]{2,1,0:T(8,128)(2,1)}), bf16[8,208,768]{2,1,0:T(8,128)(2,1)}, u32[]{:S(2)}, u32[]{:S(2)}) async-start(bf16[8,208,768]{2,1,0:T(8,128)(2,1)} %get-tuple-element.40), calls=%async_computation | async-start | bytes 5111808 | tf_op jit(solution)/shard_map/all_to_all | solution.py:841
  67.4 244.0 %reduce-scatter.3.cloned.1.call-start = ((), (), s32[]{:S(2)}) async-start(), calls=%async_computation.6 | async-start | bytes 5898240 | tf_op jit(solution)/shard_map/reduce_scatter | solution.py:894
  171.4 35.1 %all-to-all-start.3 = ((bf16[8,208,768]{2,1,0:T(8,128)(2,1)}), bf16[8,208,768]{2,1,0:T(8,128)(2,1)S(1)}, u32[]{:S(2)}, u32[]{:S(2)}) async-start(bf16[8,208,768]{2,1,0:T(8,128)(2,1)} %fusion.1.refs_2_), calls=%async_computation.3 | async-start | bytes 5111808 | tf_op jit(solution)/shard_map/all_to_all | solution.py:899
  175.0 159.2 %reduce-scatter.5.cloned.1.call-start = ((), (), s32[]{:S(2)}) async-start(), calls=%async_computation.7 | async-start | bytes 5898240 | tf_op jit(solution)/shard_map/reduce_scatter | solution.py:903
  207.9 39.2 %all-to-all-start.2 = ((bf16[8,208,768]{2,1,0:T(8,128)(2,1)}), bf16[8,208,768]{2,1,0:T(8,128)(2,1)S(1)}, u32[]{:S(2)}, u32[]{:S(2)}) async-start(bf16[8,208,768]{2,1,0:T(8,128)(2,1)} %bitcast.84), calls=%async_computation.2 | async-start | bytes 5111808 | tf_op jit(solution)/shard_map/all_to_all | solution.py:919
  240.8 4.8 %copy-start.9 = (bf16[768,2304]{1,0:T(8,128)(2,1)S(1)}, bf16[768,2304]{1,0:T(8,128)(2,1)}, u32[]{:S(2)}) copy-start(bf16[768,2304]{1,0:T(8,128)(2,1)} %refs_5_.1) | copy-start | bytes 10616836
  245.5 18.8 %collective-permute-start = (bf16[768,768]{1,0:T(8,128)(2,1)}, bf16[768,768]{1,0:T(8,128)(2,1)}, u32[]{:S(2)}, u32[]{:S(2)}) collective-permute-start(bf16[768,768]{1,0:T(8,128)(2,1)} %get-tuple-element.112.refs_6_), channel_id=1, source_target_pairs={{0,1},{1,0},{2,3},{3,2},{4,5},{5,4},{6,7},{7,6},{8,9},{9,8},{10,11... | collective-permute-start | bytes 3538952 | tf_op jit(solution)/shard_map/ppermute | solution.py:671
  259.9 4.4 %copy-start.17 = (bf16[768,768]{1,0:T(8,128)(2,1)S(1)}, bf16[768,768]{1,0:T(8,128)(2,1)}, u32[]{:S(2)}) copy-start(bf16[768,768]{1,0:T(8,128)(2,1)} %convolution_convert_fusion.5.refs_6_) | copy-start | bytes 3538948
  259.9 4.4 %copy-start.18 = (bf16[768,768]{1,0:T(8,128)(2,1)S(1)}, bf16[768,768]{1,0:T(8,128)(2,1)}, u32[]{:S(2)}) copy-start(bf16[768,768]{1,0:T(8,128)(2,1)} %get-tuple-element.113) | copy-start | bytes 3538948
  278.8 5.0 %copy-start.7 = (bf16[768,768]{1,0:T(8,128)(2,1)S(1)}, bf16[768,768]{1,0:T(8,128)(2,1)}, u32[]{:S(2)}) copy-start(bf16[768,768]{1,0:T(8,128)(2,1)} %add_convert_fusion.1.refs_6_) | copy-start | bytes 3538948
  283.7 3.4 copy-start.14
  283.7 3.4 copy-start.15
  283.7 3.4 copy-start.16
  283.7 24.1 %collective-permute-start.1 = (bf16[768,768]{1,0:T(8,128)(2,1)}, bf16[768,768]{1,0:T(8,128)(2,1)}, u32[]{:S(2)}, u32[]{:S(2)}) collective-permute-start(bf16[768,768]{1,0:T(8,128)(2,1)} %get-tuple-element.73.refs_9_), channel_id=1, source_target_pairs={{0,1},{1,0},{2,3},{3,2},{4,5},{5,4},{6,7},{7,6},{8,9},{9,8},{10,11... | collective-permute-start | bytes 3538952 | tf_op jit(solution)/shard_map/ppermute | solution.py:671
  284.7 19.7 %collective-permute-start.2 = (bf16[384,768]{1,0:T(8,128)(2,1)}, bf16[384,768]{1,0:T(8,128)(2,1)}, u32[]{:S(2)}, u32[]{:S(2)}) collective-permute-start(bf16[384,768]{1,0:T(8,128)(2,1)} %dynamic-slice_bitcast_fusion.2), channel_id=1, source_target_pairs={{0,2},{1,3},{2,0},{3,1},{4,6},{5,7},{6,4},{7,5},{8,10},{9,11},{10,... | collective-permute-start | bytes 1769480 | tf_op jit(solution)/shard_map/ppermute | solution.py:671
  288.8 3.3 copy-start.21
  304.4 3.4 copy-start.8
  305.7 3.7 copy-start.4
  306.5 24.9 %collective-permute-start.8 = (bf16[192,768]{1,0:T(8,128)(2,1)S(1)}, bf16[192,768]{1,0:T(8,128)(2,1)S(1)}, u32[]{:S(2)}, u32[]{:S(2)}) collective-permute-start(bf16[192,768]{1,0:T(8,128)(2,1)S(1)} %get-tuple-element.89), channel_id=1, source_target_pairs={{0,4},{1,5},{2,6},{3,7},{4,0},{5,1},{6,2},{7,3},{8,12},{9,13},{10,... | collective-permute-start | bytes 884744 | tf_op jit(solution)/shard_map/ppermute | solution.py:671
  310.6 18.2 %collective-permute-start.3 = (bf16[400,768]{1,0:T(8,128)(2,1)S(1)}, bf16[400,768]{1,0:T(8,128)(2,1)S(1)}, u32[]{:S(2)}, u32[]{:S(2)}) collective-permute-start(bf16[400,768]{1,0:T(8,128)(2,1)S(1)} %get-tuple-element.111), channel_id=1, source_target_pairs={{0,4},{1,5},{2,6},{3,7},{4,0},{5,1},{6,2},{7,3},{8,12},{9,13},{10,... | collective-permute-start | bytes 1843208 | tf_op jit(solution)/shard_map/ppermute | solution.py:671
  330.2 11.0 %collective-permute-start.4 = (bf16[208,768]{1,0:T(8,128)(2,1)S(1)}, bf16[208,768]{1,0:T(8,128)(2,1)S(1)}, u32[]{:S(2)}, u32[]{:S(2)}) collective-permute-start(bf16[208,768]{1,0:T(8,128)(2,1)S(1)} %pad_maximum_fusion.9), channel_id=1, source_target_pairs={{0,2},{1,3},{2,0},{3,1},{4,6},{5,7},{6,4},{7,5},{8,10},{9,11},{10,... | collective-permute-start | bytes 958472 | tf_op jit(solution)/shard_map/ppermute | solution.py:671
  332.5 5.7 %collective-permute-start.9 = (bf16[112,768]{1,0:T(8,128)(2,1)S(1)}, bf16[112,768]{1,0:T(8,128)(2,1)S(1)}, u32[]{:S(2)}, u32[]{:S(2)}) collective-permute-start(bf16[112,768]{1,0:T(8,128)(2,1)S(1)} %pad_maximum_fusion.15), channel_id=1, source_target_pairs={{0,8},{8,0},{16,24},{24,16},{1,9},{9,1},{17,25},{25,17},{2,10},{10... | collective-permute-start | bytes 516104 | tf_op jit(solution)/shard_map/ppermute | solution.py:671
  338.3 6.1 %collective-permute-start.10 = (bf16[64,768]{1,0:T(8,128)(2,1)S(1)}, bf16[64,768]{1,0:T(8,128)(2,1)S(1)}, u32[]{:S(2)}, u32[]{:S(2)}) collective-permute-start(bf16[64,768]{1,0:T(8,128)(2,1)S(1)} %pad_maximum_fusion.21), channel_id=1, source_target_pairs={{0,16},{8,24},{16,0},{24,8},{1,17},{9,25},{17,1},{25,9},{2,18},{10... | collective-permute-start | bytes 294920 | tf_op jit(solution)/shard_map/ppermute | solution.py:671
  341.4 6.9 %collective-permute-start.5 = (bf16[112,768]{1,0:T(8,128)(2,1)S(1)}, bf16[112,768]{1,0:T(8,128)(2,1)S(1)}, u32[]{:S(2)}, u32[]{:S(2)}) collective-permute-start(bf16[112,768]{1,0:T(8,128)(2,1)S(1)} %pad_maximum_fusion.13), channel_id=1, source_target_pairs={{0,8},{8,0},{16,24},{24,16},{1,9},{9,1},{17,25},{25,17},{2,10},{10... | collective-permute-start | bytes 516104 | tf_op jit(solution)/shard_map/ppermute | solution.py:671
  344.4 7.8 %collective-permute-start.11 = (bf16[48,768]{1,0:T(8,128)(2,1)S(1)}, bf16[48,768]{1,0:T(8,128)(2,1)S(1)}, u32[]{:S(2)}, u32[]{:S(2)}) collective-permute-start(bf16[48,768]{1,0:T(8,128)(2,1)S(1)} %slice.151), channel_id=1, source_target_pairs={{0,16},{8,24},{16,0},{24,8},{1,17},{9,25},{17,1},{25,9},{2,18},{10... | collective-permute-start | bytes 221192 | tf_op jit(solution)/shard_map/ppermute | solution.py:671
  348.4 6.8 %collective-permute-start.6 = (bf16[64,768]{1,0:T(8,128)(2,1)S(1)}, bf16[64,768]{1,0:T(8,128)(2,1)S(1)}, u32[]{:S(2)}, u32[]{:S(2)}) collective-permute-start(bf16[64,768]{1,0:T(8,128)(2,1)S(1)} %pad_maximum_fusion.19), channel_id=1, source_target_pairs={{0,16},{8,24},{16,0},{24,8},{1,17},{9,25},{17,1},{25,9},{2,18},{10... | collective-permute-start | bytes 294920 | tf_op jit(solution)/shard_map/ppermute | solution.py:671
  355.2 6.5 %copy-start.19 = (bf16[64,768]{1,0:T(8,128)(2,1)}, bf16[64,768]{1,0:T(8,128)(2,1)S(1)}, u32[]{:S(2)}) copy-start(bf16[64,768]{1,0:T(8,128)(2,1)S(1)} %add_convert_fusion.8) | copy-start | bytes 294916
  355.3 6.1 %collective-permute-start.16 = (bf16[48,768]{1,0:T(8,128)(2,1)S(1)}, bf16[48,768]{1,0:T(8,128)(2,1)S(1)}, u32[]{:S(2)}, u32[]{:S(2)}) collective-permute-start(bf16[48,768]{1,0:T(8,128)(2,1)S(1)} %slice.152), channel_id=1, source_target_pairs={{0,16},{8,24},{16,0},{24,8},{1,17},{9,25},{17,1},{25,9},{2,18},{10... | collective-permute-start | bytes 221192 | tf_op jit(solution)/shard_map/ppermute | solution.py:671
  355.4 7.5 %collective-permute-start.12 = (bf16[96,768]{1,0:T(8,128)(2,1)S(1)}, bf16[96,768]{1,0:T(8,128)(2,1)S(1)}, u32[]{:S(2)}, u32[]{:S(2)}) collective-permute-start(bf16[96,768]{1,0:T(8,128)(2,1)S(1)} %pad_maximum_fusion.17), channel_id=1, source_target_pairs={{0,8},{8,0},{16,24},{24,16},{1,9},{9,1},{17,25},{25,17},{2,10},{10... | collective-permute-start | bytes 442376 | tf_op jit(solution)/shard_map/ppermute | solution.py:671
  361.4 5.2 %collective-permute-start.17 = (bf16[96,768]{1,0:T(8,128)(2,1)S(1)}, bf16[96,768]{1,0:T(8,128)(2,1)S(1)}, u32[]{:S(2)}, u32[]{:S(2)}) collective-permute-start(bf16[96,768]{1,0:T(8,128)(2,1)S(1)} %pad_maximum_fusion.18), channel_id=1, source_target_pairs={{0,8},{8,0},{16,24},{24,16},{1,9},{9,1},{17,25},{25,17},{2,10},{10... | collective-permute-start | bytes 442376 | tf_op jit(solution)/shard_map/ppermute | solution.py:671
  362.9 6.8 %collective-permute-start.13 = (bf16[192,768]{1,0:T(8,128)(2,1)S(1)}, bf16[192,768]{1,0:T(8,128)(2,1)S(1)}, u32[]{:S(2)}, u32[]{:S(2)}) collective-permute-start(bf16[192,768]{1,0:T(8,128)(2,1)S(1)} %pad_maximum_fusion.11), channel_id=1, source_target_pairs={{0,4},{1,5},{2,6},{3,7},{4,0},{5,1},{6,2},{7,3},{8,12},{9,13},{10,... | collective-permute-start | bytes 884744 | tf_op jit(solution)/shard_map/ppermute | solution.py:671
  366.7 9.9 %collective-permute-start.18 = (bf16[192,768]{1,0:T(8,128)(2,1)S(1)}, bf16[192,768]{1,0:T(8,128)(2,1)S(1)}, u32[]{:S(2)}, u32[]{:S(2)}) collective-permute-start(bf16[192,768]{1,0:T(8,128)(2,1)S(1)} %pad_maximum_fusion.12), channel_id=1, source_target_pairs={{0,2},{1,3},{2,0},{3,1},{4,6},{5,7},{6,4},{7,5},{8,10},{9,11},{10,... | collective-permute-start | bytes 884744 | tf_op jit(solution)/shard_map/ppermute | solution.py:671
  369.9 15.1 %collective-permute-start.14 = (bf16[384,768]{1,0:T(8,128)(2,1)S(1)}, bf16[384,768]{1,0:T(8,128)(2,1)S(1)}, u32[]{:S(2)}, u32[]{:S(2)}) collective-permute-start(bf16[384,768]{1,0:T(8,128)(2,1)S(1)} %pad_maximum_fusion.7), channel_id=1, source_target_pairs={{0,2},{1,3},{2,0},{3,1},{4,6},{5,7},{6,4},{7,5},{8,10},{9,11},{10,... | collective-permute-start | bytes 1769480 | tf_op jit(solution)/shard_map/ppermute | solution.py:671
  376.8 9.9 %collective-permute-start.19 = (bf16[384,768]{1,0:T(8,128)(2,1)S(1)}, bf16[384,768]{1,0:T(8,128)(2,1)S(1)}, u32[]{:S(2)}, u32[]{:S(2)}) collective-permute-start(bf16[384,768]{1,0:T(8,128)(2,1)S(1)} %pad_maximum_fusion.8), channel_id=1, source_target_pairs={{0,4},{1,5},{2,6},{3,7},{4,0},{5,1},{6,2},{7,3},{8,12},{9,13},{10,... | collective-permute-start | bytes 1769480 | tf_op jit(solution)/shard_map/ppermute | solution.py:671
  378.5 7.8 %copy-start.20 = (f32[16,768]{1,0:T(8,128)}, f32[16,768]{1,0:T(8,128)S(1)}, u32[]{:S(2)}) copy-start(f32[16,768]{1,0:T(8,128)S(1)} %slice_convert_fusion) | copy-start | bytes 147460
  386.3 7.5 %collective-permute-start.15 = (bf16[768,768]{1,0:T(8,128)(2,1)}, bf16[768,768]{1,0:T(8,128)(2,1)S(1)}, u32[]{:S(2)}, u32[]{:S(2)}) collective-permute-start(bf16[768,768]{1,0:T(8,128)(2,1)} %hold.15.refs_1_), channel_id=1, source_target_pairs={{0,1},{1,0},{2,3},{3,2},{4,5},{5,4},{6,7},{7,6},{8,9},{9,8},{10,11... | collective-permute-start | bytes 3538952 | tf_op jit(solution)/shard_map/ppermute | solution.py:671
  386.9 2.9 slice-start
  386.9 6.9 %copy-start = (bf16[768,768]{1,0:T(8,128)(2,1)S(1)}, bf16[768,768]{1,0:T(8,128)(2,1)}, u32[]{:S(2)}) copy-start(bf16[768,768]{1,0:T(8,128)(2,1)} %hold.15.refs_1_) | copy-start | bytes 3538948
  387.0 8.5 %copy-start.6 = (bf16[768,768]{1,0:T(8,128)(2,1)}, bf16[768,768]{1,0:T(8,128)(2,1)S(1)}, u32[]{:S(2)}) copy-start(bf16[768,768]{1,0:T(8,128)(2,1)S(1)} %pad_maximum_fusion.4.refs_3_) | copy-start | bytes 3538948
  387.0 8.6 %collective-permute-start.20 = (bf16[768,768]{1,0:T(8,128)(2,1)S(1)}, bf16[768,768]{1,0:T(8,128)(2,1)}, u32[]{:S(2)}, u32[]{:S(2)}) collective-permute-start(bf16[768,768]{1,0:T(8,128)(2,1)S(1)} %pad_maximum_fusion.4.refs_3_), channel_id=1, source_target_pairs={{0,1},{1,0},{2,3},{3,2},{4,5},{5,4},{6,7},{7,6},{8,9},{9,8},{10,11... | collective-permute-start | bytes 3538952 | tf_op jit(solution)/shard_map/ppermute | solution.py:671
  389.1 2.7 collective-permute-start.7
  393.9 1.8 copy-start.5
  (6 other events, 8.3 us)
Sparse Core Ops, SparseCore 0:
  157.3 84.6 reduce-scatter.2
  244.3 85.7 reduce-scatter.4

commit v5 on v4

--- a/solution.py
+++ b/solution.py
@@ -260,7 +260,7 @@
                 lse_scr[lower:upper, :] = jnp.where(lane, logsum[cut], lse_scr[lower:upper, :])
                 return carry
 
-            lax.fori_loop(0, GROUP, head, 0)
+            lax.fori_loop(0, GROUP, head, 0, unroll=2)
 
     @pl.when(kind_ref[0] == 1)
     def _():
@@ -590,7 +590,7 @@
                 dq_ref[spot, :] += dot_tn(grad_scores, jnp.where(mine, keys_all, 0))
                 return carry
 
-            lax.fori_loop(0, GROUP, head, 0)
+            lax.fori_loop(0, GROUP, head, 0, unroll=2)
 
     @pl.when(kind_ref[0] == 1)
     def _():

time: 416 us -> 408 us (0.981)
  Pallas kernels: 180 us -> 163 us
  starting transfers between devices: 42.8 us -> 49.4 us
    pallas_call x11, Pallas kernels: 180 us -> 163 us  [run(): pl.pallas_call(inner, in_specs=specs, compiler_params=pltpu.CompilerParam...]
  transfers between devices with their start and end apart: 27 -> 27, of which waited for: 15 -> 13; matrix products, arithmetic and copies ran while one was open for 24% -> 24% of each run, Pallas kernels for 30% -> 26%
where the time goes in v5:
time: 408 us; the launch traced here: 401 us
  Pallas kernels  163 us (40%)
  matrix products  71.6 us (18%)
  waiting for transfers between devices  57.8 us (14%)
  starting transfers between devices  49.4 us (12%)
  other arithmetic  28.5 us (7%)
  between operations  15.8 us (4%)
  local copies, waits for them, and re-layouts  14.3 us (4%)
    pallas_call x11, Pallas kernels, run(): pl.pallas_call(inner, in_specs=specs, compiler_params=pltpu.CompilerParam...  163 us
    dot_general x6, matrix products, dot_tn(): lax.dot_general(a, b, (((0,), (0,)), ((), ())), preferred_element_type=F32)  45.5 us
    ppermute x21, waiting for transfers between devices, send_xor(): return lax.ppermute(values, axis, [(j, j ^ distance) for j in range(size)])  34.7 us
    ppermute x21, starting transfers between devices, send_xor(): return lax.ppermute(values, axis, [(j, j ^ distance) for j in range(size)])  28.2 us
    dot_general x2, matrix products, dot_nt(): lax.dot_general(a, b, (((1,), (1,)), ((), ())), preferred_element_type=F32)  26.1 us
    all_to_all x1, waiting for transfers between devices, local(): lax.all_to_all(sent, 'ex', split_axis=0, concat_axis=0, tiled=True)  18.6 us
  transfers between devices with their start and end apart: 27, of which 13 were waited for; matrix products, arithmetic and copies ran while one was open for 24% of the time, Pallas kernels for 26%

profile of v5, /device:TPU:0, one launch (start us, length us, event | category | flops | bytes accessed | tf_op | source)
XLA Modules:
  0.0 400.6 jit_solution(1902116236425673370)
XLA Ops:
  7.2 7.9 %prep.1 = (s32[8,784]{1,0:T(8,128)}, s32[784,128]{1,0:T(8,128)}, bf16[8,208,768]{2,1,0:T(8,128)(2,1)}) custom-call(s32[2,784]{1,0:T(2,128)} %bitcast.99, s32[1,784]{1,0:T(1,128)} %refs_1_.2, bf16[784,768]{1,0:T(8,128)(2,1)} %refs_6_.4), custom_call_target="tpu_custom_call" | custom-call | flops 4000000000 | bytes 6000000 | tf_op jit(solution)/shard_map/prep/pallas_call | solution.py:73
  15.1 5.3 %all-to-all-start.1 = ((bf16[8,208,768]{2,1,0:T(8,128)(2,1)}), bf16[8,208,768]{2,1,0:T(8,128)(2,1)S(1)}, u32[]{:S(2)}, u32[]{:S(2)}) async-start(bf16[8,208,768]{2,1,0:T(8,128)(2,1)} %get-tuple-element.41), calls=%async_computation.1 | async-start | bytes 5111808 | tf_op jit(solution)/shard_map/all_to_all | solution.py:780
  21.7 30.8 %attend.1 = (bf16[3,784,768]{2,1,0:T(8,128)(2,1)}, bf16[784,768]{1,0:T(8,128)(2,1)}, f32[16,784]{1,0:T(8,128)}, bf16[784,768]{1,0:T(8,128)(2,1)}, f32[784,768]{1...) custom-call(s32[1]{0:T(128)S(6)} %copy.45.refs_0_, ...), custom_call_target="tpu_custom_call" | custom-call | flops 10000000000 | bytes 20000000 | tf_op jit(solution)/shard_map/attend/pallas_call | solution.py:73
  52.6 7.9 %all-to-all-start = ((bf16[8,208,768]{2,1,0:T(8,128)(2,1)}), bf16[8,208,768]{2,1,0:T(8,128)(2,1)}, u32[]{:S(2)}, u32[]{:S(2)}) async-start(bf16[8,208,768]{2,1,0:T(8,128)(2,1)} %get-tuple-element.40), calls=%async_computation | async-start | bytes 5111808 | tf_op jit(solution)/shard_map/all_to_all | solution.py:841
  60.8 12.8 %convolution_convert_fusion = bf16[1664,3072]{1,0:T(8,128)(2,1)} fusion(bf16[1664,768]{1,0:T(8,128)(2,1)S(1)} %bitcast.93, bf16[1,3072,768]{2,1,0:T(8,128)(2,1)} %param.26), kind=kOutput, calls=%fused_computation | convolution fusion | flops 7856848896 | bytes 17498112 | tf_op jit(solution)/shard_map/dot_general | solution.py:41
  73.6 18.6 %all-to-all-done.refs_0_ = bf16[8,208,768]{2,1,0:T(8,128)(2,1)} async-done(((bf16[8,208,768]{2,1,0:T(8,128)(2,1)}), bf16[8,208,768]{2,1,0:T(8,128)(2,1)}, u32[]{:S(2)}, u32[]{:S(2)}) %all-to-all-start) | async-done | bytes 2555936 | tf_op jit(solution)/shard_map/all_to_all | solution.py:841
  92.1 44.5 %expert.1 = (bf16[8,208,3072]{2,1,0:T(8,128)(2,1)}, bf16[8,208,3072]{2,1,0:T(8,128)(2,1)}, bf16[8,208,768]{2,1,0:T(8,128)(2,1)}, f32[8,8,256]{2,1,0:T(8,128)}, f32[8,3072]{1,0:T(8,128)}, /*index=5*/f32[8,768]{1,0:T(8,128)}) custom-call(bf16[8,208,768]{2,1,0:T(8,128)(2,1)} %all-to-all-done.refs_0_, bf16[8,208,768]{2,1,0:T(8,128)(2,1)} %copy-done.10, ...), custom_call_target="tpu_custom_call" | custom-call | flops 8000000000 | bytes 40000000 | tf_op jit(solution)/shard_map/expert/pallas_call | solution.py:73
  136.7 13.7 %bitcast_convert_fusion.refs_1_.refs_10_ = bf16[768,3072]{1,0:T(8,128)(2,1)} fusion(bf16[8,208,768]{2,1,0:T(8,128)(2,1)} %all-to-all-done.refs_0_, bf16[8,208,3072]{2,1,0:T(8,128)(2,1)} %get-tuple-element.44), kind=kOutput, calls=%fused_computation.1 | convolution fusion | flops 7854096384 | bytes 17498112 | tf_op jit(solution)/shard_map/dot_general | solution.py:45
  151.3 13.3 %fusion.1.refs_2_ = bf16[8,208,768]{2,1,0:T(8,128)(2,1)} fusion(bf16[8,1,256]{2,1,0:T(2,128)(2,1)S(1)} %get-tuple-element.109, bf16[8,1,256]{2,1,0:T(2,128)(2,1)S(1)} %get-tuple-element.108, bf16[8,208,3072]{2,1,0:T(8,128)(2,1)} %bitcast.87, bf16[1,768,3072]{2,1,0:T(8,128)(2,1)} %param.24, pred[208]{0:T(512)(128)(4,1)S(1)} %iota_compare_fusion.4), kind=kOutput, calls=%fused_computation.4 | convolution fusion | flops 7867072512 | bytes 17506512 | tf_op jit(solution)/shard_map/dot_general | solution.py:41
  164.6 3.6 all-to-all-start.3
  168.7 13.8 %convolution_convert_fusion.1.refs_1_.refs_11_ = bf16[3072,768]{1,0:T(8,128)(2,1)} fusion(bf16[1664,3072]{1,0:T(8,128)(2,1)} %bitcast.82, bf16[1664,768]{1,0:T(8,128)(2,1)} %hold.9), kind=kOutput, calls=%fused_computation.7 | convolution fusion | flops 7854096384 | bytes 17498112 | tf_op jit(solution)/shard_map/dot_general | solution.py:45
  182.5 12.7 %produce.1.refs_12_ = bf16[1664,768]{1,0:T(8,128)(2,1)} custom-call(bf16[1664,3072]{1,0:T(8,128)(2,1)} %hold.10.refs_0_, bf16[3072,768]{1,0:T(8,128)(2,1)} %bitcast.89, f32[1,768]{1,0:T(1,128)} %refs_2_.6), custom_call_target="tpu_custom_call" | custom-call | flops 1 | bytes 1 | tf_op jit(solution)/shard_map/produce/pallas_call | solution.py:73
  195.2 4.5 %all-to-all-done.3.refs_9_ = bf16[8,208,768]{2,1,0:T(8,128)(2,1)S(1)} async-done(((bf16[8,208,768]{2,1,0:T(8,128)(2,1)}), bf16[8,208,768]{2,1,0:T(8,128)(2,1)S(1)}, u32[]{:S(2)}, u32[]{:S(2)}) %all-to-all-start.3) | async-done | bytes 2555936 | tf_op jit(solution)/shard_map/all_to_all | solution.py:899
  201.2 3.6 all-to-all-start.2
  204.8 13.4 %row_grad.1 = (f32[784,768]{1,0:T(8,128)}, bf16[784,768]{1,0:T(8,128)(2,1)}, f32[8,768]{1,0:T(8,128)}, f32[8,768]{1,0:T(8,128)}) custom-call(s32[784,128]{1,0:T(8,128)} %get-tuple-element.36.refs_0_, s32[8,784]{1,0:T(8,128)} %get-tuple-element.37.refs_9_.refs_1_, s32[2,784]{1,0:T(2,128)} %bitcast.101, f32[8,784]{1,0:T(8,128)} %get-tuple-element.38.refs_3_, ...), custom_call_target="tpu_custom_call" | custom-call | flops 1 | bytes 1 | tf_op jit(solution)/shard_map/row_grad/pallas_call | solution.py:73
  218.2 4.1 %convolution_convert_fusion.5.refs_6_ = bf16[768,768]{1,0:T(8,128)(2,1)} fusion(bf16[784,768]{1,0:T(8,128)(2,1)} %get-tuple-element.50.refs_4_, bf16[784,768]{1,0:T(8,128)(2,1)} %get-tuple-element.48.refs_1_), kind=kOutput, calls=%fused_computation.15 | convolution fusion | flops 925433856 | bytes 3588096 | tf_op jit(solution)/shard_map/dot_general | solution.py:45
  222.3 9.5 %attend_back_a.1.refs_0_ = bf16[784,768]{1,0:T(8,128)(2,1)} custom-call(s32[1]{0:T(128)S(6)} %copy.45.refs_0_, bf16[784,768]{1,0:T(8,128)(2,1)} %get-tuple-element.48.refs_1_, bf16[768,768]{1,0:T(8,128)(2,1)} %refs_2_.9, bf16[3,784,768]{2,1,0:T(8,128)(2,1)} %get-tuple-element.49.refs_3_, bf16[784,768]{1,0:T(8,128)(2,1)} %get-tuple-element.50.refs_4_, ...), custom_call_target="tpu_custom_call" | custom-call | flops 8000000000 | bytes 6000000 | tf_op jit(solution)/shard_map/attend_back_a/pallas_call | solution.py:73
  231.8 4.7 %broadcast_select_fusion.2 = (bf16[768,768]{1,0:T(8,128)(2,1)}, bf16[768,768]{1,0:T(8,128)(2,1)}) fusion(bf16[768,768]{1,0:T(8,128)(2,1)} %convolution_convert_fusion.5.refs_6_, pred[]{:T(512)S(6)} %eq.27, bf16[784,768]{1,0:T(8,128)(2,1)} %get-tuple-element.46, bf16[784,768]{1,0:T(8,128)(2,1)} %attend_back_a.1.refs_0_), kind=kOutput, calls=%fused_computation.27 | convolution fusion | flops 926023680 | bytes 5947393 | tf_op jit(solution)/shard_map/dot_general | solution.py:45
  236.4 2.2 collective-permute-start
  241.6 9.4 %attend_back_b.1.refs_1_ = bf16[784,768]{1,0:T(8,128)(2,1)} custom-call(s32[1]{0:T(128)S(6)} %copy.45.refs_0_, bf16[784,768]{1,0:T(8,128)(2,1)} %get-tuple-element.48.refs_1_, bf16[768,768]{1,0:T(8,128)(2,1)} %refs_2_.9, bf16[3,784,768]{2,1,0:T(8,128)(2,1)} %get-tuple-element.49.refs_3_, bf16[784,768]{1,0:T(8,128)(2,1)} %get-tuple-element.50.refs_4_, ...), custom_call_target="tpu_custom_call" | custom-call | flops 8000000000 | bytes 6000000 | tf_op jit(solution)/shard_map/attend_back_b/pallas_call | solution.py:73
  251.1 4.3 %convolution_convert_fusion.3.refs_7_ = bf16[768,768]{1,0:T(8,128)(2,1)} fusion(bf16[784,768]{1,0:T(8,128)(2,1)} %get-tuple-element.46, bf16[784,768]{1,0:T(8,128)(2,1)} %attend_back_b.1.refs_1_), kind=kOutput, calls=%fused_computation.13 | convolution fusion | flops 925433856 | bytes 3588096 | tf_op jit(solution)/shard_map/dot_general | solution.py:45
  255.4 2.8 add_convert_fusion.1.refs_6_
  258.2 9.5 %attend_back_c.1.refs_2_ = bf16[784,768]{1,0:T(8,128)(2,1)} custom-call(s32[1]{0:T(128)S(6)} %copy.45.refs_0_, bf16[784,768]{1,0:T(8,128)(2,1)} %get-tuple-element.48.refs_1_, bf16[768,768]{1,0:T(8,128)(2,1)} %refs_2_.9, bf16[3,784,768]{2,1,0:T(8,128)(2,1)} %get-tuple-element.49.refs_3_, bf16[784,768]{1,0:T(8,128)(2,1)} %get-tuple-element.50.refs_4_, ...), custom_call_target="tpu_custom_call" | custom-call | flops 8000000000 | bytes 6000000 | tf_op jit(solution)/shard_map/attend_back_c/pallas_call | solution.py:73
  267.7 4.9 %broadcast_select_fusion.1 = (bf16[768,768]{1,0:T(8,128)(2,1)}, bf16[768,768]{1,0:T(8,128)(2,1)}) fusion(bf16[768,768]{1,0:T(8,128)(2,1)} %convolution_convert_fusion.3.refs_7_, pred[]{:T(512)S(6)} %eq.27, bf16[784,768]{1,0:T(8,128)(2,1)} %get-tuple-element.46, bf16[784,768]{1,0:T(8,128)(2,1)} %attend_back_c.1.refs_2_), kind=kOutput, calls=%fused_computation.26 | convolution fusion | flops 926613504 | bytes 5947393 | tf_op jit(solution)/shard_map/dot_general | solution.py:45
  272.6 3.1 collective-permute-start.1
  276.7 1.7 collective-permute-start.2
  280.0 2.6 pad_maximum_fusion
  284.1 10.6 %final.1 = (bf16[784,768]{1,0:T(8,128)(2,1)}, f32[8,768]{1,0:T(8,128)}) custom-call(bf16[784,768]{1,0:T(8,128)(2,1)} %attend_back_a.1.refs_0_, bf16[784,768]{1,0:T(8,128)(2,1)} %attend_back_b.1.refs_1_, bf16[784,768]{1,0:T(8,128)(2,1)} %attend_back_c.1.refs_2_, bf16[768,768]{1,0:T(8,128)(2,1)} %get-tuple-element.114.refs_3_, ...), custom_call_target="tpu_custom_call" | custom-call | flops 3000000000 | bytes 14000000 | tf_op jit(solution)/shard_map/final/pallas_call | solution.py:73
  300.6 1.9 collective-permute-start.3
  302.5 4.0 %convert_bitcast_fusion.1 = (f32[1,192,3072]{2,1,0:T(8,128)}, f32[192,3072]{1,0:T(8,128)}) fusion(bf16[192,3072]{1,0:T(8,128)(2,1)} %reduce-scatter.3.cloned.1.call-done), kind=kLoop, calls=%fused_computation.37 | loop fusion | flops 589824 | bytes 5898240 | tf_op jit(solution)/shard_map/broadcast_in_dim | solution.py:1062
  306.5 9.2 %combine.1.refs_1_ = bf16[784,768]{1,0:T(8,128)(2,1)} custom-call(s32[784,128]{1,0:T(8,128)} %get-tuple-element.36.refs_0_, s32[8,784]{1,0:T(8,128)} %get-tuple-element.37.refs_9_.refs_1_, s32[2,784]{1,0:T(2,128)} %bitcast.102, f32[8,784]{1,0:T(8,128)} %get-tuple-element.38.refs_3_, f32[784,768]{1,0:T(8,128)} %get-tuple-element.39.refs_5_.refs_4_, ...), custom_call_target="tpu_custom_call" | custom-call | flops 2000000000 | bytes 8000000 | tf_op jit(solution)/shard_map/combine/pallas_call | solution.py:73
  315.8 3.7 collective-permute-done.3
  323.8 3.1 collective-permute-start.9
  326.9 3.8 convert_bitcast_fusion
  330.8 2.5 collective-permute-start.10
  333.9 2.6 collective-permute-done.10
  336.5 3.0 collective-permute-start.11
  341.1 3.0 collective-permute-done.11
  344.1 2.8 collective-permute-done.6
  347.1 2.8 collective-permute-start.12
  349.9 3.0 collective-permute-done.16
  353.2 2.0 collective-permute-done.12
  356.2 2.0 collective-permute-done.17
  359.7 2.4 collective-permute-done.13
  363.3 4.9 %collective-permute-done.18 = bf16[192,768]{1,0:T(8,128)(2,1)S(1)} collective-permute-done((bf16[192,768]{1,0:T(8,128)(2,1)S(1)}, bf16[192,768]{1,0:T(8,128)(2,1)S(1)}, u32[]{:S(2)}, u32[]{:S(2)}) %collective-permute-start.18) | collective-permute-done | bytes 294944 | tf_op jit(solution)/shard_map/ppermute | solution.py:671
  369.6 7.5 %collective-permute-done.14 = bf16[384,768]{1,0:T(8,128)(2,1)S(1)} collective-permute-done((bf16[384,768]{1,0:T(8,128)(2,1)S(1)}, bf16[384,768]{1,0:T(8,128)(2,1)S(1)}, u32[]{:S(2)}, u32[]{:S(2)}) %collective-permute-start.14) | collective-permute-done | bytes 589856 | tf_op jit(solution)/shard_map/ppermute | solution.py:671
  385.9 1.7 select_convert_fusion
  387.6 5.7 %place_qkv.1 = f32[768,2304]{1,0:T(8,128)} custom-call(s32[1]{0:T(128)} %bitcast.28.refs_0_, bf16[768,768]{1,0:T(8,128)(2,1)} %hold.15.refs_1_, bf16[768,768]{1,0:T(8,128)(2,1)} %copy-done.5, bf16[768,768]{1,0:T(8,128)(2,1)} %copy-done.6, bf16[768,768]{1,0:T(8,128)(2,1)} %collective-permute-done.20.refs_4_), custom_call_target="tpu_custom_call" | custom-call | flops 1000000 | bytes 11796480 | tf_op jit(solution)/shard_map/place_qkv/pallas_call | solution.py:73
  (170 shorter events, 37.4 us)
Async XLA Ops:
  15.0 6.0 %copy-start.22 = (f32[768]{0:T(1024)S(1)}, f32[768]{0:T(1024)}, u32[]{:S(2)}) copy-start(f32[768]{0:T(1024)} %param.22) | copy-start | bytes 9220
  15.0 6.0 %copy-start.23 = (f32[768]{0:T(1024)S(1)}, f32[768]{0:T(1024)}, u32[]{:S(2)}) copy-start(f32[768]{0:T(1024)} %param.21) | copy-start | bytes 9220
  15.0 6.0 %copy-start.24 = (f32[768]{0:T(1024)S(1)}, f32[768]{0:T(1024)}, u32[]{:S(2)}) copy-start(f32[768]{0:T(1024)} %param.18) | copy-start | bytes 9220
  15.0 6.1 %copy-start.25 = (f32[768]{0:T(1024)S(1)}, f32[768]{0:T(1024)}, u32[]{:S(2)}) copy-start(f32[768]{0:T(1024)} %param.17) | copy-start | bytes 9220
  15.1 37.5 %all-to-all-start.1 = ((bf16[8,208,768]{2,1,0:T(8,128)(2,1)}), bf16[8,208,768]{2,1,0:T(8,128)(2,1)S(1)}, u32[]{:S(2)}, u32[]{:S(2)}) async-start(bf16[8,208,768]{2,1,0:T(8,128)(2,1)} %get-tuple-element.41), calls=%async_computation.1 | async-start | bytes 5111808 | tf_op jit(solution)/shard_map/all_to_all | solution.py:780
  52.6 8.1 %copy-start.10 = (bf16[8,208,768]{2,1,0:T(8,128)(2,1)}, bf16[8,208,768]{2,1,0:T(8,128)(2,1)S(1)}, u32[]{:S(2)}) copy-start(bf16[8,208,768]{2,1,0:T(8,128)(2,1)S(1)} %all-to-all-done.1.refs_1_) | copy-start | bytes 7667716
  52.6 39.5 %all-to-all-start = ((bf16[8,208,768]{2,1,0:T(8,128)(2,1)}), bf16[8,208,768]{2,1,0:T(8,128)(2,1)}, u32[]{:S(2)}, u32[]{:S(2)}) async-start(bf16[8,208,768]{2,1,0:T(8,128)(2,1)} %get-tuple-element.40), calls=%async_computation | async-start | bytes 5111808 | tf_op jit(solution)/shard_map/all_to_all | solution.py:841
  60.5 242.0 %reduce-scatter.3.cloned.1.call-start = ((), (), s32[]{:S(2)}) async-start(), calls=%async_computation.6 | async-start | bytes 5898240 | tf_op jit(solution)/shard_map/reduce_scatter | solution.py:894
  164.6 35.1 %all-to-all-start.3 = ((bf16[8,208,768]{2,1,0:T(8,128)(2,1)}), bf16[8,208,768]{2,1,0:T(8,128)(2,1)S(1)}, u32[]{:S(2)}, u32[]{:S(2)}) async-start(bf16[8,208,768]{2,1,0:T(8,128)(2,1)} %fusion.1.refs_2_), calls=%async_computation.3 | async-start | bytes 5111808 | tf_op jit(solution)/shard_map/all_to_all | solution.py:899
  168.2 158.6 %reduce-scatter.5.cloned.1.call-start = ((), (), s32[]{:S(2)}) async-start(), calls=%async_computation.7 | async-start | bytes 5898240 | tf_op jit(solution)/shard_map/reduce_scatter | solution.py:903
  201.2 39.0 %all-to-all-start.2 = ((bf16[8,208,768]{2,1,0:T(8,128)(2,1)}), bf16[8,208,768]{2,1,0:T(8,128)(2,1)S(1)}, u32[]{:S(2)}, u32[]{:S(2)}) async-start(bf16[8,208,768]{2,1,0:T(8,128)(2,1)} %bitcast.84), calls=%async_computation.2 | async-start | bytes 5111808 | tf_op jit(solution)/shard_map/all_to_all | solution.py:919
  231.8 6.8 %copy-start.9 = (bf16[768,2304]{1,0:T(8,128)(2,1)S(1)}, bf16[768,2304]{1,0:T(8,128)(2,1)}, u32[]{:S(2)}) copy-start(bf16[768,2304]{1,0:T(8,128)(2,1)} %refs_5_.1) | copy-start | bytes 10616836
  236.4 18.9 %collective-permute-start = (bf16[768,768]{1,0:T(8,128)(2,1)}, bf16[768,768]{1,0:T(8,128)(2,1)}, u32[]{:S(2)}, u32[]{:S(2)}) collective-permute-start(bf16[768,768]{1,0:T(8,128)(2,1)} %get-tuple-element.112.refs_6_), channel_id=1, source_target_pairs={{0,1},{1,0},{2,3},{3,2},{4,5},{5,4},{6,7},{7,6},{8,9},{9,8},{10,11... | collective-permute-start | bytes 3538952 | tf_op jit(solution)/shard_map/ppermute | solution.py:671
  251.0 4.3 %copy-start.17 = (bf16[768,768]{1,0:T(8,128)(2,1)S(1)}, bf16[768,768]{1,0:T(8,128)(2,1)}, u32[]{:S(2)}) copy-start(bf16[768,768]{1,0:T(8,128)(2,1)} %convolution_convert_fusion.5.refs_6_) | copy-start | bytes 3538948
  251.0 4.3 %copy-start.18 = (bf16[768,768]{1,0:T(8,128)(2,1)S(1)}, bf16[768,768]{1,0:T(8,128)(2,1)}, u32[]{:S(2)}) copy-start(bf16[768,768]{1,0:T(8,128)(2,1)} %get-tuple-element.113) | copy-start | bytes 3538948
  267.7 8.1 %copy-start.7 = (bf16[768,768]{1,0:T(8,128)(2,1)S(1)}, bf16[768,768]{1,0:T(8,128)(2,1)}, u32[]{:S(2)}) copy-start(bf16[768,768]{1,0:T(8,128)(2,1)} %add_convert_fusion.1.refs_6_) | copy-start | bytes 3538948
  272.6 5.7 %copy-start.14 = (bf16[768,256]{1,0:T(8,128)(2,1)S(1)}, bf16[768,256]{1,0:T(8,128)(2,1)}, u32[]{:S(2)}) copy-start(bf16[768,256]{1,0:T(8,128)(2,1)} %get-tuple-element.63) | copy-start | bytes 1179652
  272.6 5.7 %copy-start.15 = (bf16[768,256]{1,0:T(8,128)(2,1)S(1)}, bf16[768,256]{1,0:T(8,128)(2,1)}, u32[]{:S(2)}) copy-start(bf16[768,256]{1,0:T(8,128)(2,1)} %get-tuple-element.70) | copy-start | bytes 1179652
  272.6 5.7 %copy-start.16 = (bf16[768,256]{1,0:T(8,128)(2,1)S(1)}, bf16[768,256]{1,0:T(8,128)(2,1)}, u32[]{:S(2)}) copy-start(bf16[768,256]{1,0:T(8,128)(2,1)} %get-tuple-element.71) | copy-start | bytes 1179652
  272.6 25.2 %collective-permute-start.1 = (bf16[768,768]{1,0:T(8,128)(2,1)}, bf16[768,768]{1,0:T(8,128)(2,1)}, u32[]{:S(2)}, u32[]{:S(2)}) collective-permute-start(bf16[768,768]{1,0:T(8,128)(2,1)} %get-tuple-element.73.refs_9_), channel_id=1, source_target_pairs={{0,1},{1,0},{2,3},{3,2},{4,5},{5,4},{6,7},{7,6},{8,9},{9,8},{10,11... | collective-permute-start | bytes 3538952 | tf_op jit(solution)/shard_map/ppermute | solution.py:671
  276.7 18.8 %collective-permute-start.2 = (bf16[384,768]{1,0:T(8,128)(2,1)}, bf16[384,768]{1,0:T(8,128)(2,1)}, u32[]{:S(2)}, u32[]{:S(2)}) collective-permute-start(bf16[384,768]{1,0:T(8,128)(2,1)} %dynamic-slice_bitcast_fusion.2), channel_id=1, source_target_pairs={{0,2},{1,3},{2,0},{3,1},{4,6},{5,7},{6,4},{7,5},{8,10},{9,11},{10,... | collective-permute-start | bytes 1769480 | tf_op jit(solution)/shard_map/ppermute | solution.py:671
  280.0 3.3 copy-start.21
  295.5 2.3 copy-start.8
  296.8 2.6 copy-start.4
  297.7 25.0 %collective-permute-start.8 = (bf16[192,768]{1,0:T(8,128)(2,1)S(1)}, bf16[192,768]{1,0:T(8,128)(2,1)S(1)}, u32[]{:S(2)}, u32[]{:S(2)}) collective-permute-start(bf16[192,768]{1,0:T(8,128)(2,1)S(1)} %get-tuple-element.89), channel_id=1, source_target_pairs={{0,4},{1,5},{2,6},{3,7},{4,0},{5,1},{6,2},{7,3},{8,12},{9,13},{10,... | collective-permute-start | bytes 884744 | tf_op jit(solution)/shard_map/ppermute | solution.py:671
  300.6 18.8 %collective-permute-start.3 = (bf16[400,768]{1,0:T(8,128)(2,1)S(1)}, bf16[400,768]{1,0:T(8,128)(2,1)S(1)}, u32[]{:S(2)}, u32[]{:S(2)}) collective-permute-start(bf16[400,768]{1,0:T(8,128)(2,1)S(1)} %get-tuple-element.111), channel_id=1, source_target_pairs={{0,4},{1,5},{2,6},{3,7},{4,0},{5,1},{6,2},{7,3},{8,12},{9,13},{10,... | collective-permute-start | bytes 1843208 | tf_op jit(solution)/shard_map/ppermute | solution.py:671
  320.8 12.5 %collective-permute-start.4 = (bf16[208,768]{1,0:T(8,128)(2,1)S(1)}, bf16[208,768]{1,0:T(8,128)(2,1)S(1)}, u32[]{:S(2)}, u32[]{:S(2)}) collective-permute-start(bf16[208,768]{1,0:T(8,128)(2,1)S(1)} %pad_maximum_fusion.9), channel_id=1, source_target_pairs={{0,2},{1,3},{2,0},{3,1},{4,6},{5,7},{6,4},{7,5},{8,10},{9,11},{10,... | collective-permute-start | bytes 958472 | tf_op jit(solution)/shard_map/ppermute | solution.py:671
  323.8 6.9 %collective-permute-start.9 = (bf16[112,768]{1,0:T(8,128)(2,1)S(1)}, bf16[112,768]{1,0:T(8,128)(2,1)S(1)}, u32[]{:S(2)}, u32[]{:S(2)}) collective-permute-start(bf16[112,768]{1,0:T(8,128)(2,1)S(1)} %pad_maximum_fusion.15), channel_id=1, source_target_pairs={{0,8},{8,0},{16,24},{24,16},{1,9},{9,1},{17,25},{25,17},{2,10},{10... | collective-permute-start | bytes 516104 | tf_op jit(solution)/shard_map/ppermute | solution.py:671
  330.8 5.7 %collective-permute-start.10 = (bf16[64,768]{1,0:T(8,128)(2,1)S(1)}, bf16[64,768]{1,0:T(8,128)(2,1)S(1)}, u32[]{:S(2)}, u32[]{:S(2)}) collective-permute-start(bf16[64,768]{1,0:T(8,128)(2,1)S(1)} %pad_maximum_fusion.21), channel_id=1, source_target_pairs={{0,16},{8,24},{16,0},{24,8},{1,17},{9,25},{17,1},{25,9},{2,18},{10... | collective-permute-start | bytes 294920 | tf_op jit(solution)/shard_map/ppermute | solution.py:671
  333.5 6.7 %collective-permute-start.5 = (bf16[112,768]{1,0:T(8,128)(2,1)S(1)}, bf16[112,768]{1,0:T(8,128)(2,1)S(1)}, u32[]{:S(2)}, u32[]{:S(2)}) collective-permute-start(bf16[112,768]{1,0:T(8,128)(2,1)S(1)} %pad_maximum_fusion.13), channel_id=1, source_target_pairs={{0,8},{8,0},{16,24},{24,16},{1,9},{9,1},{17,25},{25,17},{2,10},{10... | collective-permute-start | bytes 516104 | tf_op jit(solution)/shard_map/ppermute | solution.py:671
  336.5 7.6 %collective-permute-start.11 = (bf16[48,768]{1,0:T(8,128)(2,1)S(1)}, bf16[48,768]{1,0:T(8,128)(2,1)S(1)}, u32[]{:S(2)}, u32[]{:S(2)}) collective-permute-start(bf16[48,768]{1,0:T(8,128)(2,1)S(1)} %slice.151), channel_id=1, source_target_pairs={{0,16},{8,24},{16,0},{24,8},{1,17},{9,25},{17,1},{25,9},{2,18},{10... | collective-permute-start | bytes 221192 | tf_op jit(solution)/shard_map/ppermute | solution.py:671
  340.3 6.6 %collective-permute-start.6 = (bf16[64,768]{1,0:T(8,128)(2,1)S(1)}, bf16[64,768]{1,0:T(8,128)(2,1)S(1)}, u32[]{:S(2)}, u32[]{:S(2)}) collective-permute-start(bf16[64,768]{1,0:T(8,128)(2,1)S(1)} %pad_maximum_fusion.19), channel_id=1, source_target_pairs={{0,16},{8,24},{16,0},{24,8},{1,17},{9,25},{17,1},{25,9},{2,18},{10... | collective-permute-start | bytes 294920 | tf_op jit(solution)/shard_map/ppermute | solution.py:671
  347.0 6.2 %copy-start.19 = (bf16[64,768]{1,0:T(8,128)(2,1)}, bf16[64,768]{1,0:T(8,128)(2,1)S(1)}, u32[]{:S(2)}) copy-start(bf16[64,768]{1,0:T(8,128)(2,1)S(1)} %add_convert_fusion.8) | copy-start | bytes 294916
  347.0 5.9 %collective-permute-start.16 = (bf16[48,768]{1,0:T(8,128)(2,1)S(1)}, bf16[48,768]{1,0:T(8,128)(2,1)S(1)}, u32[]{:S(2)}, u32[]{:S(2)}) collective-permute-start(bf16[48,768]{1,0:T(8,128)(2,1)S(1)} %slice.152), channel_id=1, source_target_pairs={{0,16},{8,24},{16,0},{24,8},{1,17},{9,25},{17,1},{25,9},{2,18},{10... | collective-permute-start | bytes 221192 | tf_op jit(solution)/shard_map/ppermute | solution.py:671
  347.1 8.1 %collective-permute-start.12 = (bf16[96,768]{1,0:T(8,128)(2,1)S(1)}, bf16[96,768]{1,0:T(8,128)(2,1)S(1)}, u32[]{:S(2)}, u32[]{:S(2)}) collective-permute-start(bf16[96,768]{1,0:T(8,128)(2,1)S(1)} %pad_maximum_fusion.17), channel_id=1, source_target_pairs={{0,8},{8,0},{16,24},{24,16},{1,9},{9,1},{17,25},{25,17},{2,10},{10... | collective-permute-start | bytes 442376 | tf_op jit(solution)/shard_map/ppermute | solution.py:671
  353.0 5.2 %collective-permute-start.17 = (bf16[96,768]{1,0:T(8,128)(2,1)S(1)}, bf16[96,768]{1,0:T(8,128)(2,1)S(1)}, u32[]{:S(2)}, u32[]{:S(2)}) collective-permute-start(bf16[96,768]{1,0:T(8,128)(2,1)S(1)} %pad_maximum_fusion.18), channel_id=1, source_target_pairs={{0,8},{8,0},{16,24},{24,16},{1,9},{9,1},{17,25},{25,17},{2,10},{10... | collective-permute-start | bytes 442376 | tf_op jit(solution)/shard_map/ppermute | solution.py:671
  355.3 6.8 %collective-permute-start.13 = (bf16[192,768]{1,0:T(8,128)(2,1)S(1)}, bf16[192,768]{1,0:T(8,128)(2,1)S(1)}, u32[]{:S(2)}, u32[]{:S(2)}) collective-permute-start(bf16[192,768]{1,0:T(8,128)(2,1)S(1)} %pad_maximum_fusion.11), channel_id=1, source_target_pairs={{0,4},{1,5},{2,6},{3,7},{4,0},{5,1},{6,2},{7,3},{8,12},{9,13},{10,... | collective-permute-start | bytes 884744 | tf_op jit(solution)/shard_map/ppermute | solution.py:671
  358.3 9.9 %collective-permute-start.18 = (bf16[192,768]{1,0:T(8,128)(2,1)S(1)}, bf16[192,768]{1,0:T(8,128)(2,1)S(1)}, u32[]{:S(2)}, u32[]{:S(2)}) collective-permute-start(bf16[192,768]{1,0:T(8,128)(2,1)S(1)} %pad_maximum_fusion.12), channel_id=1, source_target_pairs={{0,2},{1,3},{2,0},{3,1},{4,6},{5,7},{6,4},{7,5},{8,10},{9,11},{10,... | collective-permute-start | bytes 884744 | tf_op jit(solution)/shard_map/ppermute | solution.py:671
  362.3 14.8 %collective-permute-start.14 = (bf16[384,768]{1,0:T(8,128)(2,1)S(1)}, bf16[384,768]{1,0:T(8,128)(2,1)S(1)}, u32[]{:S(2)}, u32[]{:S(2)}) collective-permute-start(bf16[384,768]{1,0:T(8,128)(2,1)S(1)} %pad_maximum_fusion.7), channel_id=1, source_target_pairs={{0,2},{1,3},{2,0},{3,1},{4,6},{5,7},{6,4},{7,5},{8,10},{9,11},{10,... | collective-permute-start | bytes 1769480 | tf_op jit(solution)/shard_map/ppermute | solution.py:671
  368.4 10.1 %collective-permute-start.19 = (bf16[384,768]{1,0:T(8,128)(2,1)S(1)}, bf16[384,768]{1,0:T(8,128)(2,1)S(1)}, u32[]{:S(2)}, u32[]{:S(2)}) collective-permute-start(bf16[384,768]{1,0:T(8,128)(2,1)S(1)} %pad_maximum_fusion.8), channel_id=1, source_target_pairs={{0,4},{1,5},{2,6},{3,7},{4,0},{5,1},{6,2},{7,3},{8,12},{9,13},{10,... | collective-permute-start | bytes 1769480 | tf_op jit(solution)/shard_map/ppermute | solution.py:671
  369.6 8.8 %copy-start.20 = (f32[16,768]{1,0:T(8,128)}, f32[16,768]{1,0:T(8,128)S(1)}, u32[]{:S(2)}) copy-start(f32[16,768]{1,0:T(8,128)S(1)} %slice_convert_fusion) | copy-start | bytes 147460
  378.4 7.5 %collective-permute-start.15 = (bf16[768,768]{1,0:T(8,128)(2,1)}, bf16[768,768]{1,0:T(8,128)(2,1)S(1)}, u32[]{:S(2)}, u32[]{:S(2)}) collective-permute-start(bf16[768,768]{1,0:T(8,128)(2,1)} %hold.15.refs_1_), channel_id=1, source_target_pairs={{0,1},{1,0},{2,3},{3,2},{4,5},{5,4},{6,7},{7,6},{8,9},{9,8},{10,11... | collective-permute-start | bytes 3538952 | tf_op jit(solution)/shard_map/ppermute | solution.py:671
  378.6 3.2 slice-start
  378.6 7.2 %copy-start = (bf16[768,768]{1,0:T(8,128)(2,1)S(1)}, bf16[768,768]{1,0:T(8,128)(2,1)}, u32[]{:S(2)}) copy-start(bf16[768,768]{1,0:T(8,128)(2,1)} %hold.15.refs_1_) | copy-start | bytes 3538948
  378.7 8.8 %copy-start.6 = (bf16[768,768]{1,0:T(8,128)(2,1)}, bf16[768,768]{1,0:T(8,128)(2,1)S(1)}, u32[]{:S(2)}) copy-start(bf16[768,768]{1,0:T(8,128)(2,1)S(1)} %pad_maximum_fusion.4.refs_3_) | copy-start | bytes 3538948
  378.8 8.9 %collective-permute-start.20 = (bf16[768,768]{1,0:T(8,128)(2,1)S(1)}, bf16[768,768]{1,0:T(8,128)(2,1)}, u32[]{:S(2)}, u32[]{:S(2)}) collective-permute-start(bf16[768,768]{1,0:T(8,128)(2,1)S(1)} %pad_maximum_fusion.4.refs_3_), channel_id=1, source_target_pairs={{0,1},{1,0},{2,3},{3,2},{4,5},{5,4},{6,7},{7,6},{8,9},{9,8},{10,11... | collective-permute-start | bytes 3538952 | tf_op jit(solution)/shard_map/ppermute | solution.py:671
  380.8 3.0 collective-permute-start.7
  385.9 1.8 copy-start.5
  (6 other events, 8.3 us)
Sparse Core Ops, SparseCore 0:
  150.5 85.5 reduce-scatter.2
  238.3 85.7 reduce-scatter.4
